TPU v7x, 32 devices: a whole 2x2x4 slice. The times are simulated.
32 devices in a mesh: ga: 8 (over z, y), ha: 4 (over x, core).
Axes of the slice: x: 2, y: 2, z: 4, core: 2. Of those that a mesh axis runs over, the one named last changes fastest.
Arguments:
- patches: bfloat16 [8, 2304, 768], P(None, ('ga', 'ha')), may hold values from -6 to 6
- cotangent: bfloat16 [8, 2304, 768], P(None, ('ga', 'ha')), may hold values from -6 to 6
- sides: int32 [8], replicated, may hold values from 36 to 48, as said below
- norm1_gain: bfloat16 [768], P('ha'), may hold values from 0.5 to 1.5
- norm1_bias: bfloat16 [768], P('ha'), may hold values from -1.75 to 1.75
- qkv_weight: bfloat16 [768, 2304], P('ha', 'ga'), may hold values from -0.21875 to 0.21875
- query_bias: bfloat16 [768], P('ha'), may hold values from -1.75 to 1.75
- value_bias: bfloat16 [768], P('ha'), may hold values from -1.75 to 1.75
- proj_weight: bfloat16 [768, 768], P('ha', 'ga'), may hold values from -1.25 to 1.25
- proj_bias: bfloat16 [768], P('ha'), may hold values from -1.75 to 1.75
- norm2_gain: bfloat16 [768], P('ha'), may hold values from 0.5 to 1.5
- norm2_bias: bfloat16 [768], P('ha'), may hold values from -1.75 to 1.75
- fc1_weight: bfloat16 [768, 3072], P('ha', 'ga'), may hold values from -0.21875 to 0.21875
- fc1_bias: bfloat16 [3072], P('ha'), may hold values from -1.75 to 1.75
- fc2_weight: bfloat16 [3072, 768], P('ha', 'ga'), may hold values from -0.109375 to 0.109375
- fc2_bias: bfloat16 [768], P('ha'), may hold values from -1.75 to 1.75
- rel_height: bfloat16 [95, 64], replicated, may hold values from -0.875 to 0.875
- rel_width: bfloat16 [95, 64], replicated, may hold values from -0.875 to 0.875
Outputs:
- block_out: bfloat16 [8, 2304, 768], P(None, ('ga', 'ha'))
- input_grad: bfloat16 [8, 2304, 768], P(None, ('ga', 'ha'))
- norm1_gain_grad: float32 [768], P('ha')
- norm1_bias_grad: float32 [768], P('ha')
- qkv_weight_grad: float32 [768, 2304], P('ha', 'ga')
- query_bias_grad: float32 [768], P('ha')
- value_bias_grad: float32 [768], P('ha')
- proj_weight_grad: float32 [768, 768], P('ha', 'ga')
- proj_bias_grad: float32 [768], P('ha')
- norm2_gain_grad: float32 [768], P('ha')
- norm2_bias_grad: float32 [768], P('ha')
- fc1_weight_grad: float32 [768, 3072], P('ha', 'ga')
- fc1_bias_grad: float32 [3072], P('ha')
- fc2_weight_grad: float32 [3072, 768], P('ha', 'ga')
- fc2_bias_grad: float32 [768], P('ha')
- rel_height_grad: float32 [95, 64], replicated
- rel_width_grad: float32 [95, 64], replicated
Inputs may be any that keep to these rules, and one draw needn't show every extreme that they name: Image i fills the top-left sides[i] x sides[i] patches of its 48 x 48 grid; every entry is 36 or 48, and both values occur in every draw.
All inputs are finite; a program needn't handle non-finite values.
Results may differ from a plain program's by a relative error of at most 0.02.
Values may be sent and summed in bfloat16 or wider, within the bound.
No kernel may reach another device: no remote copies, remote signals or barrier semaphores. Data moves between devices by JAX's collectives and lax.ppermute only.
A program may use at most 192 MiB of HBM per device.

v0:
```python
from functools import partial

import jax
import jax.numpy as jnp
from jax import lax
from jax.sharding import PartitionSpec as P

HEADS = 12
HD = 64
SMAX = 48


exact_mode = lax.Precision.HIGHEST


def layer_norm(values, gain, shift):
    center = values - jnp.mean(values, axis=-1, keepdims=True)
    spread = jnp.mean(center * center, axis=-1, keepdims=True)
    return center * lax.rsqrt(spread + 1e-06) * gain + shift


def interp_matrix(img_side):
    coord = jnp.arange(SMAX, dtype=jnp.int32)
    length_in = 2 * SMAX - 1
    length_out = 2 * img_side - 1
    offset = jnp.clip(coord[:, None] - coord[None, :] + img_side - 1, 0, length_out - 1)
    numer = jnp.maximum((2 * offset + 1) * length_in - length_out, 0)
    lower = numer // (2 * length_out)
    weight_hi = (numer - lower * 2 * length_out).astype(jnp.float32) / (2 * length_out).astype(
        jnp.float32
    )
    upper = jnp.minimum(lower + 1, length_in - 1)
    target = jnp.arange(length_in, dtype=jnp.int32)
    lower_hot = (target == lower[..., None]).astype(jnp.float32)
    upper_hot = (target == upper[..., None]).astype(jnp.float32)
    return (1.0 - weight_hi)[..., None] * lower_hot + weight_hi[..., None] * upper_hot


def contract_rows(left, right):
    return lax.dot_general(
        left, right, (((0,), (0,)), ((), ())), preferred_element_type=jnp.float32
    )


def contract_cols(left, right):
    return lax.dot_general(
        left, right, (((1,), (1,)), ((), ())), preferred_element_type=jnp.float32
    )


def split_product(form, wide_sum, narrow):
    upper_part = wide_sum.astype(jnp.bfloat16)
    lower_part = (wide_sum - upper_part.astype(jnp.float32)).astype(jnp.bfloat16)
    return jnp.einsum(form, upper_part, narrow, preferred_element_type=jnp.float32) + jnp.einsum(
        form, lower_part, narrow, preferred_element_type=jnp.float32
    )


def gather_first(
    triple_w,
    proj_w,
    up_w,
    down_w,
    first_gain,
    first_shift,
    query_shift,
    value_shift,
    proj_shift,
    second_gain,
    second_shift,
    up_shift,
    down_shift,
):
    rows_all = (
        lax.all_gather(triple_w, "ha", axis=0, tiled=True),
        lax.all_gather(proj_w, "ha", axis=0, tiled=True),
        lax.all_gather(up_w, "ha", axis=0, tiled=True),
        lax.all_gather(down_w, "ha", axis=0, tiled=True),
        lax.all_gather(first_gain, "ha", axis=0, tiled=True),
        lax.all_gather(first_shift, "ha", axis=0, tiled=True),
        lax.all_gather(query_shift, "ha", axis=0, tiled=True),
        lax.all_gather(value_shift, "ha", axis=0, tiled=True),
        lax.all_gather(proj_shift, "ha", axis=0, tiled=True),
        lax.all_gather(second_gain, "ha", axis=0, tiled=True),
        lax.all_gather(second_shift, "ha", axis=0, tiled=True),
        lax.all_gather(up_shift, "ha", axis=0, tiled=True),
        lax.all_gather(down_shift, "ha", axis=0, tiled=True),
    )
    full_mats = (
        lax.all_gather(rows_all[0], "ga", axis=1, tiled=True),
        lax.all_gather(rows_all[1], "ga", axis=1, tiled=True),
        lax.all_gather(rows_all[2], "ga", axis=1, tiled=True),
        lax.all_gather(rows_all[3], "ga", axis=1, tiled=True),
    )
    return tuple(full_mats) + tuple(rows_all[4:])


def gather_again(
    triple_w,
    proj_w,
    up_w,
    down_w,
    first_gain,
    first_shift,
    query_shift,
    value_shift,
    proj_shift,
    second_gain,
    second_shift,
    up_shift,
    down_shift,
):
    rows_all = (
        lax.all_gather(triple_w, "ha", axis=0, tiled=True),
        lax.all_gather(proj_w, "ha", axis=0, tiled=True),
        lax.all_gather(up_w, "ha", axis=0, tiled=True),
        lax.all_gather(down_w, "ha", axis=0, tiled=True),
        lax.all_gather(first_gain, "ha", axis=0, tiled=True),
        lax.all_gather(first_shift, "ha", axis=0, tiled=True),
        lax.all_gather(query_shift, "ha", axis=0, tiled=True),
        lax.all_gather(value_shift, "ha", axis=0, tiled=True),
        lax.all_gather(proj_shift, "ha", axis=0, tiled=True),
        lax.all_gather(second_gain, "ha", axis=0, tiled=True),
        lax.all_gather(second_shift, "ha", axis=0, tiled=True),
        lax.all_gather(up_shift, "ha", axis=0, tiled=True),
        lax.all_gather(down_shift, "ha", axis=0, tiled=True),
    )
    full_mats = (
        lax.all_gather(rows_all[0], "ga", axis=1, tiled=True),
        lax.all_gather(rows_all[1], "ga", axis=1, tiled=True),
        lax.all_gather(rows_all[2], "ga", axis=1, tiled=True),
        lax.all_gather(rows_all[3], "ga", axis=1, tiled=True),
    )
    return tuple(full_mats) + tuple(rows_all[4:])


def local(
    patches,
    cotangent,
    sides,
    norm1_gain,
    norm1_bias,
    qkv_weight,
    query_bias,
    value_bias,
    proj_weight,
    proj_bias,
    norm2_gain,
    norm2_bias,
    fc1_weight,
    fc1_bias,
    fc2_weight,
    fc2_bias,
    rel_height,
    rel_width,
):
    group_count = lax.axis_size("ga")
    head_groups = lax.axis_size("ha")
    group_index = lax.axis_index("ga")
    head_index = lax.axis_index("ha")
    block_len = patches.shape[1]
    model_width = patches.shape[2]
    local_tokens = group_count * block_len
    group_width = model_width // head_groups
    group_heads = HEADS // head_groups
    cap_tokens = SMAX * SMAX
    score_scale = HD ** (-0.5)
    row_count = SMAX // 4
    block_count = SMAX // row_count
    f32 = jnp.float32
    bf16 = jnp.bfloat16
    weights_fwd = gather_first(
        qkv_weight,
        proj_weight,
        fc1_weight,
        fc2_weight,
        norm1_gain,
        norm1_bias,
        query_bias,
        value_bias,
        proj_bias,
        norm2_gain,
        norm2_bias,
        fc1_bias,
        fc2_bias,
    )
    (
        triple_full,
        proj_full,
        up_full,
        down_full,
        first_gain,
        first_shift,
        query_shift,
        value_shift,
        proj_shift,
        second_gain,
        second_shift,
        up_shift,
        down_shift,
    ) = weights_fwd
    arrived = (
        lax.all_to_all(patches, "ga", split_axis=0, concat_axis=1, tiled=True),
        lax.all_to_all(cotangent, "ga", split_axis=0, concat_axis=1, tiled=True),
    )
    tokens32 = arrived[0][0].astype(f32)
    cot32 = arrived[1][0].astype(f32)
    slot_index = jnp.arange(local_tokens, dtype=jnp.int32)
    grid_index = (
        slot_index // block_len * head_groups + head_index
    ) * block_len + slot_index % block_len
    img_side = lax.dynamic_index_in_dim(sides, group_index, 0, keepdims=False)
    tok_mask = ((grid_index // SMAX < img_side) & (grid_index % SMAX < img_side)).astype(f32)[
        :, None
    ]
    all_index = jnp.arange(cap_tokens, dtype=jnp.int32)
    key_valid = (all_index // SMAX < img_side) & (all_index % SMAX < img_side)
    line_index = jnp.arange(2 * SMAX, dtype=jnp.int32)[:, None]
    expand = jnp.where(
        line_index < SMAX,
        (all_index // SMAX)[None, :] == line_index,
        (all_index % SMAX)[None, :] == line_index - SMAX,
    ).astype(bf16)
    matrix = interp_matrix(img_side)
    table_h = jnp.einsum(
        "qkj,jd->qkd", matrix, rel_height.astype(f32), precision=exact_mode
    ).astype(bf16)
    table_w = jnp.einsum("qkj,jd->qkd", matrix, rel_width.astype(f32), precision=exact_mode).astype(
        bf16
    )
    h_blocks = table_h.reshape(block_count, row_count, SMAX, HD)

    def project_qkv(weight_tuple):
        normed_here = layer_norm(
            tokens32, weight_tuple[4].astype(f32), weight_tuple[5].astype(f32)
        ).astype(bf16)
        bias_all = jnp.concatenate(
            [weight_tuple[6], jnp.zeros_like(weight_tuple[6]), weight_tuple[7]]
        ).astype(f32)
        mixed = (
            jnp.dot(normed_here, weight_tuple[0], preferred_element_type=f32) + bias_all
        ).astype(bf16)
        return (normed_here, mixed.reshape(group_count, 1, block_len, 3, head_groups, group_width))

    def split_heads(heads_all):
        q_all = heads_all[:, 0].reshape(block_count, row_count, SMAX, group_heads, HD)
        key_all = heads_all[:, 1].reshape(cap_tokens, group_heads, HD)
        value_all = heads_all[:, 2].reshape(cap_tokens, group_heads, HD)
        return (q_all, key_all, value_all)

    def score_block(q_rows, h_rows, key_all):
        dot_part = (
            jnp.einsum("rwhd,khd->hrwk", q_rows, key_all, preferred_element_type=f32) * score_scale
        )
        rel_h = jnp.einsum("rwhd,rkd->hrwk", q_rows, h_rows, preferred_element_type=f32)
        rel_w = jnp.einsum("rwhd,wkd->hrwk", q_rows, table_w, preferred_element_type=f32)
        rel_both = jnp.concatenate([rel_h, rel_w], axis=-1)
        combined = dot_part + split_product("hrwj,ju->hrwu", rel_both, expand)
        return jnp.where(key_valid, combined, -1e30)

    normed, sectioned = project_qkv(weights_fwd)
    heads_in = lax.all_to_all(sectioned, "ha", split_axis=4, concat_axis=1, tiled=True).reshape(
        cap_tokens, 3, group_width
    )
    q_all, key_all, value_all = split_heads(heads_in)

    def forward_block(inputs):
        q_rows, h_rows = inputs
        scores = score_block(q_rows, h_rows, key_all)
        top_score = jnp.max(scores, axis=-1, keepdims=True)
        expo = jnp.exp(scores - top_score)
        total = jnp.sum(expo, axis=-1, keepdims=True)
        probs = (expo / total).astype(bf16)
        attended = jnp.einsum("hrwk,khd->rwhd", probs, value_all, preferred_element_type=f32)
        return (
            attended.astype(bf16).reshape(row_count * SMAX, group_width),
            (top_score + jnp.log(total))[..., 0],
        )

    att_heads, log_sums = lax.map(forward_block, (q_all, h_blocks))
    att_back = lax.all_to_all(
        att_heads.reshape(group_count, head_groups, block_len, 1, group_width),
        "ha",
        split_axis=1,
        concat_axis=3,
        tiled=True,
    )
    att_tok = att_back.reshape(local_tokens, model_width)
    branch = jnp.dot(att_tok, proj_full, preferred_element_type=f32) + proj_shift.astype(f32)
    middle = tokens32 + tok_mask * branch
    normed2 = layer_norm(middle, second_gain.astype(f32), second_shift.astype(f32)).astype(bf16)
    hidden = jnp.dot(normed2, up_full, preferred_element_type=f32) + up_shift.astype(f32)
    activated = jax.nn.gelu(hidden, approximate=False).astype(bf16)
    block_out = (
        middle
        + tok_mask
        * (jnp.dot(activated, down_full, preferred_element_type=f32) + down_shift.astype(f32))
    ).astype(bf16)
    weights_bwd = gather_again(
        qkv_weight,
        proj_weight,
        fc1_weight,
        fc2_weight,
        norm1_gain,
        norm1_bias,
        query_bias,
        value_bias,
        proj_bias,
        norm2_gain,
        norm2_bias,
        fc1_bias,
        fc2_bias,
    )
    triple_back = weights_bwd[0]
    proj_back = weights_bwd[1]
    up_back = weights_bwd[2]
    down_back = weights_bwd[3]
    masked_cot = tok_mask * cot32
    down_in = masked_cot.astype(bf16)
    down_grad = contract_rows(activated, down_in)
    down_bias_grad = jnp.sum(masked_cot, axis=0)
    act_grad = contract_cols(down_in, down_back)
    gelu_value, gelu_pull = jax.vjp(partial(jax.nn.gelu, approximate=False), hidden)
    hidden_grad = gelu_pull(act_grad)[0].astype(bf16)
    up_grad = contract_rows(normed2, hidden_grad)
    up_bias_grad = jnp.sum(hidden_grad.astype(f32), axis=0)
    norm2_in = contract_cols(hidden_grad, up_back)
    norm2_value, norm2_pull = jax.vjp(
        layer_norm, middle, weights_bwd[9].astype(f32), weights_bwd[10].astype(f32)
    )
    mid_grad, second_gain_grad, second_shift_grad = norm2_pull(norm2_in)
    mid_total = cot32 + mid_grad
    branch_grad = (tok_mask * mid_total).astype(bf16)
    proj_grad = contract_rows(att_tok, branch_grad)
    proj_bias_grad = jnp.sum(branch_grad.astype(f32), axis=0)
    att_grad_tok = contract_cols(branch_grad, proj_back).astype(bf16)
    att_grad = lax.all_to_all(
        att_grad_tok.reshape(group_count, 1, block_len, head_groups, group_width),
        "ha",
        split_axis=3,
        concat_axis=1,
        tiled=True,
    )
    grad_rows = att_grad.reshape(block_count, row_count, SMAX, group_heads, HD)
    normed_use, sectioned_again = project_qkv(weights_bwd)
    heads_again = lax.all_to_all(
        sectioned_again, "ha", split_axis=4, concat_axis=1, tiled=True
    ).reshape(cap_tokens, 3, group_width)
    q_use, key_use, value_use = split_heads(heads_again)

    def backward_block(carry, inputs):
        key_grad, value_grad, width_table_grad = carry
        q_rows, h_rows, g_rows, lse_rows = inputs
        scores = score_block(q_rows, h_rows, key_use)
        probs = jnp.exp(scores - lse_rows[..., None])
        prob_grad = jnp.einsum("rwhd,khd->hrwk", g_rows, value_use, preferred_element_type=f32)
        row_dot = jnp.sum(probs * prob_grad, axis=-1, keepdims=True)
        score_grad = (probs * (prob_grad - row_dot)).astype(bf16)
        line_sums = jnp.einsum("hrwu,ju->hrwj", score_grad, expand, preferred_element_type=f32)
        height_grad = line_sums[..., :SMAX]
        width_grad = line_sums[..., SMAX:]
        query_grad = (
            score_scale
            * jnp.einsum("hrwk,khd->rwhd", score_grad, key_use, preferred_element_type=f32)
            + split_product("hrwj,rjd->rwhd", height_grad, h_rows)
            + split_product("hrwj,wjd->rwhd", width_grad, table_w)
        )
        key_grad = key_grad + score_scale * jnp.einsum(
            "hrwk,rwhd->khd", score_grad, q_rows, preferred_element_type=f32
        )
        value_grad = value_grad + jnp.einsum(
            "hrwk,rwhd->khd", probs.astype(bf16), g_rows, preferred_element_type=f32
        )
        h_table_grad = split_product("hrwj,rwhd->rjd", height_grad, q_rows)
        width_table_grad = width_table_grad + split_product("hrwj,rwhd->wjd", width_grad, q_rows)
        return ((key_grad, value_grad, width_table_grad), (query_grad, h_table_grad))

    zero_keys = jnp.zeros((cap_tokens, group_heads, HD), f32)
    zero_table = jnp.zeros((SMAX, SMAX, HD), f32)
    (key_grad, value_grad, width_table_grad), (query_grad, h_table_grad) = lax.scan(
        backward_block, (zero_keys, zero_keys, zero_table), (q_use, h_blocks, grad_rows, log_sums)
    )
    heads_grad = jnp.stack(
        [
            query_grad.reshape(cap_tokens, group_width),
            key_grad.reshape(cap_tokens, group_width),
            value_grad.reshape(cap_tokens, group_width),
        ],
        axis=1,
    ).astype(bf16)
    mixed_back = lax.all_to_all(
        heads_grad.reshape(group_count, head_groups, block_len, 3, 1, group_width),
        "ha",
        split_axis=1,
        concat_axis=4,
        tiled=True,
    )
    mixed_grad = mixed_back.reshape(local_tokens, 3 * model_width)
    triple_grad = contract_rows(normed_use, mixed_grad)
    mixed_float = mixed_grad.astype(f32)
    query_bias_grad = jnp.sum(mixed_float[:, :model_width], axis=0)
    value_bias_grad = jnp.sum(mixed_float[:, 2 * model_width :], axis=0)
    norm1_in = contract_cols(mixed_grad, triple_back)
    norm1_value, norm1_pull = jax.vjp(
        layer_norm, tokens32, weights_bwd[4].astype(f32), weights_bwd[5].astype(f32)
    )
    in_grad, first_gain_grad, first_shift_grad = norm1_pull(norm1_in)
    input_grad = (mid_total + in_grad).astype(bf16)
    height_rel_grad = jnp.einsum(
        "qkj,qkd->jd", matrix, h_table_grad.reshape(SMAX, SMAX, HD), precision=exact_mode
    )
    width_rel_grad = jnp.einsum("qkj,qkd->jd", matrix, width_table_grad, precision=exact_mode)
    summed = lax.psum(
        (
            first_gain_grad,
            first_shift_grad,
            query_bias_grad,
            value_bias_grad,
            proj_bias_grad,
            second_gain_grad,
            second_shift_grad,
            up_bias_grad,
            down_bias_grad,
            height_rel_grad,
            width_rel_grad,
        ),
        ("ga", "ha"),
    )

    def own_slice(vector):
        width_here = vector.shape[0] // head_groups
        return lax.dynamic_slice_in_dim(vector, head_index * width_here, width_here)

    column_sums = (
        lax.psum_scatter(triple_grad, "ga", scatter_dimension=1, tiled=True),
        lax.psum_scatter(proj_grad, "ga", scatter_dimension=1, tiled=True),
        lax.psum_scatter(up_grad, "ga", scatter_dimension=1, tiled=True),
        lax.psum_scatter(down_grad, "ga", scatter_dimension=1, tiled=True),
    )
    mat_grads = (
        lax.psum_scatter(
            column_sums[0].astype(jnp.bfloat16), "ha", scatter_dimension=0, tiled=True
        ).astype(jnp.float32),
        lax.psum_scatter(
            column_sums[1].astype(jnp.bfloat16), "ha", scatter_dimension=0, tiled=True
        ).astype(jnp.float32),
        lax.psum_scatter(
            column_sums[2].astype(jnp.bfloat16), "ha", scatter_dimension=0, tiled=True
        ).astype(jnp.float32),
        lax.psum_scatter(
            column_sums[3].astype(jnp.bfloat16), "ha", scatter_dimension=0, tiled=True
        ).astype(jnp.float32),
    )
    returned = (
        lax.all_to_all(
            block_out.reshape(1, local_tokens, model_width),
            "ga",
            split_axis=1,
            concat_axis=0,
            tiled=True,
        ),
        lax.all_to_all(
            input_grad.reshape(1, local_tokens, model_width),
            "ga",
            split_axis=1,
            concat_axis=0,
            tiled=True,
        ),
    )
    return (
        returned[0],
        returned[1],
        own_slice(summed[0]),
        own_slice(summed[1]),
        mat_grads[0],
        own_slice(summed[2]),
        own_slice(summed[3]),
        mat_grads[1],
        own_slice(summed[4]),
        own_slice(summed[5]),
        own_slice(summed[6]),
        mat_grads[2],
        own_slice(summed[7]),
        mat_grads[3],
        own_slice(summed[8]),
        summed[9],
        summed[10],
    )


def solution(mesh):
    placed = (
        P(None, ("ga", "ha"), None),
        P(None, ("ga", "ha"), None),
        P(),
        P("ha"),
        P("ha"),
        P("ha", "ga"),
        P("ha"),
        P("ha"),
        P("ha", "ga"),
        P("ha"),
        P("ha"),
        P("ha"),
        P("ha", "ga"),
        P("ha"),
        P("ha", "ga"),
        P("ha"),
        P(),
        P(),
    )
    return jax.shard_map(
        local,
        mesh=mesh,
        in_specs=placed,
        out_specs=(
            P(None, ("ga", "ha"), None),
            P(None, ("ga", "ha"), None),
            P("ha"),
            P("ha"),
            P("ha", "ga"),
            P("ha"),
            P("ha"),
            P("ha", "ga"),
            P("ha"),
            P("ha"),
            P("ha"),
            P("ha", "ga"),
            P("ha"),
            P("ha", "ga"),
            P("ha"),
            P(),
            P(),
        ),
        check_vma=False,
    )
```

profile of v0, /device:TPU:0, one launch (start us, length us, event | category | flops | bytes accessed | tf_op | source)
XLA Modules:
  0.0 1732.5 jit_solution(3867037603326788035)
XLA Ops:
  7.3 9.3 all_gather.66
  24.2 8.1 all_gather.75
  41.4 12.0 all-reduce.9
  55.2 20.9 %all-to-all-done = bf16[8,72,768]{2,1,0:T(8,128)(2,1)S(1)} async-done(((bf16[8,72,768]{2,1,0:T(8,128)(2,1)}), bf16[8,72,768]{2,1,0:T(8,128)(2,1)S(1)}, u32[]{:S(2)}, u32[]{:S(2)}) %all-to-all-start) | async-done | bytes 884768 | tf_op jit(solution)/shard_map/all_to_all | solution.py:203
  78.7 14.1 all-gather.6.cloned.1.call-done
  110.9 45.5 %all_gather.78 = bf16[3072,96]{0,1:T(8,128)(2,1)} all-gather(bf16[768,96]{0,1:T(8,128)(2,1)S(1)} %copy-done.39), channel_id=1, replica_groups=mesh['ga'=8,'ha'=4] {'ha'}, dimensions={0}, use_global_device_ids=true | all-gather | bytes 737280 | tf_op jit(solution)/shard_map/all_gather | solution.py:78
  180.8 221.2 %while.34 = (s32[]{:T(128)}, bf16[4,576,192]{2,1,0:T(8,128)(2,1)}, f32[4,3,12,48]{3,2,1,0:T(8,128)S(1)}, bf16[4,12,48,3,64]{4,2,1,3,0:T(8,128)(2,1)}, bf16[2304,...) while((s32[]{:T(128)}, bf16[4,576,192]{2,1,0:T(8,128)(2,1)}, ...), condition=%wide.region_5.6_spmd.clone.clone, body=%wide.region_2.5_spmd.clone.clone.sunk | while | flops 2612492288 | bytes 119442776 | solution.py:280
  184.2 7.9 fusion.306
  192.1 8.9 fusion.307
  201.6 18.3 %fusion.309 = (f32[3,12,48]{2,1,0:T(8,128)S(1)}, f32[3,12,48,2304]{3,2,1,0:T(8,128)}) fusion(f32[3,12,48,2304]{3,2,1,0:T(8,128)} %fusion.306, s32[2304]{0:T(1024)S(1)} %get-tuple-element.939, s32[2304]{0:T(1024)S(1)} %get-tuple-element.937, s32[96]{0:T(128)S(1)} %get-tuple-element.938, pred[96]{0:T(512)(128)(4,1)S(1)} %get-tuple-element.940, ...), kind=kOutput, calls=%fused_computation.293.clone.1 | convolution fusion | flops 786030912 | bytes 48467424 | tf_op jit(solution)/shard_map/while/body/eval_jaxpr/hrwj,ju->hrwu/dot_general | solution.py:54
  220.0 7.8 fusion.310
  227.8 7.0 fusion.311
  239.5 7.9 fusion.306
  247.3 8.9 fusion.307
  256.9 18.4 %fusion.309 = (f32[3,12,48]{2,1,0:T(8,128)S(1)}, f32[3,12,48,2304]{3,2,1,0:T(8,128)}) fusion(f32[3,12,48,2304]{3,2,1,0:T(8,128)} %fusion.306, s32[2304]{0:T(1024)S(1)} %get-tuple-element.939, s32[2304]{0:T(1024)S(1)} %get-tuple-element.937, s32[96]{0:T(128)S(1)} %get-tuple-element.938, pred[96]{0:T(512)(128)(4,1)S(1)} %get-tuple-element.940, ...), kind=kOutput, calls=%fused_computation.293.clone.1 | convolution fusion | flops 786030912 | bytes 48467424 | tf_op jit(solution)/shard_map/while/body/eval_jaxpr/hrwj,ju->hrwu/dot_general | solution.py:54
  275.3 7.9 fusion.310
  283.1 7.0 fusion.311
  294.9 7.9 fusion.306
  302.8 8.9 fusion.307
  312.3 18.3 %fusion.309 = (f32[3,12,48]{2,1,0:T(8,128)S(1)}, f32[3,12,48,2304]{3,2,1,0:T(8,128)}) fusion(f32[3,12,48,2304]{3,2,1,0:T(8,128)} %fusion.306, s32[2304]{0:T(1024)S(1)} %get-tuple-element.939, s32[2304]{0:T(1024)S(1)} %get-tuple-element.937, s32[96]{0:T(128)S(1)} %get-tuple-element.938, pred[96]{0:T(512)(128)(4,1)S(1)} %get-tuple-element.940, ...), kind=kOutput, calls=%fused_computation.293.clone.1 | convolution fusion | flops 786030912 | bytes 48467424 | tf_op jit(solution)/shard_map/while/body/eval_jaxpr/hrwj,ju->hrwu/dot_general | solution.py:54
  330.6 7.8 fusion.310
  350.1 7.9 fusion.306
  357.9 8.9 fusion.307
  367.5 18.3 %fusion.309 = (f32[3,12,48]{2,1,0:T(8,128)S(1)}, f32[3,12,48,2304]{3,2,1,0:T(8,128)}) fusion(f32[3,12,48,2304]{3,2,1,0:T(8,128)} %fusion.306, s32[2304]{0:T(1024)S(1)} %get-tuple-element.939, s32[2304]{0:T(1024)S(1)} %get-tuple-element.937, s32[96]{0:T(128)S(1)} %get-tuple-element.938, pred[96]{0:T(512)(128)(4,1)S(1)} %get-tuple-element.940, ...), kind=kOutput, calls=%fused_computation.293.clone.1 | convolution fusion | flops 786030912 | bytes 48467424 | tf_op jit(solution)/shard_map/while/body/eval_jaxpr/hrwj,ju->hrwu/dot_general | solution.py:54
  385.8 7.8 fusion.310
  409.3 16.7 all-gather
  437.5 8.8 fusion.189
  446.4 22.9 %convert_reduce_fusion = (f32[3072]{0:T(1024)}, bf16[576,3072]{1,0:T(8,128)(2,1)S(1)}, f32[576,3072]{1,0:T(8,128)}) fusion(f32[576,3072]{1,0:T(8,128)} %fusion.189, f32[3072]{0:T(1024)S(1)} %bitcast.379, bf16[576,768]{1,0:T(8,128)(2,1)S(1)} %copy-done.27, bf16[3072,768]{0,1:T(8,128)(2,1)} %all-gather.12.cloned.1.call-done), kind=kOutput, calls=%fused_computation.149 | convolution fusion | flops 2850616320 | bytes 23322624 | tf_op jit(solution)/shard_map/dot_general | solution.py:46
  489.1 11.8 all-to-all-done.5
  511.9 384.5 %while.35 = (s32[]{:T(128)}, f32[2304,3,64]{0,2,1:T(8,128)}, f32[2304,3,64]{0,2,1:T(8,128)S(1)}, f32[48,48,64]{2,1,0:T(8,128)}, bf16[4,12,48,3,64]{4,2,1,3,0:T(8...) while((s32[]{:T(128)}, f32[2304,3,64]{0,2,1:T(8,128)}, ...), condition=%wide.region_12.13_spmd.clone.clone, body=%wide.region_10.12_spmd.clone.clone.sunk | while | flops 4999574528 | bytes 259564624 | solution.py:380
  513.2 8.7 fusion.343
  525.0 7.9 fusion.345
  532.9 8.9 fusion.346
  542.5 23.5 %multiply_reduce_fusion.8 = (f32[3,12,48]{2,1,0:T(8,128)S(1)}, f32[3,12,48,2304]{3,2,1,0:T(8,128)}) fusion(f32[3,12,48,2304]{3,2,1,0:T(8,128)} %fusion.343, f32[3,12,48]{2,1,0:T(8,128)S(1)} %dynamic-slice_bitcast_fusion.8, f32[3,12,48,2304]{3,2,1,0:T(8,128)} %fusion.345, s32[2304]{0:T(1024)S(1)} %get-tuple-element.998, ...), kind=kOutput, calls=%fused_computation.51.clone.1 | convolution fusion | flops 793993536 | bytes 64399584 | tf_op jit(solution)/shard_map/while/body/eval_jaxpr/hrwj,ju->hrwu/dot_general | solution.py:54
  565.9 14.2 multiply_convert_fusion.5
  586.2 7.9 fusion.349
  609.1 8.7 fusion.343
  620.9 7.9 fusion.345
  628.8 8.9 fusion.346
  638.4 23.1 %multiply_reduce_fusion.8 = (f32[3,12,48]{2,1,0:T(8,128)S(1)}, f32[3,12,48,2304]{3,2,1,0:T(8,128)}) fusion(f32[3,12,48,2304]{3,2,1,0:T(8,128)} %fusion.343, f32[3,12,48]{2,1,0:T(8,128)S(1)} %dynamic-slice_bitcast_fusion.8, f32[3,12,48,2304]{3,2,1,0:T(8,128)} %fusion.345, s32[2304]{0:T(1024)S(1)} %get-tuple-element.998, ...), kind=kOutput, calls=%fused_computation.51.clone.1 | convolution fusion | flops 793993536 | bytes 64399584 | tf_op jit(solution)/shard_map/while/body/eval_jaxpr/hrwj,ju->hrwu/dot_general | solution.py:54
  661.5 14.2 multiply_convert_fusion.5
  682.2 7.9 fusion.349
  705.1 8.7 fusion.343
  716.9 7.9 fusion.345
  724.8 8.9 fusion.346
  734.4 23.1 %multiply_reduce_fusion.8 = (f32[3,12,48]{2,1,0:T(8,128)S(1)}, f32[3,12,48,2304]{3,2,1,0:T(8,128)}) fusion(f32[3,12,48,2304]{3,2,1,0:T(8,128)} %fusion.343, f32[3,12,48]{2,1,0:T(8,128)S(1)} %dynamic-slice_bitcast_fusion.8, f32[3,12,48,2304]{3,2,1,0:T(8,128)} %fusion.345, s32[2304]{0:T(1024)S(1)} %get-tuple-element.998, ...), kind=kOutput, calls=%fused_computation.51.clone.1 | convolution fusion | flops 793993536 | bytes 64399584 | tf_op jit(solution)/shard_map/while/body/eval_jaxpr/hrwj,ju->hrwu/dot_general | solution.py:54
  757.5 14.2 multiply_convert_fusion.5
  778.2 7.9 fusion.349
  801.1 8.7 fusion.343
  812.9 7.9 fusion.345
  820.8 8.9 fusion.346
  830.4 23.1 %multiply_reduce_fusion.8 = (f32[3,12,48]{2,1,0:T(8,128)S(1)}, f32[3,12,48,2304]{3,2,1,0:T(8,128)}) fusion(f32[3,12,48,2304]{3,2,1,0:T(8,128)} %fusion.343, f32[3,12,48]{2,1,0:T(8,128)S(1)} %dynamic-slice_bitcast_fusion.8, f32[3,12,48,2304]{3,2,1,0:T(8,128)} %fusion.345, s32[2304]{0:T(1024)S(1)} %get-tuple-element.998, ...), kind=kOutput, calls=%fused_computation.51.clone.1 | convolution fusion | flops 793993536 | bytes 64399584 | tf_op jit(solution)/shard_map/while/body/eval_jaxpr/hrwj,ju->hrwu/dot_general | solution.py:54
  853.5 14.2 multiply_convert_fusion.5
  874.2 7.9 fusion.349
  927.6 39.8 %all-to-all-done.6 = bf16[8,4,72,3,1,192]{5,2,0,4,3,1:T(8,128)(2,1)} async-done(((bf16[8,4,72,3,1,192]{5,2,0,4,3,1:T(8,128)(2,1)}), bf16[8,4,72,3,1,192]{5,2,0,4,3,1:T(8,128)(2,1)}, u32[]{:S(2)}, u32[]{:S(2)}) %all-to-all-start.6) | async-done | bytes 2654240 | tf_op jit(solution)/shard_map/all_to_all | solution.py:391
  988.3 8.5 fusion.188
  1033.9 82.8 %reduce-scatter.13.cloned.1.call-done = f32[768,288]{0,1:T(8,128)} async-done(((f32[768,2304]{0,1:T(8,128)}), f32[768,288]{0,1:T(8,128)}) %reduce-scatter.13.cloned.1.call-update) | async-done | bytes 884752 | tf_op jit(solution)/shard_map/reduce_scatter | solution.py:435
  1139.1 164.2 %reduce-scatter.17.cloned.1.call-done = f32[768,384]{1,0:T(8,128)} async-done(((f32[768,3072]{1,0:T(8,128)}), f32[768,384]{1,0:T(8,128)}) %reduce-scatter.17.cloned.1.call-update) | async-done | bytes 1179664 | tf_op jit(solution)/shard_map/reduce_scatter | solution.py:437
  1322.7 166.4 %reduce-scatter.21.cloned.1.call-done = f32[3072,96]{0,1:T(8,128)} async-done(((f32[3072,768]{0,1:T(8,128)}), f32[3072,96]{0,1:T(8,128)}) %reduce-scatter.21.cloned.1.call-update) | async-done | bytes 1179664 | tf_op jit(solution)/shard_map/reduce_scatter | solution.py:438
  1496.4 129.1 %all-reduce.12.cloned.1.call-done = (f32[768]{0:T(1024)}, f32[768]{0:T(1024)}, f32[768]{0:T(1024)}, f32[768]{0:T(1024)}, f32[768]{0:T(1024)}, /*index=5*/f32[768...) async-done(((f32[768]{0:T(1024)}, f32[768]{0:T(1024)}, f32[768]{0:T(1024)}, f32[768]{0:T(1024)}, ...) | async-done | bytes 85520 | tf_op jit(solution)/shard_map/psum | solution.py:413
  1639.3 10.0 reduce-scatter.27.cloned.1.call-done
  1650.9 23.0 %reduce-scatter.25.cloned.1.call-done = bf16[192,288]{1,0:T(8,128)(2,1)} async-done(((bf16[768,288]{1,0:T(8,128)(2,1)}), bf16[192,288]{1,0:T(8,128)(2,1)}) %reduce-scatter.25.cloned.1.call-update) | async-done | bytes 110608
  1675.7 22.6 %reduce-scatter.19.cloned.1.call-done = bf16[192,384]{1,0:T(8,128)(2,1)} async-done(((bf16[768,384]{1,0:T(8,128)(2,1)}), bf16[192,384]{1,0:T(8,128)(2,1)}) %reduce-scatter.19.cloned.1.call-update) | async-done | bytes 147472 | tf_op jit(solution)/shard_map/reduce_scatter | solution.py:447
  1699.9 23.0 %reduce-scatter.23.cloned.1.call-done = bf16[768,96]{0,1:T(8,128)(2,1)} async-done(((bf16[3072,96]{0,1:T(8,128)(2,1)}), bf16[768,96]{0,1:T(8,128)(2,1)}) %reduce-scatter.23.cloned.1.call-update) | async-done | bytes 147472 | tf_op jit(solution)/shard_map/reduce_scatter | solution.py:450
  (525 shorter events, 406.1 us)
Async XLA Ops:
  7.2 153.8 %copy-start = (bf16[95,64]{0,1:T(8,128)(2,1)S(1)}, bf16[95,64]{0,1:T(8,128)(2,1)}, u32[]{:S(2)}) copy-start(bf16[95,64]{0,1:T(8,128)(2,1)} %param.38) | copy-start | bytes 36484
  7.2 10.5 copy-start.52
  7.2 17.0 copy-start.38
  7.2 85.5 %all-gather.6.cloned.1.call-start = ((), (), s32[]{:S(2)}) async-start(), calls=%async_computation.16 | async-start | bytes 3981312 | tf_op jit(solution)/shard_map/all_gather | solution.py:90
  17.6 415.7 %all-gather.8.cloned.1.call-start = ((), (), s32[]{:S(2)}) async-start(), calls=%async_computation.17 | async-start | bytes 1327104 | tf_op jit(solution)/shard_map/all_gather | solution.py:91
  23.3 14.9 copy-start.87
  23.3 16.2 copy-start.78
  23.3 16.4 copy-start.79
  23.3 16.6 copy-start.80
  23.3 16.9 copy-start.81
  23.3 17.1 copy-start.82
  23.3 17.3 %copy-start.83 = (bf16[192]{0:T(256)(128)(2,1)S(1)}, bf16[192]{0:T(256)(128)(2,1)}, u32[]{:S(2)}) copy-start(bf16[192]{0:T(256)(128)(2,1)} %param.33) | copy-start | bytes 1156
  23.3 17.6 %copy-start.84 = (bf16[192]{0:T(256)(128)(2,1)S(1)}, bf16[192]{0:T(256)(128)(2,1)}, u32[]{:S(2)}) copy-start(bf16[192]{0:T(256)(128)(2,1)} %param.32) | copy-start | bytes 1156
  23.4 17.8 %copy-start.85 = (bf16[192]{0:T(256)(128)(2,1)S(1)}, bf16[192]{0:T(256)(128)(2,1)}, u32[]{:S(2)}) copy-start(bf16[192]{0:T(256)(128)(2,1)} %param.37) | copy-start | bytes 1156
  24.2 413.3 %all-gather.10.cloned.1.call-start = ((), (), s32[]{:S(2)}) async-start(), calls=%async_computation.18 | async-start | bytes 5308416 | tf_op jit(solution)/shard_map/all_gather | solution.py:92
  32.4 43.7 %all-to-all-start = ((bf16[8,72,768]{2,1,0:T(8,128)(2,1)}), bf16[8,72,768]{2,1,0:T(8,128)(2,1)S(1)}, u32[]{:S(2)}, u32[]{:S(2)}) async-start(bf16[8,72,768]{2,1,0:T(8,128)(2,1)} %param.22), calls=%async_computation | async-start | bytes 1769472 | tf_op jit(solution)/shard_map/all_to_all | solution.py:203
  76.1 21.1 %copy-start.6 = (bf16[8,72,768]{2,1,0:T(8,128)(2,1)}, bf16[8,72,768]{2,1,0:T(8,128)(2,1)S(1)}, u32[]{:S(2)}) copy-start(bf16[8,72,768]{2,1,0:T(8,128)(2,1)S(1)} %all-to-all-done) | copy-start | bytes 2654212
  76.3 16.4 copy-start.48
  78.1 14.7 copy-start.53
  106.0 50.5 %copy-start.86 = (s32[8]{0:T(128)S(1)}, s32[8]{0:T(128)}, u32[]{:S(2)}) copy-start(s32[8]{0:T(128)} %param.24) | copy-start | bytes 100
  106.0 57.9 %all-to-all-start.1 = ((bf16[8,1,72,3,4,192]{5,2,0,3,1,4:T(8,128)(2,1)}), bf16[8,1,72,3,4,192]{5,2,0,3,1,4:T(8,128)(2,1)}, u32[]{:S(2)}, u32[]{:S(2)}) async-start(bf16[8,1,72,3,4,192]{5,2,0,3,1,4:T(8,128)(2,1)} %copy.284), calls=%async_computation.1 | async-start | bytes 7077888 | tf_op jit(solution)/shard_map/all_to_all | solution.py:262
  110.8 335.5 %all-gather.12.cloned.1.call-start = ((), (), s32[]{:S(2)}) async-start(), calls=%async_computation.19 | async-start | bytes 5308416 | tf_op jit(solution)/shard_map/all_gather | solution.py:93
  163.9 240.8 %all-to-all-start.4 = ((bf16[8,72,768]{2,1,0:T(8,128)(2,1)}), bf16[8,72,768]{2,1,0:T(8,128)(2,1)}, u32[]{:S(2)}, u32[]{:S(2)}) async-start(bf16[8,72,768]{2,1,0:T(8,128)(2,1)} %param.23), calls=%async_computation.4 | async-start | bytes 1769472 | tf_op jit(solution)/shard_map/all_to_all | solution.py:204
  404.7 24.4 %all-to-all-start.2 = ((bf16[8,4,72,1,192]{4,2,0,3,1:T(8,128)(2,1)}), bf16[8,4,72,1,192]{4,2,0,3,1:T(8,128)(2,1)}, u32[]{:S(2)}, u32[]{:S(2)}) async-start(bf16[8,4,72,1,192]{4,2,0,3,1:T(8,128)(2,1)} %copy.291), calls=%async_computation.2 | async-start | bytes 2359296 | tf_op jit(solution)/shard_map/all_to_all | solution.py:281
  409.3 28.2 %copy-start.36 = (f32[768]{0:T(1024)}, f32[768]{0:T(1024)S(1)}, u32[]{:S(2)}) copy-start(f32[768]{0:T(1024)S(1)} %convert_element_type.251) | copy-start | bytes 9220
  409.3 63.8 %copy-start.32 = (f32[768]{0:T(1024)}, f32[768]{0:T(1024)S(1)}, u32[]{:S(2)}) copy-start(f32[768]{0:T(1024)S(1)} %convert_element_type.250) | copy-start | bytes 9220
  426.0 20.3 %copy-start.50 = (f32[4,1,768]{2,1,0:T(1,128)}, f32[4,1,768]{2,1,0:T(1,128)S(1)}, u32[]{:S(2)}) copy-start(f32[4,1,768]{2,1,0:T(1,128)S(1)} %convert_element_type.298) | copy-start | bytes 36868
  426.7 47.2 %copy-start.55 = (f32[576]{0:T(1024)}, f32[576]{0:T(1024)S(1)}, u32[]{:S(2)}) copy-start(f32[576]{0:T(1024)S(1)} %fusion.183) | copy-start | bytes 6916
  435.9 37.2 %copy-start.30 = (f32[576]{0:T(1024)}, f32[576]{0:T(1024)S(1)}, u32[]{:S(2)}) copy-start(f32[576]{0:T(1024)S(1)} %broadcast_multiply_fusion) | copy-start | bytes 6916
  437.5 35.7 %copy-start.34 = (f32[576]{0:T(1024)}, f32[576]{0:T(1024)S(1)}, u32[]{:S(2)}) copy-start(f32[576]{0:T(1024)S(1)} %fusion.184) | copy-start | bytes 6916
  437.5 8.9 copy-start.27
  446.3 22.9 %copy-start.12 = (f32[576,768]{1,0:T(8,128)S(1)}, f32[576,768]{1,0:T(8,128)}, u32[]{:S(2)}) copy-start(f32[576,768]{1,0:T(8,128)} %copy-done.11) | copy-start | bytes 5308420
  446.4 22.9 %copy-start.75 = (bf16[768,3072]{1,0:T(8,128)(2,1)S(1)}, bf16[768,3072]{1,0:T(8,128)(2,1)}, u32[]{:S(2)}) copy-start(bf16[768,3072]{1,0:T(8,128)(2,1)} %all-gather.10.cloned.1.call-done) | copy-start | bytes 14155780
  480.7 20.2 %all-to-all-start.5 = ((bf16[8,1,72,4,192]{4,2,0,1,3:T(8,128)(2,1)}), bf16[8,1,72,4,192]{4,2,0,1,3:T(8,128)(2,1)}, u32[]{:S(2)}, u32[]{:S(2)}) async-start(bf16[8,1,72,4,192]{4,2,0,1,3:T(8,128)(2,1)} %copy.295), calls=%async_computation.5 | async-start | bytes 2359296 | tf_op jit(solution)/shard_map/all_to_all | solution.py:337
  485.0 546.6 %reduce-scatter.15.cloned.1.call-start = ((), (), s32[]{:S(2)}) async-start(), calls=%async_computation.21 | async-start | bytes 2654208 | tf_op jit(solution)/shard_map/reduce_scatter | solution.py:436
  580.1 14.0 slice-start
  586.2 7.9 slice-start.1
  675.6 14.5 slice-start
  682.2 7.9 slice-start.1
  771.7 14.5 slice-start
  778.2 7.9 slice-start.1
  867.7 14.5 slice-start
  874.2 7.9 slice-start.1
  921.3 46.1 %all-to-all-start.6 = ((bf16[8,4,72,3,1,192]{5,2,0,4,3,1:T(8,128)(2,1)}), bf16[8,4,72,3,1,192]{5,2,0,4,3,1:T(8,128)(2,1)}, u32[]{:S(2)}, u32[]{:S(2)}) async-start(bf16[8,4,72,3,1,192]{5,2,0,4,3,1:T(8,128)(2,1)} %copy.302), calls=%async_computation.6 | async-start | bytes 7077888 | tf_op jit(solution)/shard_map/all_to_all | solution.py:391
  926.2 190.5 %reduce-scatter.13.cloned.1.call-start = ((), (), s32[]{:S(2)}) async-start(), calls=%async_computation.20 | async-start | bytes 7962624 | tf_op jit(solution)/shard_map/reduce_scatter | solution.py:435
  979.9 6.9 copy-start.16
  986.8 316.4 %reduce-scatter.17.cloned.1.call-start = ((), (), s32[]{:S(2)}) async-start(), calls=%async_computation.22 | async-start | bytes 10616832 | tf_op jit(solution)/shard_map/reduce_scatter | solution.py:437
  996.8 492.3 %reduce-scatter.21.cloned.1.call-start = ((), (), s32[]{:S(2)}) async-start(), calls=%async_computation.24 | async-start | bytes 10616832 | tf_op jit(solution)/shard_map/reduce_scatter | solution.py:438
  997.5 8.8 copy-start.28
  1012.5 613.0 %all-reduce.12.cloned.1.call-start = ((), (), s32[]{:S(2)}) async-start(), calls=%async_computation.28 | async-start | bytes 221184 | tf_op jit(solution)/shard_map/psum | solution.py:413
  1013.5 7.5 copy-start.5
  1027.2 6.7 copy-start.70
  1031.5 617.7 %reduce-scatter.27.cloned.1.call-start = ((), (), s32[]{:S(2)}) async-start(), calls=%async_computation.27 | async-start | bytes 245760
  1032.6 86.4 %copy-start.56 = (f32[576]{0:T(1024)S(1)}, f32[576]{0:T(1024)}, u32[]{:S(2)}) copy-start(f32[576]{0:T(1024)} %copy-done.55) | copy-start | bytes 6916
  1033.4 640.4 %reduce-scatter.25.cloned.1.call-start = ((), (), s32[]{:S(2)}) async-start(), calls=%async_computation.26 | async-start | bytes 737280
  1133.3 5.7 copy-start.54
  1134.4 171.0 %copy-start.68 = (f32[576]{0:T(1024)S(1)}, f32[576]{0:T(1024)}, u32[]{:S(2)}) copy-start(f32[576]{0:T(1024)} %rsqrt.26) | copy-start | bytes 6916
  1134.4 184.5 %all-to-all-start.3 = ((bf16[8,2,27648]{2,1,0:T(2,128)(2,1)}), bf16[8,2,27648]{2,1,0:T(2,128)(2,1)}, u32[]{:S(2)}, u32[]{:S(2)}) async-start(bf16[8,2,27648]{2,1,0:T(2,128)(2,1)} %reshape.534), calls=%async_computation.3 | async-start | bytes 1769472 | tf_op jit(solution)/shard_map/all_to_all | solution.py:455
  1138.8 559.5 %reduce-scatter.19.cloned.1.call-start = ((), (), s32[]{:S(2)}) async-start(), calls=%async_computation.23 | async-start | bytes 737280 | tf_op jit(solution)/shard_map/reduce_scatter | solution.py:447
  1319.0 318.5 %all-to-all-start.7 = ((bf16[8,2,27648]{2,1,0:T(2,128)(2,1)}), bf16[8,2,27648]{2,1,0:T(2,128)(2,1)S(1)}, u32[]{:S(2)}, u32[]{:S(2)}) async-start(bf16[8,2,27648]{2,1,0:T(2,128)(2,1)} %reshape.536), calls=%async_computation.7 | async-start | bytes 1769472 | tf_op jit(solution)/shard_map/all_to_all | solution.py:462
  1322.7 400.2 %reduce-scatter.23.cloned.1.call-start = ((), (), s32[]{:S(2)}) async-start(), calls=%async_computation.25 | async-start | bytes 737280 | tf_op jit(solution)/shard_map/reduce_scatter | solution.py:450
  1638.2 87.6 %copy-start.1 = (bf16[95,64]{0,1:T(8,128)(2,1)S(1)}, bf16[95,64]{0,1:T(8,128)(2,1)}, u32[]{:S(2)}) copy-start(bf16[95,64]{0,1:T(8,128)(2,1)} %param.38) | copy-start | bytes 36484
  1638.2 86.3 %copy-start.62 = (f32[95,64]{0,1:T(8,128)S(1)}, f32[95,64]{0,1:T(8,128)}, u32[]{:S(2)}) copy-start(f32[95,64]{0,1:T(8,128)} %get-tuple-element.1017) | copy-start | bytes 72964
  1638.2 86.9 %copy-start.61 = (f32[95,64]{0,1:T(8,128)S(1)}, f32[95,64]{0,1:T(8,128)}, u32[]{:S(2)}) copy-start(f32[95,64]{0,1:T(8,128)} %get-tuple-element.1018) | copy-start | bytes 72964
  (68 other events, 203.6 us)
Sparse Core Ops, SparseCore 0:
  17.8 74.9 all-gather.5
  95.5 40.0 all-gather.7
  137.7 92.8 all-gather.9
  232.6 79.0 all-gather.11
  489.2 71.3 reduce-scatter.14
  986.9 129.6 reduce-scatter.12
  1120.3 182.9 reduce-scatter.16
  1306.8 182.2 reduce-scatter.20
  1497.2 128.2 all-reduce.11
  1628.4 20.7 reduce-scatter.26
  1651.7 22.0 reduce-scatter.24
  1676.2 22.0 reduce-scatter.18
  1700.8 22.0 reduce-scatter.22
where the time goes:
time: 1740 us; the launch traced here: 1730 us
  waiting for transfers between devices  708 us (41%)
  matrix products  583 us (34%)
  other arithmetic  149 us (9%)
  local copies, waits for them, and re-layouts  140 us (8%)
  blocking collectives  97.2 us (6%)
  starting transfers between devices  38 us (2%)
    dot_general x24, matrix products, split_product(): jnp.einsum(form, lower_part, narrow, preferred_element_type=jnp.float32)  179 us
    reduce_scatter x1, waiting for transfers between devices, local(): lax.psum_scatter(down_grad, 'ga', scatter_dimension=1, tiled=True)  166 us
    reduce_scatter x1, waiting for transfers between devices, local(): lax.psum_scatter(up_grad, 'ga', scatter_dimension=1, tiled=True)  164 us
    psum x1, waiting for transfers between devices, local(): lax.psum((first_gain_grad, first_shift_grad, query_bias_grad, value_bias_...  129 us
    reduce_scatter x1, waiting for transfers between devices, local(): lax.psum_scatter(triple_grad, 'ga', scatter_dimension=1, tiled=True)  82.8 us
    dot_general x24, matrix products, split_product(): jnp.einsum(form, upper_part, narrow, preferred_element_type=jnp.float32)  77.7 us
    dot_general x8, matrix products, score_block(): jnp.einsum('rwhd,khd->hrwk', q_rows, key_all, preferred_element_type=f32)  71 us
    convert_element_type x4, other arithmetic, backward_block(): score_grad = (probs * (prob_grad - row_dot)).astype(bf16)  56.7 us
  transfers between devices with their start and end apart: 21, of which 12 were waited for; matrix products, arithmetic and copies ran while one was open for 48% of the time, Pallas kernels for 0%

commit v1 on v0

v1 whole, which is shorter than its diff:
```python
from functools import partial

import jax
import jax.numpy as jnp
from jax import lax
from jax.experimental import pallas as pl
from jax.experimental.pallas import tpu as pltpu
from jax.sharding import PartitionSpec as P

HEADS = 12
HD = 64
SMAX = 48
BOTH = ("ga", "ha")


exact_mode = lax.Precision.HIGHEST


TBLK = 256
UBLK = 768

NT = (((1,), (1,)), ((), ()))


def mm(left, right):
    return jnp.dot(left, right, preferred_element_type=jnp.float32)


def mm_nt(left, right):
    return lax.dot_general(left, right, NT, preferred_element_type=jnp.float32)


def forward_kernel(q_ref, k_ref, v_ref, out_ref, lse_ref):
    heads = q_ref.shape[0]
    dim = 64
    outs = []
    for h in range(heads):
        scores = mm_nt(k_ref[h], q_ref[h])
        top = jnp.max(scores, axis=0, keepdims=True)
        expo = jnp.exp(scores - top).astype(jnp.bfloat16)
        mixed = mm(v_ref[h], expo)
        total = mixed[dim : dim + 1]
        outs.append((mixed[:dim] / total).T.astype(jnp.bfloat16))
        lse_ref[h] = top + jnp.log(total)
    out_ref[...] = jnp.concatenate(outs, axis=1)


def attend_forward(q_aug, k_aug, v_aug):
    heads, tokens, depth = q_aug.shape
    dim = 64
    return pl.pallas_call(
        forward_kernel,
        grid=(tokens // TBLK,),
        in_specs=[
            pl.BlockSpec((heads, TBLK, depth), lambda t: (0, t, 0)),
            pl.BlockSpec((heads, tokens, depth), lambda t: (0, 0, 0)),
            pl.BlockSpec((heads, v_aug.shape[1], tokens), lambda t: (0, 0, 0)),
        ],
        out_specs=[
            pl.BlockSpec((TBLK, heads * dim), lambda t: (t, 0)),
            pl.BlockSpec((heads, 1, TBLK), lambda t: (0, 0, t)),
        ],
        out_shape=[
            jax.ShapeDtypeStruct((tokens, heads * dim), jnp.bfloat16),
            jax.ShapeDtypeStruct((heads, 1, tokens), jnp.float32),
        ],
        name="attend_forward",
        compiler_params=pltpu.CompilerParams(dimension_semantics=("arbitrary",)),
    )(q_aug, k_aug, v_aug)


def backward_kernel(
    q_ref, g_ref, lse_ref, delta_ref, k_ref, v_ref, kt_ref, dq_ref, line_ref, dkv_ref
):
    heads, tokens, depth = k_ref.shape
    dim = 64
    blk = q_ref.shape[1]

    @pl.when(pl.program_id(0) == 0)
    def _():
        dkv_ref[...] = jnp.zeros_like(dkv_ref)

    for h in range(heads):
        q_here = q_ref[h]
        g_here = g_ref[h]
        zero = jnp.zeros((blk, dim), jnp.bfloat16)
        g_wide = jnp.concatenate([g_here, zero], axis=1)
        q_wide = jnp.concatenate([zero, q_here[:, :dim]], axis=1)
        lse = lse_ref[h]
        delta = delta_ref[h]
        total = None
        for c in range(tokens // UBLK):
            span = pl.ds(c * UBLK, UBLK)
            scores = mm_nt(k_ref[h, span, :], q_here)
            probs = jnp.exp(scores - lse)
            pgrad = mm_nt(v_ref[h, span, :], g_here)
            sgrad = (probs * (pgrad - delta)).astype(jnp.bfloat16)
            dkv_ref[h, span, :] += mm(probs.astype(jnp.bfloat16), g_wide) + mm(sgrad, q_wide)
            part = mm(kt_ref[h, :, span], sgrad)
            total = part if total is None else total + part
        dq_ref[h] = total[:dim].T
        line_ref[h] = total[dim:].T.astype(jnp.bfloat16)


def attend_backward(q_aug, grads, lse, delta, k_aug, values, k_turn):
    heads, tokens, depth = q_aug.shape
    dim = 64
    lines = k_turn.shape[1] - dim
    return pl.pallas_call(
        backward_kernel,
        grid=(tokens // TBLK,),
        in_specs=[
            pl.BlockSpec((heads, TBLK, depth), lambda t: (0, t, 0)),
            pl.BlockSpec((heads, TBLK, dim), lambda t: (0, t, 0)),
            pl.BlockSpec((heads, 1, TBLK), lambda t: (0, 0, t)),
            pl.BlockSpec((heads, 1, TBLK), lambda t: (0, 0, t)),
            pl.BlockSpec((heads, tokens, depth), lambda t: (0, 0, 0)),
            pl.BlockSpec((heads, tokens, dim), lambda t: (0, 0, 0)),
            pl.BlockSpec((heads, dim + lines, tokens), lambda t: (0, 0, 0)),
        ],
        out_specs=[
            pl.BlockSpec((heads, TBLK, dim), lambda t: (0, t, 0)),
            pl.BlockSpec((heads, TBLK, lines), lambda t: (0, t, 0)),
            pl.BlockSpec((heads, tokens, 2 * dim), lambda t: (0, 0, 0)),
        ],
        out_shape=[
            jax.ShapeDtypeStruct((heads, tokens, dim), jnp.float32),
            jax.ShapeDtypeStruct((heads, tokens, lines), jnp.bfloat16),
            jax.ShapeDtypeStruct((heads, tokens, 2 * dim), jnp.float32),
        ],
        name="attend_backward",
        compiler_params=pltpu.CompilerParams(dimension_semantics=("arbitrary",)),
    )(q_aug, grads, lse, delta, k_aug, values, k_turn)


def layer_norm(values, gain, shift):
    center = values - jnp.mean(values, axis=-1, keepdims=True)
    spread = jnp.mean(center * center, axis=-1, keepdims=True)
    return center * lax.rsqrt(spread + 1e-06) * gain + shift


def interp_matrix(img_side):
    coord = jnp.arange(SMAX, dtype=jnp.int32)
    length_in = 2 * SMAX - 1
    length_out = 2 * img_side - 1
    offset = jnp.clip(coord[:, None] - coord[None, :] + img_side - 1, 0, length_out - 1)
    numer = jnp.maximum((2 * offset + 1) * length_in - length_out, 0)
    lower = numer // (2 * length_out)
    weight_hi = (numer - lower * 2 * length_out).astype(jnp.float32) / (2 * length_out).astype(
        jnp.float32
    )
    upper = jnp.minimum(lower + 1, length_in - 1)
    target = jnp.arange(length_in, dtype=jnp.int32)
    lower_hot = (target == lower[..., None]).astype(jnp.float32)
    upper_hot = (target == upper[..., None]).astype(jnp.float32)
    return (1.0 - weight_hi)[..., None] * lower_hot + weight_hi[..., None] * upper_hot


def contract_rows(left, right):
    return lax.dot_general(
        left, right, (((0,), (0,)), ((), ())), preferred_element_type=jnp.float32
    )


def contract_cols(left, right):
    return lax.dot_general(
        left, right, (((1,), (1,)), ((), ())), preferred_element_type=jnp.float32
    )


def exchange(values, axis):
    return lax.all_to_all(values, axis, split_axis=0, concat_axis=0, tiled=True)


def spread(values, axis):
    count = lax.axis_size(axis)
    return exchange(jnp.broadcast_to(values, (count,) + values.shape), axis)


def pack_up(piece):
    rows, width = piece.shape[-2:]
    lead = piece.shape[:-2]
    fold = 4 * rows // width
    cut = piece.reshape(lead + (fold, rows // fold, width))
    return jnp.swapaxes(cut, -3, -2).reshape(lead + (rows // fold, fold * width))


def unpack_up(packed, rows, width):
    fold = packed.shape[-1] // width
    lead = packed.shape[:-2]
    cut = packed.reshape(lead + (rows // fold, fold, width))
    return jnp.swapaxes(cut, -3, -2).reshape(lead + (rows, width))


def local(
    patches,
    cotangent,
    sides,
    norm1_gain,
    norm1_bias,
    qkv_weight,
    query_bias,
    value_bias,
    proj_weight,
    proj_bias,
    norm2_gain,
    norm2_bias,
    fc1_weight,
    fc1_bias,
    fc2_weight,
    fc2_bias,
    rel_height,
    rel_width,
):
    group_count = lax.axis_size("ga")
    head_groups = lax.axis_size("ha")
    group_index = lax.axis_index("ga")
    head_index = lax.axis_index("ha")
    device_count = group_count * head_groups
    block_len = patches.shape[1]
    model_width = patches.shape[2]
    hidden_width = fc1_bias.shape[0] * head_groups
    local_tokens = group_count * block_len
    group_width = model_width // head_groups
    group_heads = HEADS // head_groups
    cap_tokens = SMAX * SMAX
    f32 = jnp.float32
    bf16 = jnp.bfloat16

    triple_rows = lax.all_gather(qkv_weight, "ga", axis=1, tiled=True)
    triple_cut = triple_rows.reshape(group_width, 3, head_groups, group_width).transpose(2, 0, 1, 3)
    triple_own = exchange(
        triple_cut.reshape(head_groups, group_width, 3 * group_width), "ha"
    ).reshape(model_width, 3 * group_width)

    up_rows, up_cols = fc1_weight.shape
    out_cols = fc2_weight.shape[1]
    packed = jnp.concatenate(
        [
            pack_up(fc1_weight),
            fc2_weight.T,
            proj_weight.T.reshape(out_cols // head_groups, model_width),
        ],
        axis=0,
    )
    pack_rows = packed.shape[0]
    up_height = up_rows * up_cols // model_width

    vectors = jnp.concatenate(
        [norm1_gain, norm1_bias, proj_bias, norm2_gain, norm2_bias, fc2_bias, fc1_bias]
    )
    vectors_all = lax.all_gather(vectors, "ha", axis=0, tiled=False)
    wide = model_width // head_groups

    def vector_at(slot, width):
        return vectors_all[:, slot * wide : slot * wide + width].reshape(-1)

    first_gain = vector_at(0, wide)
    first_shift = vector_at(1, wide)
    proj_shift = vector_at(2, wide)
    second_gain = vector_at(3, wide)
    second_shift = vector_at(4, wide)
    down_shift = vector_at(5, wide)
    up_shift = vector_at(6, 4 * wide)

    tokens_in = lax.all_to_all(patches, "ga", split_axis=0, concat_axis=1, tiled=True)[0]
    cot_in = lax.all_to_all(cotangent, "ga", split_axis=0, concat_axis=1, tiled=True)[0]
    tokens32 = tokens_in.astype(f32)
    cot32 = cot_in.astype(f32)
    slot_index = jnp.arange(local_tokens, dtype=jnp.int32)
    grid_index = (
        slot_index // block_len * head_groups + head_index
    ) * block_len + slot_index % block_len
    img_side = lax.dynamic_index_in_dim(sides, group_index, 0, keepdims=False)
    tok_mask = ((grid_index // SMAX < img_side) & (grid_index % SMAX < img_side)).astype(f32)[
        :, None
    ]
    all_index = jnp.arange(cap_tokens, dtype=jnp.int32)[:, None]
    line_index = jnp.arange(2 * SMAX, dtype=jnp.int32)[None, :]
    expand = jnp.where(
        line_index < SMAX,
        all_index // SMAX == line_index,
        all_index % SMAX == line_index - SMAX,
    ).astype(bf16)
    line_valid = line_index[0] % SMAX < img_side
    matrix = interp_matrix(img_side)
    table_h = jnp.einsum(
        "qkj,jd->qkd", matrix, rel_height.astype(f32), precision=exact_mode
    ).astype(bf16)
    table_w = jnp.einsum("qkj,jd->qkd", matrix, rel_width.astype(f32), precision=exact_mode).astype(
        bf16
    )

    normed = layer_norm(tokens32, first_gain.astype(f32), first_shift.astype(f32)).astype(bf16)
    normed_all = (
        spread(normed, "ha")
        .reshape(head_groups, group_count, block_len, model_width)
        .transpose(1, 0, 2, 3)
        .reshape(cap_tokens, model_width)
    )
    bias_own = jnp.concatenate([query_bias, jnp.zeros_like(query_bias), value_bias]).astype(f32)
    mixed = (jnp.dot(normed_all, triple_own, preferred_element_type=f32) + bias_own).astype(bf16)
    by_head = mixed.reshape(cap_tokens, 3, group_heads, HD).transpose(1, 2, 0, 3)
    q_all, key_all, value_all = by_head[0], by_head[1], by_head[2]

    q_grid = q_all.reshape(group_heads, SMAX, SMAX, HD)
    rel_h = jnp.einsum("hrwd,rkd->hrwk", q_grid, table_h, preferred_element_type=f32)
    rel_w = jnp.einsum("hrwd,wkd->hrwk", q_grid, table_w, preferred_element_type=f32)
    rel_both = jnp.concatenate([rel_h, rel_w], axis=-1).reshape(
        group_heads, cap_tokens, 2 * SMAX
    )
    rel_upper = lax.reduce_precision(rel_both, 8, 7)
    rel_lower = jnp.where(line_valid, rel_both - rel_upper, 0.0).astype(bf16)
    rel_upper = jnp.where(line_valid, rel_upper, -1e30).astype(bf16)
    q_aug = jnp.concatenate([q_all * jnp.asarray(HD**-0.5, bf16), rel_upper, rel_lower], axis=-1)
    expand_all = jnp.broadcast_to(expand, (group_heads,) + expand.shape)
    k_aug = jnp.concatenate([key_all, expand_all, expand_all], axis=-1)
    v_aug = jnp.concatenate(
        [
            value_all.swapaxes(1, 2),
            jnp.ones((group_heads, 1, cap_tokens), bf16),
            jnp.zeros((group_heads, 15, cap_tokens), bf16),
        ],
        axis=1,
    )
    k_turn = jnp.concatenate([key_all, expand_all], axis=-1).swapaxes(1, 2)
    att_heads, log_sums = attend_forward(q_aug, k_aug, v_aug)

    gathered = lax.all_gather(packed, BOTH, axis=0, tiled=False).reshape(
        group_count, head_groups, pack_rows, model_width
    )
    up_full = (
        unpack_up(gathered[:, :, :up_height], up_rows, up_cols)
        .transpose(1, 2, 0, 3)
        .reshape(model_width, hidden_width)
    )
    down_turn = (
        gathered[:, :, up_height : up_height + out_cols]
        .transpose(0, 2, 1, 3)
        .reshape(model_width, hidden_width)
    )
    proj_turn = (
        gathered[:, :, up_height + out_cols :]
        .reshape(group_count, head_groups, out_cols, group_width)
        .transpose(0, 2, 1, 3)
        .reshape(model_width, model_width)
    )

    att_back = lax.all_to_all(
        att_heads.reshape(group_count, head_groups, block_len, 1, group_width),
        "ha",
        split_axis=1,
        concat_axis=3,
        tiled=True,
    )
    att_tok = att_back.reshape(local_tokens, model_width)
    branch = contract_cols(att_tok, proj_turn) + proj_shift.astype(f32)
    middle = tokens32 + tok_mask * branch
    normed2 = layer_norm(middle, second_gain.astype(f32), second_shift.astype(f32)).astype(bf16)
    hidden = jnp.dot(normed2, up_full, preferred_element_type=f32) + up_shift.astype(f32)
    activated = jax.nn.gelu(hidden, approximate=False).astype(bf16)
    block_out = (
        middle + tok_mask * (contract_cols(activated, down_turn) + down_shift.astype(f32))
    ).astype(bf16)
    out_back = exchange(block_out.reshape(group_count, block_len, model_width), "ga")

    masked_cot = tok_mask * cot32
    down_in = masked_cot.astype(bf16)
    down_grad = contract_rows(down_in, activated).astype(bf16)
    down_bias_grad = jnp.sum(masked_cot, axis=0)
    act_grad = jnp.dot(down_in, down_turn, preferred_element_type=f32)
    gelu_value, gelu_pull = jax.vjp(partial(jax.nn.gelu, approximate=False), hidden)
    hidden_grad = gelu_pull(act_grad)[0].astype(bf16)
    up_grad = contract_rows(normed2, hidden_grad).astype(bf16)
    up_bias_grad = jnp.sum(hidden_grad.astype(f32), axis=0)
    norm2_in = contract_cols(hidden_grad, up_full)
    norm2_value, norm2_pull = jax.vjp(
        layer_norm, middle, second_gain.astype(f32), second_shift.astype(f32)
    )
    mid_grad, second_gain_grad, second_shift_grad = norm2_pull(norm2_in)
    mid_total = cot32 + mid_grad
    branch_grad = (tok_mask * mid_total).astype(bf16)
    proj_grad = contract_rows(branch_grad, att_tok).astype(bf16)
    proj_bias_grad = jnp.sum(branch_grad.astype(f32), axis=0)
    att_grad_tok = jnp.dot(branch_grad, proj_turn, preferred_element_type=f32).astype(bf16)
    att_grad = lax.all_to_all(
        att_grad_tok.reshape(group_count, 1, block_len, head_groups, group_width),
        "ha",
        split_axis=3,
        concat_axis=1,
        tiled=True,
    ).reshape(cap_tokens, group_width)

    grads_packed = jnp.concatenate(
        [
            pack_up(
                up_grad.reshape(head_groups, up_rows, group_count, up_cols).transpose(2, 0, 1, 3)
            ),
            down_grad.reshape(group_count, out_cols, head_groups, model_width).transpose(
                0, 2, 1, 3
            ),
            proj_grad.reshape(group_count, out_cols, head_groups, group_width)
            .transpose(0, 2, 1, 3)
            .reshape(group_count, head_groups, out_cols // head_groups, model_width),
        ],
        axis=2,
    ).reshape(device_count * pack_rows, model_width)
    grads_own = lax.psum_scatter(grads_packed, BOTH, scatter_dimension=0, tiled=True)
    up_own = unpack_up(grads_own[:up_height], up_rows, up_cols).astype(f32)
    down_own = grads_own[up_height : up_height + out_cols].T.astype(f32)
    proj_own = grads_own[up_height + out_cols :].reshape(out_cols, group_width).T.astype(f32)

    def reduce_vectors(vectors_in):
        stacked = jnp.concatenate(
            [
                vector.reshape(head_groups, group_count, -1)
                .transpose(1, 0, 2)
                .reshape(device_count, -1)
                for vector in vectors_in
            ],
            axis=1,
        )
        part = jnp.sum(exchange(stacked[:, None], BOTH), axis=0)
        own = spread(part, "ga")[:, 0]
        result = []
        at = 0
        for vector in vectors_in:
            size = vector.shape[0] // device_count
            result.append(own[:, at : at + size].reshape(-1))
            at += size
        return result

    early = reduce_vectors(
        [proj_bias_grad, second_gain_grad, second_shift_grad, down_bias_grad, up_bias_grad]
    )

    grad_heads = att_grad.reshape(cap_tokens, group_heads, HD)
    delta = (
        jnp.sum(
            grad_heads.astype(f32) * att_heads.reshape(cap_tokens, group_heads, HD).astype(f32),
            axis=-1,
        )
        .transpose(1, 0)
        .reshape(group_heads, 1, cap_tokens)
    )
    query_part, line_sums, dkv = attend_backward(
        q_aug, grad_heads.transpose(1, 0, 2), log_sums, delta, k_aug, value_all, k_turn
    )
    lines = line_sums.reshape(group_heads, SMAX, SMAX, 2 * SMAX)
    height_grad = lines[..., :SMAX]
    width_grad = lines[..., SMAX:]
    query_grad = (
        HD**-0.5 * query_part.reshape(group_heads, SMAX, SMAX, HD)
        + jnp.einsum("hrwj,rjd->hrwd", height_grad, table_h, preferred_element_type=f32)
        + jnp.einsum("hrwj,wjd->hrwd", width_grad, table_w, preferred_element_type=f32)
    ).reshape(group_heads, cap_tokens, HD)
    h_table_grad = jnp.einsum("hrwj,hrwd->rjd", height_grad, q_grid, preferred_element_type=f32)
    w_table_grad = jnp.einsum("hrwj,hrwd->wjd", width_grad, q_grid, preferred_element_type=f32)
    mixed_grad = (
        jnp.stack([query_grad, dkv[..., HD:], dkv[..., :HD]])
        .astype(bf16)
        .transpose(2, 0, 1, 3)
        .reshape(cap_tokens, 3 * group_width)
    )
    norm1_part = contract_cols(mixed_grad, triple_own).astype(bf16)
    norm1_in = jnp.sum(
        exchange(
            norm1_part.reshape(group_count, head_groups, block_len, model_width)
            .transpose(1, 0, 2, 3)
            .reshape(head_groups, local_tokens, model_width),
            "ha",
        ).astype(f32),
        axis=0,
    )
    triple_part = contract_rows(normed_all, mixed_grad).astype(bf16)
    triple_rows_grad = (
        exchange(triple_part.reshape(head_groups, group_width, 3 * group_width), "ha")
        .reshape(head_groups, group_width, 3, group_width)
        .transpose(1, 2, 0, 3)
        .reshape(group_width, group_count, 3 * model_width // group_count)
        .transpose(1, 0, 2)
    )
    triple_grad = jnp.sum(exchange(triple_rows_grad, "ga").astype(f32), axis=0)
    mixed_float = mixed_grad.astype(f32)
    bias_part = jnp.concatenate(
        [
            jnp.sum(mixed_float[:, :group_width], axis=0),
            jnp.sum(mixed_float[:, 2 * group_width :], axis=0),
        ]
    )
    bias_sum = jnp.sum(spread(bias_part[None], "ga"), axis=0)[0]
    height_rel = jnp.einsum("qkj,qkd->jd", matrix, h_table_grad, precision=exact_mode)
    width_rel = jnp.einsum("qkj,qkd->jd", matrix, w_table_grad, precision=exact_mode)
    rel_flat = jnp.concatenate([height_rel, width_rel]).reshape(-1)
    rel_size = rel_flat.shape[0]
    chunk = -(-rel_size // (128 * device_count)) * 128
    rel_flat = jnp.pad(rel_flat, (0, chunk * device_count - rel_size))
    rel_part = jnp.sum(exchange(rel_flat.reshape(device_count, 1, chunk), BOTH), axis=0)
    rel_sum = spread(rel_part, BOTH).reshape(-1)[:rel_size].reshape(2, 2 * SMAX - 1, HD)

    norm1_value, norm1_pull = jax.vjp(
        layer_norm, tokens32, first_gain.astype(f32), first_shift.astype(f32)
    )
    in_grad, first_gain_grad, first_shift_grad = norm1_pull(norm1_in)
    input_grad = (mid_total + in_grad).astype(bf16)
    in_back = exchange(input_grad.reshape(group_count, block_len, model_width), "ga")
    late = reduce_vectors([first_gain_grad, first_shift_grad])
    return (
        out_back,
        in_back,
        late[0],
        late[1],
        triple_grad,
        bias_sum[:group_width],
        bias_sum[group_width:],
        proj_own,
        early[0],
        early[1],
        early[2],
        up_own,
        early[4],
        down_own,
        early[3],
        rel_sum[0],
        rel_sum[1],
    )


def solution(mesh):
    placed = (
        P(None, ("ga", "ha"), None),
        P(None, ("ga", "ha"), None),
        P(),
        P("ha"),
        P("ha"),
        P("ha", "ga"),
        P("ha"),
        P("ha"),
        P("ha", "ga"),
        P("ha"),
        P("ha"),
        P("ha"),
        P("ha", "ga"),
        P("ha"),
        P("ha", "ga"),
        P("ha"),
        P(),
        P(),
    )
    return jax.shard_map(
        local,
        mesh=mesh,
        in_specs=placed,
        out_specs=(
            P(None, ("ga", "ha"), None),
            P(None, ("ga", "ha"), None),
            P("ha"),
            P("ha"),
            P("ha", "ga"),
            P("ha"),
            P("ha"),
            P("ha", "ga"),
            P("ha"),
            P("ha"),
            P("ha"),
            P("ha", "ga"),
            P("ha"),
            P("ha", "ga"),
            P("ha"),
            P(),
            P(),
        ),
        check_vma=False,
    )
```

time: 1740 us -> 740 us (0.43)
  waiting for transfers between devices: 708 us -> 169 us
  matrix products: 583 us -> 82.4 us
  Pallas kernels: 0 us -> 86.1 us
  other arithmetic: 149 us -> 68.5 us
  blocking collectives: 97.2 us -> 41.8 us
  local copies, waits for them, and re-layouts: 140 us -> 187 us
  starting transfers between devices: 38 us -> 79.1 us
    dot_general x101 -> x9, matrix products: 513 us -> 36.7 us  [the longest x1 19.6 us: local(): act_grad = jnp.dot(down_in, down_turn, preferred_element_type=f32)]
    reduce_scatter x6 -> x1, waiting for transfers between devices: 459 us -> 0.01 us  [local(): lax.psum_scatter(grads_packed, BOTH, scatter_dimension=0, tiled=True)]
    psum x1 -> x0, waiting for transfers between devices: 129 us -> none  [local(): lax.psum((first_gain_grad, first_shift_grad, query_bias_grad, value_bias_...]
    all_to_all x6 -> x16, waiting for transfers between devices: 60.7 us -> 161 us  [the longest x14 138 us: exchange(): return lax.all_to_all(values, axis, split_axis=0, concat_axis=0, tiled=True)]
    pallas_call x0 -> x2, Pallas kernels: none -> 86.1 us  [the longest x1 48.4 us: attend_backward(): pl.pallas_call(backward_kernel, grid=(tokens // TBLK,), in_specs=[pl.Bloc...]
    convert_element_type x22 -> x6, other arithmetic: 73.6 us -> 6.5 us  [the longest x1 2.51 us: local(): rel_upper = jnp.where(line_valid, rel_upper, -1e+30).astype(bf16)]
    all_gather x5 -> x2, blocking collectives: 85.2 us -> 41.8 us  [the longest x1 36.6 us: local(): triple_rows = lax.all_gather(qkv_weight, 'ga', axis=1, tiled=True)]
    all_to_all x6 -> x16, starting transfers between devices: 27.9 us -> 70.8 us  [the longest x14 58.3 us: exchange(): return lax.all_to_all(values, axis, split_axis=0, concat_axis=0, tiled=True)]
  transfers between devices with their start and end apart: 21 -> 20, of which waited for: 12 -> 15; matrix products, arithmetic and copies ran while one was open for 48% -> 31% of each run, Pallas kernels for 0% -> 12%
where the time goes in v1:
time: 740 us; the launch traced here: 730 us
  local copies, waits for them, and re-layouts  187 us (25%)
  waiting for transfers between devices  169 us (23%)
  Pallas kernels  86.1 us (12%)
  matrix products  82.4 us (11%)
  starting transfers between devices  79.1 us (11%)
  other arithmetic  68.5 us (9%)
  blocking collectives  41.8 us (6%)
  between operations  16.5 us (2%)
    all_to_all x14, waiting for transfers between devices, exchange(): return lax.all_to_all(values, axis, split_axis=0, concat_axis=0, tiled=True)  138 us
    all_to_all x14, starting transfers between devices, exchange(): return lax.all_to_all(values, axis, split_axis=0, concat_axis=0, tiled=True)  58.3 us
    pallas_call x1, Pallas kernels, attend_backward(): pl.pallas_call(backward_kernel, grid=(tokens // TBLK,), in_specs=[pl.Bloc...  48.4 us
    pallas_call x1, Pallas kernels, attend_forward(): pl.pallas_call(forward_kernel, grid=(tokens // TBLK,), in_specs=[pl.Block...  37.7 us
    all_gather x1, blocking collectives, local(): triple_rows = lax.all_gather(qkv_weight, 'ga', axis=1, tiled=True)  36.6 us
    unnamed x183, local copies, waits for them, and re-layouts  28.5 us
    all_to_all x1, waiting for transfers between devices, local(): lax.all_to_all(patches, 'ga', split_axis=0, concat_axis=1, tiled=True)[0]  23.2 us
    dot_general x1, matrix products, local(): act_grad = jnp.dot(down_in, down_turn, preferred_element_type=f32)  19.6 us
  transfers between devices with their start and end apart: 20, of which 15 were waited for; matrix products, arithmetic and copies ran while one was open for 31% of the time, Pallas kernels for 12%

profile of v1, /device:TPU:0, one launch (start us, length us, event | category | flops | bytes accessed | tf_op | source)
XLA Modules:
  0.0 730.2 jit_solution(11272133017877062684)
XLA Ops:
  11.1 7.3 %all-to-all-start = ((bf16[8,72,768]{2,1,0:T(8,128)(2,1)}), bf16[8,72,768]{2,1,0:T(8,128)(2,1)S(1)}, u32[]{:S(2)}, u32[]{:S(2)}) async-start(bf16[8,72,768]{2,1,0:T(8,128)(2,1)} %param.18), calls=%async_computation | async-start | bytes 1769472 | tf_op jit(solution)/shard_map/all_to_all | solution.py:266
  18.6 5.2 all-gather.2
  24.7 23.2 %all-to-all-done = bf16[8,72,768]{2,1,0:T(8,128)(2,1)S(1)} async-done(((bf16[8,72,768]{2,1,0:T(8,128)(2,1)}), bf16[8,72,768]{2,1,0:T(8,128)(2,1)S(1)}, u32[]{:S(2)}, u32[]{:S(2)}) %all-to-all-start) | async-done | bytes 884768 | tf_op jit(solution)/shard_map/all_to_all | solution.py:266
  52.3 4.9 all-to-all-start.1
  59.0 36.6 %all_gather.17 = bf16[192,2304]{0,1:T(8,128)(2,1)S(1)} all-gather(bf16[192,288]{0,1:T(8,128)(2,1)S(1)} %copy.272), channel_id=1, replica_groups=mesh['ga'=8,'ha'=4] {'ga'}, dimensions={1}, use_global_device_ids=true | all-gather | bytes 995328 | tf_op jit(solution)/shard_map/all_gather | solution.py:230
  106.8 10.5 %all-to-all-done.1 = bf16[4,576,768]{2,1,0:T(8,128)(2,1)} async-done(((bf16[4,576,768]{2,1,0:T(8,128)(2,1)}), bf16[4,576,768]{2,1,0:T(8,128)(2,1)}, u32[]{:S(2)}, u32[]{:S(2)}) %all-to-all-start.1) | async-done | bytes 3538976 | tf_op jit(solution)/shard_map/all_to_all | solution.py:172
  117.4 3.5 all-to-all-start.2
  121.9 4.1 copy.271
  126.0 8.6 %all-to-all-done.2 = bf16[4,192,576]{2,1,0:T(8,128)(2,1)S(1)} async-done(((bf16[4,192,576]{2,1,0:T(8,128)(2,1)}), bf16[4,192,576]{2,1,0:T(8,128)(2,1)S(1)}, u32[]{:S(2)}, u32[]{:S(2)}) %all-to-all-start.2) | async-done | bytes 884768 | tf_op jit(solution)/shard_map/all_to_all | solution.py:172
  134.6 5.2 all-to-all-start.5
  139.8 4.3 add_convert_fusion.1
  146.2 4.2 reshape_squeeze.3
  150.5 3.7 copy.278
  170.7 5.8 copy.282.k_ref
  176.4 5.3 pad_maximum_fusion.2.q_ref
  183.0 37.7 %attend_forward.1 = (bf16[2304,192]{1,0:T(8,128)(2,1)}, f32[3,1,2304]{2,1,0:T(1,128)}) custom-call(bf16[3,2304,256]{2,1,0:T(8,128)(2,1)} %pad_maximum_fusion.2.q_ref, bf16[3,2304,256]{2,1,0:T(8,128)(2,1)} %copy.282.k_ref, bf16[3,80,2304]{2,1,0:T(8,128)(2,1)} %maximum_maximum_fusion.v_ref), custom_call_target="tpu_custom_call" | custom-call | tf_op jit(solution)/shard_map/attend_forward/pallas_call | solution.py:51
  223.1 4.7 all-to-all-start.3
  237.5 6.2 all-to-all-done.3
  249.6 8.1 %fusion.87 = (bf16[8,4,96,768]{3,2,1,0:T(8,128)(2,1)}, bf16[8,4,96,768]{3,2,1,0:T(8,128)(2,1)}) fusion(bf16[8,4,216,768]{3,2,1,0:T(8,128)(2,1)} %bitcast.252), kind=kLoop, calls=%fused_computation.206 | loop fusion | bytes 18874368 | tf_op jit(solution)/shard_map/slice | solution.py:333
  257.8 10.1 %reshape.701 = bf16[8,4,96,2,384]{4,3,2,1,0:T(2,128)(2,1)} reshape(bf16[8,4,96,768]{3,2,1,0:T(8,128)(2,1)} %get-tuple-element.128) | data formatting | bytes 9437184 | tf_op jit(solution)/shard_map/reshape | solution.py:191
  267.9 5.2 copy.339
  273.1 3.4 copy.348
  281.2 3.1 reshape.700
  287.7 3.6 copy.344
  295.5 19.6 %convert_reduce_fusion.2 = (f32[3072]{0:T(1024)S(1)}, bf16[576,3072]{1,0:T(8,128)(2,1)S(1)}, f32[576,3072]{1,0:T(8,128)S(1)}) fusion(f32[576,3072]{1,0:T(8,128)S(1)} %fusion.84, f32[3072]{0:T(1024)S(1)} %reshape.752, bf16[576,768]{1,0:T(8,128)(2,1)S(1)} %bitcast.288, bf16[768,3072]{1,0:T(8,128)(2,1)S(1)} %bitcast.263), kind=kOutput, calls=%fused_computation.5 | convolution fusion | flops 2850616320 | bytes 23322624 | tf_op jit(solution)/shard_map/dot_general | solution.py:371
  315.2 4.4 multiply_reduce_fusion
  319.6 6.2 convolution_convert_fusion.2
  325.8 3.5 multiply_convert_fusion
  337.0 5.5 all-to-all-start.14
  342.6 7.7 %convolution_convert_fusion.1 = bf16[768,3072]{1,0:T(8,128)(2,1)} fusion(bf16[576,768]{1,0:T(8,128)(2,1)S(1)} %get-tuple-element.143, bf16[576,3072]{1,0:T(8,128)(2,1)} %multiply_convert_fusion), kind=kOutput, calls=%fused_computation.26 | convolution fusion | flops 2720268288 | bytes 9142272 | tf_op jit(solution)/shard_map/dot_general | solution.py:160
  351.4 3.4 copy.350
  354.8 9.4 %copy.311 = bf16[8,4,96,2,384]{4,3,1,2,0:T(2,128)(2,1)} copy(bf16[8,4,96,2,384]{4,0,2,3,1:T(8,128)(2,1)} %bitcast.242) | data formatting | bytes 9437184 | tf_op jit(solution)/shard_map/transpose | solution.py:185
  364.2 12.0 %reshape.724 = bf16[8,4,96,768]{3,1,2,0:T(4,128)(2,1)} reshape(bf16[8,4,96,2,384]{4,3,1,2,0:T(2,128)(2,1)} %copy.311) | data formatting | bytes 9437184 | tf_op jit(solution)/shard_map/reshape | solution.py:185
  384.4 9.8 %reshape.725 = bf16[8,96,4,768]{3,2,1,0:T(4,128)(2,1)} reshape(bf16[768,3072]{1,0:T(8,128)(2,1)} %convolution_convert_fusion.1) | data formatting | bytes 9437184 | tf_op jit(solution)/shard_map/reshape | solution.py:399
  394.1 3.5 all-to-all-start.6
  397.7 9.1 %pad_maximum_fusion = bf16[8,4,216,768]{3,1,2,0:T(4,128)(2,1)S(1)} fusion(bf16[8,4,24,768]{3,1,2,0:T(4,128)(2,1)S(1)} %copy.313, bf16[8,4,96,768]{3,1,2,0:T(4,128)(2,1)} %bitcast.245, bf16[8,4,96,768]{3,1,2,0:T(4,128)(2,1)} %reshape.724), kind=kLoop, calls=%fused_computation | loop fusion | flops 10616832 | bytes 21233664 | tf_op jit(solution)/shard_map/concatenate | solution.py:394
  406.8 5.0 copy.314
  414.1 5.9 all-to-all-start.15
  428.7 48.4 %attend_backward.1 = (f32[3,2304,64]{2,1,0:T(8,128)}, bf16[3,2304,96]{2,1,0:T(8,128)(2,1)}, f32[3,2304,128]{2,1,0:T(8,128)}) custom-call(bf16[3,2304,256]{2,1,0:T(8,128)(2,1)} %pad_maximum_fusion.2.q_ref, bf16[3,2304,64]{2,1,0:T(8,128)(2,1)} %bitcast.258, f32[3,1,2304]{2,1,0:T(1,128)} %get-tuple-element.23.lse_ref, f32[3,1,2304]{2,1,0:T(1,128)} %reshape.707.delta_ref, ...), custom_call_target="tpu_custom_call" | custom-call | tf_op jit(solution)/shard_map/attend_backward/pallas_call | solution.py:109
  487.2 3.3 maximum_bitcast_fusion
  490.5 6.9 copy.302
  501.9 3.4 fusion.31
  506.1 3.4 fusion.28
  510.4 5.1 all-to-all-start.16
  515.6 7.9 %all-to-all-done.16 = f32[32,1,384]{2,1,0:T(1,128)S(1)} async-done(((f32[32,1,384]{2,1,0:T(1,128)}), f32[32,1,384]{2,1,0:T(1,128)S(1)}, u32[]{:S(2)}, u32[]{:S(2)}) %all-to-all-start.16) | async-done | bytes 49184 | tf_op jit(solution)/shard_map/all_to_all | solution.py:172
  524.1 3.3 all-to-all-start.13
  527.5 6.7 all-to-all-done.13
  534.9 3.3 all-to-all-start.17
  538.2 4.2 convolution_convert_fusion.5
  545.6 4.4 all-to-all-start.11
  550.0 4.5 convolution_convert_fusion
  556.6 7.2 all-to-all-done.11
  563.8 3.9 all-to-all-start.7
  567.8 7.8 %add_convert_fusion.2 = bf16[576,768]{1,0:T(8,128)(2,1)} fusion(f32[576,768]{1,0:T(8,128)} %copy-done.12, bf16[576,3072]{1,0:T(8,128)(2,1)} %multiply_convert_fusion, bf16[768,3072]{1,0:T(8,128)(2,1)} %bitcast.264, f32[768]{0:T(1024)S(1)} %reshape.753, f32[576]{0:T(1024)S(1)} %copy-done.63), kind=kOutput, calls=%fused_computation.66 | convolution fusion | flops 2719678464 | bytes 10917120 | tf_op jit(solution)/shard_map/dot_general | solution.py:166
  575.6 33.2 %all-to-all-done.7 = bf16[4,576,768]{2,1,0:T(8,128)(2,1)S(1)} async-done(((bf16[4,576,768]{2,1,0:T(8,128)(2,1)}), bf16[4,576,768]{2,1,0:T(8,128)(2,1)S(1)}, u32[]{:S(2)}, u32[]{:S(2)}) %all-to-all-start.7) | async-done | bytes 3538976 | tf_op jit(solution)/shard_map/all_to_all | solution.py:172
  610.6 4.2 all-to-all-start.4
  614.9 3.8 convert_reduce_fusion
  621.2 16.0 %all-to-all-done.4 = bf16[8,72,768]{2,1,0:T(8,128)(2,1)} async-done(((bf16[8,72,768]{2,1,0:T(8,128)(2,1)}), bf16[8,72,768]{2,1,0:T(8,128)(2,1)}, u32[]{:S(2)}, u32[]{:S(2)}) %all-to-all-start.4) | async-done | bytes 884768 | tf_op jit(solution)/shard_map/all_to_all | solution.py:172
  647.1 4.2 all-to-all-start.12
  651.6 28.7 %all-to-all-done.12 = bf16[8,192,288]{1,2,0:T(8,128)(2,1)} async-done(((bf16[8,192,288]{1,2,0:T(8,128)(2,1)}), bf16[8,192,288]{1,2,0:T(8,128)(2,1)}, u32[]{:S(2)}, u32[]{:S(2)}) %all-to-all-start.12) | async-done | bytes 884768 | tf_op jit(solution)/shard_map/all_to_all | solution.py:172
  680.8 3.6 all-to-all-start.10
  687.5 3.4 all-to-all-done.10
  690.9 3.6 all-to-all-start.8
  704.7 11.2 %all-to-all-done.8 = bf16[8,72,768]{2,1,0:T(8,128)(2,1)S(1)} async-done(((bf16[8,72,768]{2,1,0:T(8,128)(2,1)}), bf16[8,72,768]{2,1,0:T(8,128)(2,1)S(1)}, u32[]{:S(2)}, u32[]{:S(2)}) %all-to-all-start.8) | async-done | bytes 884768 | tf_op jit(solution)/shard_map/all_to_all | solution.py:172
  (359 shorter events, 158.4 us)
Async XLA Ops:
  7.2 96.0 %copy-start = (bf16[95,64]{0,1:T(8,128)(2,1)S(1)}, bf16[95,64]{0,1:T(8,128)(2,1)}, u32[]{:S(2)}) copy-start(bf16[95,64]{0,1:T(8,128)(2,1)} %param.34) | copy-start | bytes 36484
  7.2 239.7 %all-gather.5.cloned.1.call-start = ((), (), s32[]{:S(2)}) async-start(), calls=%async_computation.20 | async-start | bytes 10948608 | tf_op jit(solution)/shard_map/all_gather | solution.py:329
  7.3 11.2 %copy-start.66 = (bf16[768]{0:T(1024)(128)(2,1)S(1)}, bf16[768]{0:T(1024)(128)(2,1)}, u32[]{:S(2)}) copy-start(bf16[768]{0:T(1024)(128)(2,1)} %param.31) | copy-start | bytes 4612
  7.3 11.2 %copy-start.67 = (bf16[192]{0:T(256)(128)(2,1)S(1)}, bf16[192]{0:T(256)(128)(2,1)}, u32[]{:S(2)}) copy-start(bf16[192]{0:T(256)(128)(2,1)} %param.21) | copy-start | bytes 1156
  7.3 11.2 %copy-start.68 = (bf16[192]{0:T(256)(128)(2,1)S(1)}, bf16[192]{0:T(256)(128)(2,1)}, u32[]{:S(2)}) copy-start(bf16[192]{0:T(256)(128)(2,1)} %param.22) | copy-start | bytes 1156
  7.3 11.2 %copy-start.69 = (bf16[192]{0:T(256)(128)(2,1)S(1)}, bf16[192]{0:T(256)(128)(2,1)}, u32[]{:S(2)}) copy-start(bf16[192]{0:T(256)(128)(2,1)} %param.27) | copy-start | bytes 1156
  7.3 11.2 %copy-start.70 = (bf16[192]{0:T(256)(128)(2,1)S(1)}, bf16[192]{0:T(256)(128)(2,1)}, u32[]{:S(2)}) copy-start(bf16[192]{0:T(256)(128)(2,1)} %param.28) | copy-start | bytes 1156
  7.3 11.2 %copy-start.71 = (bf16[192]{0:T(256)(128)(2,1)S(1)}, bf16[192]{0:T(256)(128)(2,1)}, u32[]{:S(2)}) copy-start(bf16[192]{0:T(256)(128)(2,1)} %param.29) | copy-start | bytes 1156
  7.3 11.2 %copy-start.72 = (bf16[192]{0:T(256)(128)(2,1)S(1)}, bf16[192]{0:T(256)(128)(2,1)}, u32[]{:S(2)}) copy-start(bf16[192]{0:T(256)(128)(2,1)} %param.33) | copy-start | bytes 1156
  11.1 36.8 %all-to-all-start = ((bf16[8,72,768]{2,1,0:T(8,128)(2,1)}), bf16[8,72,768]{2,1,0:T(8,128)(2,1)S(1)}, u32[]{:S(2)}, u32[]{:S(2)}) async-start(bf16[8,72,768]{2,1,0:T(8,128)(2,1)} %param.18), calls=%async_computation | async-start | bytes 1769472 | tf_op jit(solution)/shard_map/all_to_all | solution.py:266
  24.6 25.7 %copy-start.34 = (f32[768]{0:T(1024)}, f32[768]{0:T(1024)S(1)}, u32[]{:S(2)}) copy-start(f32[768]{0:T(1024)S(1)} %reshape.747) | copy-start | bytes 9220
  47.9 236.5 %copy-start.2 = (bf16[8,72,768]{2,1,0:T(8,128)(2,1)}, bf16[8,72,768]{2,1,0:T(8,128)(2,1)S(1)}, u32[]{:S(2)}) copy-start(bf16[8,72,768]{2,1,0:T(8,128)(2,1)S(1)} %all-to-all-done) | copy-start | bytes 2654212
  48.1 4.2 copy-start.36
  48.2 4.1 copy-start.49
  52.3 4.9 copy-start.75
  52.3 6.6 copy-start.33
  52.3 65.0 %all-to-all-start.1 = ((bf16[4,576,768]{2,1,0:T(8,128)(2,1)}), bf16[4,576,768]{2,1,0:T(8,128)(2,1)}, u32[]{:S(2)}, u32[]{:S(2)}) async-start(bf16[4,576,768]{2,1,0:T(8,128)(2,1)} %broadcast_in_dim.105), calls=%async_computation.1 | async-start | bytes 7077888 | tf_op jit(solution)/shard_map/all_to_all | solution.py:172
  97.1 7.9 %copy-start.61 = (bf16[95,64]{0,1:T(8,128)(2,1)S(1)}, bf16[95,64]{0,1:T(8,128)(2,1)}, u32[]{:S(2)}) copy-start(bf16[95,64]{0,1:T(8,128)(2,1)} %param.35) | copy-start | bytes 36484
  98.5 233.7 %copy-start.62 = (f32[576]{0:T(1024)}, f32[576]{0:T(1024)S(1)}, u32[]{:S(2)}) copy-start(f32[576]{0:T(1024)S(1)} %fusion.77) | copy-start | bytes 6916
  117.4 17.2 %all-to-all-start.2 = ((bf16[4,192,576]{2,1,0:T(8,128)(2,1)}), bf16[4,192,576]{2,1,0:T(8,128)(2,1)S(1)}, u32[]{:S(2)}, u32[]{:S(2)}) async-start(bf16[4,192,576]{2,1,0:T(8,128)(2,1)} %copy.274), calls=%async_computation.2 | async-start | bytes 1966080 | tf_op jit(solution)/shard_map/all_to_all | solution.py:172
  134.6 9.5 %copy-start.27 = (bf16[4,192,576]{2,1,0:T(8,128)(2,1)}, bf16[4,192,576]{2,1,0:T(8,128)(2,1)S(1)}, u32[]{:S(2)}) copy-start(bf16[4,192,576]{2,1,0:T(8,128)(2,1)S(1)} %all-to-all-done.2) | copy-start | bytes 2654212
  134.6 88.5 %all-to-all-start.5 = ((bf16[8,72,768]{2,1,0:T(8,128)(2,1)}), bf16[8,72,768]{2,1,0:T(8,128)(2,1)}, u32[]{:S(2)}, u32[]{:S(2)}) async-start(bf16[8,72,768]{2,1,0:T(8,128)(2,1)} %param.19), calls=%async_computation.5 | async-start | bytes 1769472 | tf_op jit(solution)/shard_map/all_to_all | solution.py:267
  176.4 5.3 copy-start.23
  223.1 20.6 %all-to-all-start.3 = ((bf16[8,4,72,1,192]{4,2,0,3,1:T(8,128)(2,1)}), bf16[8,4,72,1,192]{4,2,0,3,1:T(8,128)(2,1)}, u32[]{:S(2)}, u32[]{:S(2)}) async-start(bf16[8,4,72,1,192]{4,2,0,3,1:T(8,128)(2,1)} %copy.283), calls=%async_computation.3 | async-start | bytes 2359296 | tf_op jit(solution)/shard_map/all_to_all | solution.py:349
  246.9 37.4 %copy-start.31 = (bf16[576,768]{1,0:T(8,128)(2,1)}, bf16[576,768]{1,0:T(8,128)(2,1)S(1)}, u32[]{:S(2)}) copy-start(bf16[576,768]{1,0:T(8,128)(2,1)S(1)} %reshape.694) | copy-start | bytes 2654212
  285.4 7.0 copy-start.12
  287.7 4.7 slice-start.4
  292.5 22.7 %slice-start.6 = ((s8[4718592]{0:T(1024)(128)(4,1)}), s8[4194304]{0:T(1024)(128)(4,1)S(1)}, s32[]{:S(2)}) async-start(s8[4718592]{0:T(1024)(128)(4,1)} %bitcast.271), calls=%async_computation.27 | async-start | bytes 8388608
  295.5 19.7 %copy-start.13 = (f32[576,768]{1,0:T(8,128)S(1)}, f32[576,768]{1,0:T(8,128)}, u32[]{:S(2)}) copy-start(f32[576,768]{1,0:T(8,128)} %copy-done.12) | copy-start | bytes 5308420
  295.5 19.7 %slice-start.7 = ((s8[4718592]{0:T(1024)(128)(4,1)}), s8[524288]{0:T(1024)(128)(4,1)S(1)}, s32[]{:S(2)}) async-start(s8[4718592]{0:T(1024)(128)(4,1)} %bitcast.271), calls=%async_computation.28 | async-start | bytes 1048576
  334.3 17.1 %slice-start.2 = ((s8[4718592]{0:T(1024)(128)(4,1)}), s8[524288]{0:T(1024)(128)(4,1)S(1)}, s32[]{:S(2)}) async-start(s8[4718592]{0:T(1024)(128)(4,1)} %bitcast.265), calls=%async_computation.23 | async-start | bytes 1048576
  337.0 57.1 %all-to-all-start.14 = ((f32[32,1,192]{2,1,0:T(1,128)}), f32[32,1,192]{2,1,0:T(1,128)S(1)}, u32[]{:S(2)}, u32[]{:S(2)}) async-start(f32[32,1,192]{2,1,0:T(1,128)} %copy.321), calls=%async_computation.15 | async-start | bytes 65536 | tf_op jit(solution)/shard_map/all_to_all | solution.py:172
  342.6 7.7 %copy-start.30 = (bf16[576,768]{1,0:T(8,128)(2,1)S(1)}, bf16[576,768]{1,0:T(8,128)(2,1)}, u32[]{:S(2)}) copy-start(bf16[576,768]{1,0:T(8,128)(2,1)} %copy-done.29) | copy-start | bytes 2654212
  342.6 7.7 %copy-start.32 = (bf16[576,768]{1,0:T(8,128)(2,1)S(1)}, bf16[576,768]{1,0:T(8,128)(2,1)}, u32[]{:S(2)}) copy-start(bf16[576,768]{1,0:T(8,128)(2,1)} %copy-done.31) | copy-start | bytes 2654212
  342.6 8.8 %slice-start.3 = ((s8[4718592]{0:T(1024)(128)(4,1)}), s8[4194304]{0:T(1024)(128)(4,1)S(1)}, s32[]{:S(2)}) async-start(s8[4718592]{0:T(1024)(128)(4,1)} %bitcast.265), calls=%async_computation.24 | async-start | bytes 8388608
  394.1 19.3 %all-to-all-start.6 = ((bf16[8,1,72,4,192]{4,2,1,0,3:T(8,128)(2,1)}), bf16[8,1,72,4,192]{4,2,1,0,3:T(8,128)(2,1)S(1)}, u32[]{:S(2)}, u32[]{:S(2)}) async-start(bf16[8,1,72,4,192]{4,2,1,0,3:T(8,128)(2,1)} %copy.291), calls=%async_computation.6 | async-start | bytes 2359296 | tf_op jit(solution)/shard_map/all_to_all | solution.py:386
  397.7 318.2 %reduce-scatter.2.cloned.1.call-start = ((), (), s32[]{:S(2)}) async-start(), calls=%async_computation.19 | async-start | bytes 10948608 | tf_op jit(solution)/shard_map/reduce_scatter | solution.py:408
  413.5 6.6 copy-start.21
  414.1 96.3 %all-to-all-start.15 = ((f32[8,1,192]{2,1,0:T(1,128)}), f32[8,1,192]{2,1,0:T(1,128)S(1)}, u32[]{:S(2)}, u32[]{:S(2)}) async-start(f32[8,1,192]{2,1,0:T(1,128)} %broadcast_in_dim.123), calls=%async_computation.16 | async-start | bytes 16384 | tf_op jit(solution)/shard_map/all_to_all | solution.py:172
  506.1 9.4 %copy-start.65 = (f32[192]{0:T(256)S(1)}, f32[192]{0:T(256)}, u32[]{:S(2)}) copy-start(f32[192]{0:T(256)} %get-tuple-element.113) | copy-start | bytes 2308
  506.1 32.1 %copy-start.10 = (bf16[2304,3,3,64]{0,3,2,1:T(8,128)(2,1)S(1)}, bf16[2304,3,3,64]{0,3,2,1:T(8,128)(2,1)}, u32[]{:S(2)}) copy-start(bf16[2304,3,3,64]{0,3,2,1:T(8,128)(2,1)} %copy.302) | copy-start | bytes 7962628
  510.4 13.7 %copy-start.59 = (f32[8,1,192]{2,1,0:T(1,128)}, f32[8,1,192]{2,1,0:T(1,128)S(1)}, u32[]{:S(2)}) copy-start(f32[8,1,192]{2,1,0:T(1,128)S(1)} %all-to-all-done.15) | copy-start | bytes 18436
  510.4 13.1 %all-to-all-start.16 = ((f32[32,1,384]{2,1,0:T(1,128)}), f32[32,1,384]{2,1,0:T(1,128)S(1)}, u32[]{:S(2)}, u32[]{:S(2)}) async-start(f32[32,1,384]{2,1,0:T(1,128)} %bitcast.108), calls=%async_computation.17 | async-start | bytes 98304 | tf_op jit(solution)/shard_map/all_to_all | solution.py:172
  524.1 10.1 %all-to-all-start.13 = ((f32[8,1,384]{2,1,0:T(1,128)}), f32[8,1,384]{2,1,0:T(1,128)S(1)}, u32[]{:S(2)}, u32[]{:S(2)}) async-start(f32[8,1,384]{2,1,0:T(1,128)} %broadcast_in_dim.121), calls=%async_computation.13 | async-start | bytes 24576 | tf_op jit(solution)/shard_map/all_to_all | solution.py:172
  534.3 8.2 %copy-start.47 = (f32[8,1,384]{2,1,0:T(1,128)}, f32[8,1,384]{2,1,0:T(1,128)S(1)}, u32[]{:S(2)}) copy-start(f32[8,1,384]{2,1,0:T(1,128)S(1)} %all-to-all-done.13) | copy-start | bytes 36868
  534.9 10.7 %all-to-all-start.17 = ((f32[32,1,384]{2,1,0:T(1,128)}), f32[32,1,384]{2,1,0:T(1,128)}, u32[]{:S(2)}, u32[]{:S(2)}) async-start(f32[32,1,384]{2,1,0:T(1,128)} %broadcast_in_dim.124), calls=%async_computation.18 | async-start | bytes 98304 | tf_op jit(solution)/shard_map/all_to_all | solution.py:172
  545.6 18.2 %all-to-all-start.11 = ((bf16[4,192,576]{2,1,0:T(8,128)(2,1)}), bf16[4,192,576]{2,1,0:T(8,128)(2,1)}, u32[]{:S(2)}, u32[]{:S(2)}) async-start(bf16[4,192,576]{2,1,0:T(8,128)(2,1)} %bitcast.280), calls=%async_computation.11 | async-start | bytes 1966080 | tf_op jit(solution)/shard_map/all_to_all | solution.py:172
  563.8 3.9 copy-start.64
  563.8 4.0 copy-start.63
  563.8 45.0 %all-to-all-start.7 = ((bf16[4,576,768]{2,1,0:T(8,128)(2,1)}), bf16[4,576,768]{2,1,0:T(8,128)(2,1)S(1)}, u32[]{:S(2)}, u32[]{:S(2)}) async-start(bf16[4,576,768]{2,1,0:T(8,128)(2,1)} %bitcast.64), calls=%async_computation.7 | async-start | bytes 7077888 | tf_op jit(solution)/shard_map/all_to_all | solution.py:172
  610.6 26.5 %all-to-all-start.4 = ((bf16[8,72,768]{2,1,0:T(8,128)(2,1)}), bf16[8,72,768]{2,1,0:T(8,128)(2,1)}, u32[]{:S(2)}, u32[]{:S(2)}) async-start(bf16[8,72,768]{2,1,0:T(8,128)(2,1)} %bitcast.289), calls=%async_computation.4 | async-start | bytes 1769472 | tf_op jit(solution)/shard_map/all_to_all | solution.py:172
  614.8 3.9 copy-start.3
  614.9 3.9 copy-start.35
  614.9 3.9 copy-start.37
  637.2 9.9 %all-to-all-start.9 = ((f32[32,1,48]{2,1,0:T(1,128)}), f32[32,1,48]{2,1,0:T(1,128)S(1)}, u32[]{:S(2)}, u32[]{:S(2)}) async-start(f32[32,1,48]{2,1,0:T(1,128)} %bitcast.72), calls=%async_computation.9 | async-start | bytes 32768 | tf_op jit(solution)/shard_map/all_to_all | solution.py:172
  644.7 6.8 copy-start.58
  644.7 39.7 %copy-start.50 = (f32[576]{0:T(1024)S(1)}, f32[576]{0:T(1024)}, u32[]{:S(2)}) copy-start(f32[576]{0:T(1024)} %copy-done.49) | copy-start | bytes 6916
  644.7 39.7 %copy-start.52 = (f32[576]{0:T(1024)S(1)}, f32[576]{0:T(1024)}, u32[]{:S(2)}) copy-start(f32[576]{0:T(1024)} %copy-done.51) | copy-start | bytes 6916
  644.7 39.7 %copy-start.54 = (f32[576]{0:T(1024)S(1)}, f32[576]{0:T(1024)}, u32[]{:S(2)}) copy-start(f32[576]{0:T(1024)} %copy-done.53) | copy-start | bytes 6916
  647.1 33.1 %all-to-all-start.12 = ((bf16[8,192,288]{1,2,0:T(8,128)(2,1)}), bf16[8,192,288]{1,2,0:T(8,128)(2,1)}, u32[]{:S(2)}, u32[]{:S(2)}) async-start(bf16[8,192,288]{1,2,0:T(8,128)(2,1)} %bitcast.274), calls=%async_computation.12 | async-start | bytes 2359296 | tf_op jit(solution)/shard_map/all_to_all | solution.py:172
  680.8 10.0 %all-to-all-start.10 = ((f32[8,1,48]{2,1,0:T(1,128)}), f32[8,1,48]{2,1,0:T(1,128)S(1)}, u32[]{:S(2)}, u32[]{:S(2)}) async-start(f32[8,1,48]{2,1,0:T(1,128)} %broadcast_in_dim.120), calls=%async_computation.10 | async-start | bytes 8192 | tf_op jit(solution)/shard_map/all_to_all | solution.py:172
  687.5 7.0 copy-start.60
  687.5 10.4 %copy-start.48 = (f32[8,1,384]{2,1,0:T(1,128)S(1)}, f32[8,1,384]{2,1,0:T(1,128)}, u32[]{:S(2)}) copy-start(f32[8,1,384]{2,1,0:T(1,128)} %copy-done.47) | copy-start | bytes 36868
  690.9 25.0 %all-to-all-start.8 = ((bf16[8,72,768]{2,1,0:T(8,128)(2,1)}), bf16[8,72,768]{2,1,0:T(8,128)(2,1)S(1)}, u32[]{:S(2)}, u32[]{:S(2)}) async-start(bf16[8,72,768]{2,1,0:T(8,128)(2,1)} %bitcast.66), calls=%async_computation.8 | async-start | bytes 1769472 | tf_op jit(solution)/shard_map/all_to_all | solution.py:172
  (40 other events, 74.5 us)
Sparse Core Ops, SparseCore 0:
  11.2 120.7 all-gather.4
  411.9 144.9 reduce-scatter.1

commit v2 on v1

--- a/solution.py
+++ b/solution.py
@@ -70,7 +70,7 @@
 
 
 def backward_kernel(
-    q_ref, g_ref, lse_ref, delta_ref, k_ref, v_ref, kt_ref, dq_ref, line_ref, dkv_ref
+    q_ref, g_ref, lse_ref, delta_ref, k_ref, v_ref, kt_ref, dq_ref, line_ref, out_ref, dkv_ref
 ):
     heads, tokens, depth = k_ref.shape
     dim = 64
@@ -101,6 +101,12 @@
         dq_ref[h] = total[:dim].T
         line_ref[h] = total[dim:].T.astype(jnp.bfloat16)
 
+    @pl.when(pl.program_id(0) == pl.num_programs(0) - 1)
+    def _():
+        keys = [dkv_ref[h, :, dim:] for h in range(heads)]
+        values = [dkv_ref[h, :, :dim] for h in range(heads)]
+        out_ref[...] = jnp.concatenate(keys + values, axis=1).astype(jnp.bfloat16)
+
 
 def attend_backward(q_aug, grads, lse, delta, k_aug, values, k_turn):
     heads, tokens, depth = q_aug.shape
@@ -121,12 +127,13 @@
         out_specs=[
             pl.BlockSpec((heads, TBLK, dim), lambda t: (0, t, 0)),
             pl.BlockSpec((heads, TBLK, lines), lambda t: (0, t, 0)),
-            pl.BlockSpec((heads, tokens, 2 * dim), lambda t: (0, 0, 0)),
-        ],
+            pl.BlockSpec((tokens, 2 * heads * dim), lambda t: (0, 0)),
+        ],
+        scratch_shapes=[pltpu.VMEM((heads, tokens, 2 * dim), jnp.float32)],
         out_shape=[
             jax.ShapeDtypeStruct((heads, tokens, dim), jnp.float32),
             jax.ShapeDtypeStruct((heads, tokens, lines), jnp.bfloat16),
-            jax.ShapeDtypeStruct((heads, tokens, 2 * dim), jnp.float32),
+            jax.ShapeDtypeStruct((tokens, 2 * heads * dim), jnp.bfloat16),
         ],
         name="attend_backward",
         compiler_params=pltpu.CompilerParams(dimension_semantics=("arbitrary",)),
@@ -175,6 +182,29 @@
 def spread(values, axis):
     count = lax.axis_size(axis)
     return exchange(jnp.broadcast_to(values, (count,) + values.shape), axis)
+
+
+def swap(values, step):
+    pairs = [(i, i ^ step) for i in range(lax.axis_size("ha"))]
+    return lax.ppermute(values, "ha", pairs)
+
+
+def gather_heads(values):
+    me = lax.axis_index("ha")
+    far = swap(values, 2)
+    near = swap(values, 1)
+    corner = swap(far, 1)
+    blocks = jnp.stack([values, near, far, corner])
+    return [lax.dynamic_index_in_dim(blocks, jnp.bitwise_xor(me, i), 0, False) for i in range(4)]
+
+
+def scatter_heads(parts):
+    me = lax.axis_index("ha")
+    other = [lax.dynamic_index_in_dim(parts, jnp.bitwise_xor(me, i), 0, False) for i in range(4)]
+    arrived = swap(jnp.stack([other[3], other[1]]), 1).astype(jnp.float32)
+    far = (other[2].astype(jnp.float32) + arrived[0]).astype(jnp.bfloat16)
+    near = other[0].astype(jnp.float32) + arrived[1]
+    return near + swap(far, 2).astype(jnp.float32)
 
 
 def pack_up(piece):
@@ -228,11 +258,6 @@
     bf16 = jnp.bfloat16
 
     triple_rows = lax.all_gather(qkv_weight, "ga", axis=1, tiled=True)
-    triple_cut = triple_rows.reshape(group_width, 3, head_groups, group_width).transpose(2, 0, 1, 3)
-    triple_own = exchange(
-        triple_cut.reshape(head_groups, group_width, 3 * group_width), "ha"
-    ).reshape(model_width, 3 * group_width)
-
     up_rows, up_cols = fc1_weight.shape
     out_cols = fc2_weight.shape[1]
     packed = jnp.concatenate(
@@ -264,7 +289,12 @@
     up_shift = vector_at(6, 4 * wide)
 
     tokens_in = lax.all_to_all(patches, "ga", split_axis=0, concat_axis=1, tiled=True)[0]
+    tokens_in, triple_rows = lax.optimization_barrier((tokens_in, triple_rows))
     cot_in = lax.all_to_all(cotangent, "ga", split_axis=0, concat_axis=1, tiled=True)[0]
+    triple_cut = triple_rows.reshape(group_width, 3, head_groups, group_width).transpose(2, 0, 1, 3)
+    triple_own = exchange(
+        triple_cut.reshape(head_groups, group_width, 3 * group_width), "ha"
+    ).reshape(model_width, 3 * group_width)
     tokens32 = tokens_in.astype(f32)
     cot32 = cot_in.astype(f32)
     slot_index = jnp.arange(local_tokens, dtype=jnp.int32)
@@ -291,13 +321,17 @@
         bf16
     )
 
-    normed = layer_norm(tokens32, first_gain.astype(f32), first_shift.astype(f32)).astype(bf16)
-    normed_all = (
-        spread(normed, "ha")
-        .reshape(head_groups, group_count, block_len, model_width)
-        .transpose(1, 0, 2, 3)
+    tokens_all = (
+        jnp.stack(
+            [block.reshape(group_count, block_len, model_width) for block in gather_heads(tokens_in)],
+            axis=1,
+        )
         .reshape(cap_tokens, model_width)
-    )
+        .astype(f32)
+    )
+    gain32 = first_gain.astype(f32)
+    shift32 = first_shift.astype(f32)
+    normed_all = layer_norm(tokens_all, gain32, shift32).astype(bf16)
     bias_own = jnp.concatenate([query_bias, jnp.zeros_like(query_bias), value_bias]).astype(f32)
     mixed = (jnp.dot(normed_all, triple_own, preferred_element_type=f32) + bias_own).astype(bf16)
     by_head = mixed.reshape(cap_tokens, 3, group_heads, HD).transpose(1, 2, 0, 3)
@@ -443,7 +477,8 @@
         .transpose(1, 0)
         .reshape(group_heads, 1, cap_tokens)
     )
-    query_part, line_sums, dkv = attend_backward(
+    delta, out_back = lax.optimization_barrier((delta, out_back))
+    query_part, line_sums, key_value_grad = attend_backward(
         q_aug, grad_heads.transpose(1, 0, 2), log_sums, delta, k_aug, value_all, k_turn
     )
     lines = line_sums.reshape(group_heads, SMAX, SMAX, 2 * SMAX)
@@ -456,22 +491,21 @@
     ).reshape(group_heads, cap_tokens, HD)
     h_table_grad = jnp.einsum("hrwj,hrwd->rjd", height_grad, q_grid, preferred_element_type=f32)
     w_table_grad = jnp.einsum("hrwj,hrwd->wjd", width_grad, q_grid, preferred_element_type=f32)
-    mixed_grad = (
-        jnp.stack([query_grad, dkv[..., HD:], dkv[..., :HD]])
-        .astype(bf16)
-        .transpose(2, 0, 1, 3)
-        .reshape(cap_tokens, 3 * group_width)
-    )
-    norm1_part = contract_cols(mixed_grad, triple_own).astype(bf16)
-    norm1_in = jnp.sum(
-        exchange(
-            norm1_part.reshape(group_count, head_groups, block_len, model_width)
-            .transpose(1, 0, 2, 3)
-            .reshape(head_groups, local_tokens, model_width),
-            "ha",
-        ).astype(f32),
-        axis=0,
-    )
+    mixed_grad = jnp.concatenate(
+        [
+            query_grad.astype(bf16).transpose(1, 0, 2).reshape(cap_tokens, group_width),
+            key_value_grad,
+        ],
+        axis=1,
+    )
+    norm1_wide = contract_cols(mixed_grad, triple_own)
+    norm1_part = (
+        norm1_wide.astype(bf16)
+        .reshape(group_count, head_groups, block_len, model_width)
+        .transpose(1, 0, 2, 3)
+        .reshape(head_groups, local_tokens, model_width)
+    )
+    norm1_in = scatter_heads(norm1_part)
     triple_part = contract_rows(normed_all, mixed_grad).astype(bf16)
     triple_rows_grad = (
         exchange(triple_part.reshape(head_groups, group_width, 3 * group_width), "ha")
@@ -481,38 +515,56 @@
         .transpose(1, 0, 2)
     )
     triple_grad = jnp.sum(exchange(triple_rows_grad, "ga").astype(f32), axis=0)
+
+    center = tokens_all - jnp.mean(tokens_all, axis=-1, keepdims=True)
+    unit = center * lax.rsqrt(jnp.mean(center * center, axis=-1, keepdims=True) + 1e-06)
+    first_gain_grad = jnp.sum(norm1_wide * unit, axis=0)
+    first_shift_grad = jnp.sum(norm1_wide, axis=0)
     mixed_float = mixed_grad.astype(f32)
-    bias_part = jnp.concatenate(
-        [
-            jnp.sum(mixed_float[:, :group_width], axis=0),
-            jnp.sum(mixed_float[:, 2 * group_width :], axis=0),
-        ]
-    )
-    bias_sum = jnp.sum(spread(bias_part[None], "ga"), axis=0)[0]
+    zero_wide = jnp.zeros((model_width,), f32)
+
+    def own_slot(vector):
+        return lax.dynamic_update_slice(zero_wide, vector, (head_index * group_width,))
+
+    query_bias_grad = own_slot(jnp.sum(mixed_float[:, :group_width], axis=0))
+    value_bias_grad = own_slot(jnp.sum(mixed_float[:, 2 * group_width :], axis=0))
     height_rel = jnp.einsum("qkj,qkd->jd", matrix, h_table_grad, precision=exact_mode)
     width_rel = jnp.einsum("qkj,qkd->jd", matrix, w_table_grad, precision=exact_mode)
     rel_flat = jnp.concatenate([height_rel, width_rel]).reshape(-1)
     rel_size = rel_flat.shape[0]
-    chunk = -(-rel_size // (128 * device_count)) * 128
+    chunk = -(-rel_size // device_count)
     rel_flat = jnp.pad(rel_flat, (0, chunk * device_count - rel_size))
-    rel_part = jnp.sum(exchange(rel_flat.reshape(device_count, 1, chunk), BOTH), axis=0)
-    rel_sum = spread(rel_part, BOTH).reshape(-1)[:rel_size].reshape(2, 2 * SMAX - 1, HD)
-
-    norm1_value, norm1_pull = jax.vjp(
-        layer_norm, tokens32, first_gain.astype(f32), first_shift.astype(f32)
-    )
-    in_grad, first_gain_grad, first_shift_grad = norm1_pull(norm1_in)
-    input_grad = (mid_total + in_grad).astype(bf16)
+    piece = model_width // device_count
+    last_vectors = [first_gain_grad, first_shift_grad, query_bias_grad, value_bias_grad]
+    stacked = jnp.concatenate(
+        [
+            vector.reshape(head_groups, group_count, piece)
+            .transpose(1, 0, 2)
+            .reshape(device_count, piece)
+            for vector in last_vectors
+        ]
+        + [rel_flat.reshape(device_count, chunk)],
+        axis=1,
+    )
+    last_part = jnp.sum(exchange(stacked[:, None], BOTH), axis=0)
+    last_all = spread(last_part, BOTH)[:, 0].reshape(group_count, head_groups, -1)
+    last_here = lax.dynamic_index_in_dim(last_all, head_index, 1, False)
+    late = [last_here[:, i * piece : (i + 1) * piece].reshape(-1) for i in range(4)]
+    rel_sum = (
+        last_all[:, :, 4 * piece :].reshape(-1)[:rel_size].reshape(2, 2 * SMAX - 1, HD)
+    )
+
+    norm1_value, norm1_pull = jax.vjp(lambda tokens: layer_norm(tokens, gain32, shift32), tokens32)
+    input_grad = (mid_total + norm1_pull(norm1_in)[0]).astype(bf16)
     in_back = exchange(input_grad.reshape(group_count, block_len, model_width), "ga")
-    late = reduce_vectors([first_gain_grad, first_shift_grad])
     return (
         out_back,
         in_back,
         late[0],
         late[1],
         triple_grad,
-        bias_sum[:group_width],
-        bias_sum[group_width:],
+        late[2],
+        late[3],
         proj_own,
         early[0],
         early[1],

time: 740 us -> 734 us (level)
  waiting for transfers between devices: 169 us -> 91.4 us
  blocking collectives: 41.8 us -> 87 us
  local copies, waits for them, and re-layouts: 187 us -> 204 us
  starting transfers between devices: 79.1 us -> 65.3 us
  matrix products: 82.4 us -> 94.7 us
  other arithmetic: 68.5 us -> 79.4 us
    all_to_all x14 -> x9, waiting for transfers between devices: 138 us -> 71.9 us  [exchange(): return lax.all_to_all(values, axis, split_axis=0, concat_axis=0, tiled=True)]
    all_gather x1, blocking collectives: 5.22 us -> 32.2 us  [local(): vectors_all = lax.all_gather(vectors, 'ha', axis=0, tiled=False)]
    all_to_all x1, waiting for transfers between devices: 23.2 us -> 0.01 us  [local(): lax.all_to_all(patches, 'ga', split_axis=0, concat_axis=1, tiled=True)[0]]
    all_gather x1, blocking collectives: 36.6 us -> 54.8 us  [local(): triple_rows = lax.all_gather(qkv_weight, 'ga', axis=1, tiled=True)]
    all_to_all x14 -> x9, starting transfers between devices: 58.3 us -> 41.6 us  [exchange(): return lax.all_to_all(values, axis, split_axis=0, concat_axis=0, tiled=True)]
    transpose x2 -> x4, local copies, waits for them, and re-layouts: 11 us -> 0.02 us  [local(): stacked = jnp.concatenate([vector.reshape(head_groups, group_count, piece...]
    convert_element_type x2 -> x4, local copies, waits for them, and re-layouts: 0.15 us -> 9.25 us  [the longest x2 9.09 us: local(): query_grad.astype(bf16).transpose(1, 0, 2).reshape(cap_tokens, group_width)]
    unnamed x183 -> x182, local copies, waits for them, and re-layouts: 28.5 us -> 27.8 us
  transfers between devices with their start and end apart: 20 -> 20, of which waited for: 15 -> 9; matrix products, arithmetic and copies ran while one was open for 31% -> 27% of each run, Pallas kernels for 12% -> 12%
where the time goes in v2:
time: 734 us; the launch traced here: 724 us
  local copies, waits for them, and re-layouts  204 us (28%)
  matrix products  94.7 us (13%)
  waiting for transfers between devices  91.4 us (12%)
  blocking collectives  87 us (12%)
  Pallas kernels  85.8 us (12%)
  other arithmetic  79.4 us (11%)
  starting transfers between devices  65.3 us (9%)
  between operations  16.6 us (2%)
    all_to_all x9, waiting for transfers between devices, exchange(): return lax.all_to_all(values, axis, split_axis=0, concat_axis=0, tiled=True)  71.9 us
    all_gather x1, blocking collectives, local(): triple_rows = lax.all_gather(qkv_weight, 'ga', axis=1, tiled=True)  54.8 us
    pallas_call x1, Pallas kernels, attend_backward(): pl.pallas_call(backward_kernel, grid=(tokens // TBLK,), in_specs=[pl.Bloc...  48.1 us
    all_to_all x9, starting transfers between devices, exchange(): return lax.all_to_all(values, axis, split_axis=0, concat_axis=0, tiled=True)  41.6 us
    pallas_call x1, Pallas kernels, attend_forward(): pl.pallas_call(forward_kernel, grid=(tokens // TBLK,), in_specs=[pl.Block...  37.7 us
    all_gather x1, blocking collectives, local(): vectors_all = lax.all_gather(vectors, 'ha', axis=0, tiled=False)  32.2 us
    unnamed x182, local copies, waits for them, and re-layouts  27.8 us
    dot_general x4, matrix products, contract_cols(): lax.dot_general(left, right, (((1,), (1,)), ((), ())), preferred_element_...  22.7 us
  transfers between devices with their start and end apart: 20, of which 9 were waited for; matrix products, arithmetic and copies ran while one was open for 27% of the time, Pallas kernels for 12%

profile of v2, /device:TPU:0, one launch (start us, length us, event | category | flops | bytes accessed | tf_op | source)
XLA Modules:
  0.0 724.0 jit_solution(16022870675263002662)
XLA Ops:
  11.2 7.3 %all-to-all-start.1 = ((bf16[8,72,768]{2,1,0:T(8,128)(2,1)}), bf16[8,72,768]{2,1,0:T(8,128)(2,1)S(1)}, u32[]{:S(2)}, u32[]{:S(2)}) async-start(bf16[8,72,768]{2,1,0:T(8,128)(2,1)} %param.18), calls=%async_computation.1 | async-start | bytes 1769472 | tf_op jit(solution)/shard_map/all_to_all | solution.py:291
  21.6 54.8 %all_gather.15 = bf16[192,2304]{0,1:T(8,128)(2,1)S(1)} all-gather(bf16[192,288]{0,1:T(8,128)(2,1)S(1)} %copy.149), channel_id=1, replica_groups=mesh['ga'=8,'ha'=4] {'ga'}, dimensions={1}, use_global_device_ids=true | all-gather | bytes 995328 | tf_op jit(solution)/shard_map/all_gather | solution.py:260
  78.1 32.2 %all-gather.2 = bf16[4,1,1920]{2,1,0:T(2,128)(2,1)S(1)} all-gather(bf16[1,1,1920]{2,1,0:T(2,128)(2,1)S(1)} %reshape.779), channel_id=2, replica_groups=mesh['ga'=8,'ha'=4] {'ha'}, dimensions={0}, use_global_device_ids=true | all-gather | bytes 19200 | tf_op jit(solution)/shard_map/all_gather | solution.py:277
  122.2 3.9 all-to-all-start.2
  131.4 3.2 add_convert_fusion.2
  134.6 5.7 all-to-all-done.2
  140.3 4.4 all-to-all-start
  144.8 4.3 add_convert_fusion.3
  151.2 4.2 reshape_squeeze.6
  155.4 3.7 copy.155
  159.1 3.1 copy.153
  172.4 4.1 fusion.7
  179.7 5.8 copy.159.k_ref
  185.5 5.2 pad_maximum_fusion.4.q_ref
  191.9 37.7 %attend_forward.1 = (bf16[2304,192]{1,0:T(8,128)(2,1)}, f32[3,1,2304]{2,1,0:T(1,128)}) custom-call(bf16[3,2304,256]{2,1,0:T(8,128)(2,1)} %pad_maximum_fusion.4.q_ref, bf16[3,2304,256]{2,1,0:T(8,128)(2,1)} %copy.159.k_ref, bf16[3,80,2304]{2,1,0:T(8,128)(2,1)} %maximum_maximum_fusion.v_ref), custom_call_target="tpu_custom_call" | custom-call | tf_op jit(solution)/shard_map/attend_forward/pallas_call | solution.py:51
  232.0 3.5 all-to-all-start.3
  237.0 3.0 fusion.20
  240.0 11.4 %all-to-all-done.3 = bf16[8,4,72,1,192]{4,2,0,3,1:T(8,128)(2,1)S(1)} async-done(((bf16[8,4,72,1,192]{4,2,0,3,1:T(8,128)(2,1)}), bf16[8,4,72,1,192]{4,2,0,3,1:T(8,128)(2,1)S(1)}, u32[]{:S(2)}, u32[]{:S(2)}) %all-to-all-start.3) | async-done | bytes 884768 | tf_op jit(solution)/shard_map/all_to_all | solution.py:383
  256.6 8.1 %fusion.100 = (bf16[8,4,96,768]{3,2,1,0:T(8,128)(2,1)}, bf16[8,4,96,768]{3,2,1,0:T(8,128)(2,1)}) fusion(bf16[8,4,216,768]{3,2,1,0:T(8,128)(2,1)} %bitcast.296), kind=kLoop, calls=%fused_computation.229 | loop fusion | bytes 18874368 | tf_op jit(solution)/shard_map/slice | solution.py:367
  264.8 3.0 reshape.711
  269.6 3.8 reshape.712
  276.0 10.5 %reshape.713 = bf16[8,4,96,2,384]{4,3,2,1,0:T(2,128)(2,1)} reshape(bf16[8,4,96,768]{3,2,1,0:T(8,128)(2,1)} %get-tuple-element.104) | data formatting | bytes 9437184 | tf_op jit(solution)/shard_map/reshape | solution.py:221
  286.6 5.3 copy.216
  291.9 3.3 copy.225
  295.2 3.6 copy.221
  302.0 3.0 fusion.95
  305.1 21.1 %convert_reduce_fusion = (f32[3072]{0:T(1024)}, bf16[576,3072]{1,0:T(8,128)(2,1)S(1)}, f32[576,3072]{1,0:T(8,128)}) fusion(f32[576,3072]{1,0:T(8,128)S(1)} %fusion.95, f32[3072]{0:T(1024)S(1)} %reshape.769, bf16[576,768]{1,0:T(8,128)(2,1)S(1)} %bitcast.322, bf16[768,3072]{1,0:T(8,128)(2,1)S(1)} %bitcast.303), kind=kOutput, calls=%fused_computation.5 | convolution fusion | flops 2850616320 | bytes 23322624 | tf_op jit(solution)/shard_map/dot_general | solution.py:405
  326.1 3.8 multiply_reduce_fusion.2
  330.0 6.1 convolution_convert_fusion.1
  336.8 7.2 multiply_convert_fusion
  348.5 4.4 reshape.745
  355.8 4.1 reshape.746
  362.7 7.6 %convolution_convert_fusion = bf16[768,3072]{1,0:T(8,128)(2,1)} fusion(bf16[576,768]{1,0:T(8,128)(2,1)S(1)} %get-tuple-element.125, bf16[576,3072]{1,0:T(8,128)(2,1)} %multiply_convert_fusion), kind=kOutput, calls=%fused_computation.29 | convolution fusion | flops 2720268288 | bytes 9142272 | tf_op jit(solution)/shard_map/dot_general | solution.py:167
  370.3 9.8 %reshape.744 = bf16[8,96,4,768]{3,2,1,0:T(4,128)(2,1)} reshape(bf16[768,3072]{1,0:T(8,128)(2,1)} %convolution_convert_fusion) | data formatting | bytes 9437184 | tf_op jit(solution)/shard_map/reshape | solution.py:433
  380.0 5.7 copy.227
  385.7 9.3 %copy.196 = bf16[8,4,96,2,384]{4,3,1,2,0:T(2,128)(2,1)} copy(bf16[8,4,96,2,384]{4,0,2,3,1:T(8,128)(2,1)} %bitcast.266) | data formatting | bytes 9437184 | tf_op jit(solution)/shard_map/transpose | solution.py:215
  395.0 12.0 %reshape.743 = bf16[8,4,96,768]{3,1,2,0:T(4,128)(2,1)} reshape(bf16[8,4,96,2,384]{4,3,1,2,0:T(2,128)(2,1)} %copy.196) | data formatting | bytes 9437184 | tf_op jit(solution)/shard_map/reshape | solution.py:215
  407.1 9.6 %pad_maximum_fusion = bf16[8,4,216,768]{3,1,2,0:T(4,128)(2,1)S(1)} fusion(bf16[8,4,24,768]{3,1,2,0:T(4,128)(2,1)} %copy.198, bf16[8,4,96,768]{3,1,2,0:T(4,128)(2,1)} %bitcast.269, bf16[8,4,96,768]{3,1,2,0:T(4,128)(2,1)} %reshape.743), kind=kLoop, calls=%fused_computation | loop fusion | flops 10616832 | bytes 21233664 | tf_op jit(solution)/shard_map/concatenate | solution.py:428
  416.6 5.0 copy.199
  424.3 5.2 all-to-all-start.11
  436.7 4.3 all-to-all-start.4
  441.0 7.7 %add_convert_fusion.5 = bf16[576,768]{1,0:T(8,128)(2,1)} fusion(f32[576,768]{1,0:T(8,128)S(1)} %get-tuple-element.147, bf16[576,3072]{1,0:T(8,128)(2,1)} %multiply_convert_fusion, bf16[768,3072]{1,0:T(8,128)(2,1)} %bitcast.304, f32[768]{0:T(1024)S(1)} %copy-done.70, f32[576]{0:T(1024)S(1)} %copy-done.59), kind=kOutput, calls=%fused_computation.76 | convolution fusion | flops 2719678464 | bytes 10917120 | tf_op jit(solution)/shard_map/dot_general | solution.py:173
  448.7 8.2 %all-to-all-done.4 = bf16[8,1,72,4,192]{4,2,1,0,3:T(8,128)(2,1)} async-done(((bf16[8,1,72,4,192]{4,2,1,0,3:T(8,128)(2,1)}), bf16[8,1,72,4,192]{4,2,1,0,3:T(8,128)(2,1)}, u32[]{:S(2)}, u32[]{:S(2)}) %all-to-all-start.4) | async-done | bytes 884768 | tf_op jit(solution)/shard_map/all_to_all | solution.py:420
  456.9 5.6 all-to-all-start.5
  471.3 4.1 copy.169
  475.4 4.4 reshape_reshape.4
  482.4 16.2 %all-to-all-done.5 = bf16[8,72,768]{2,1,0:T(8,128)(2,1)S(1)} async-done(((bf16[8,72,768]{2,1,0:T(8,128)(2,1)}), bf16[8,72,768]{2,1,0:T(8,128)(2,1)S(1)}, u32[]{:S(2)}, u32[]{:S(2)}) %all-to-all-start.5) | async-done | bytes 884768 | tf_op jit(solution)/shard_map/all_to_all | solution.py:179
  499.2 4.1 all-to-all-start.12
  503.4 48.1 %attend_backward.1 = (f32[3,2304,64]{2,1,0:T(8,128)}, bf16[3,2304,96]{2,1,0:T(8,128)(2,1)}, bf16[2304,384]{1,0:T(8,128)(2,1)}) custom-call(bf16[3,2304,256]{2,1,0:T(8,128)(2,1)} %pad_maximum_fusion.4.q_ref, bf16[3,2304,64]{2,1,0:T(8,128)(2,1)} %bitcast.299, f32[3,1,2304]{2,1,0:T(1,128)} %get-tuple-element.30.lse_ref, f32[3,1,2304]{2,1,0:T(1,128)} %reshape.718.delta_ref, ...), custom_call_target="tpu_custom_call" | custom-call | tf_op jit(solution)/shard_map/attend_backward/pallas_call | solution.py:115
  560.7 4.5 copy.178
  565.2 4.6 convert_element_type.343
  572.2 8.9 %fusion.96 = (f32[768]{0:T(1024)}, f32[768]{0:T(1024)}, bf16[2304,768]{1,0:T(8,128)(2,1)S(1)}, bf16[2304,768]{1,0:T(8,128)(2,1)}) fusion(f32[2304]{0:T(1024)} %rsqrt.37, f32[2304]{0:T(1024)} %div.139, bf16[8,1,72,768]{3,2,1,0:T(8,128)(2,1)} %bitcast.286, bf16[8,1,72,768]{3,2,1,0:T(8,128)(2,1)} %bitcast.290, bf16[8,1,72,768]{3,2,1,0:T(8,128)(2,1)} %bitcast.294, ...), kind=kOutput, calls=%fused_computation.226 | convolution fusion | flops 2066741760 | bytes 14186496 | tf_op jit(solution)/shard_map/dot_general | solution.py:173
  586.1 3.4 fusion.37
  589.6 3.4 fusion.34
  597.0 5.2 all-to-all-start.7
  602.2 5.8 convolution_convert_fusion.4
  612.1 4.3 all-to-all-start.9
  621.5 9.2 %all-to-all-done.9 = bf16[4,192,576]{2,1,0:T(8,128)(2,1)} async-done(((bf16[4,192,576]{2,1,0:T(8,128)(2,1)}), bf16[4,192,576]{2,1,0:T(8,128)(2,1)}, u32[]{:S(2)}, u32[]{:S(2)}) %all-to-all-start.9) | async-done | bytes 884768 | tf_op jit(solution)/shard_map/all_to_all | solution.py:179
  631.4 5.0 all-to-all-start.8
  642.5 8.5 %all-to-all-done.8 = f32[32,1,476]{2,1,0:T(1,128)} async-done(((f32[32,1,476]{2,1,0:T(1,128)}), f32[32,1,476]{2,1,0:T(1,128)}, u32[]{:S(2)}, u32[]{:S(2)}) %all-to-all-start.8) | async-done | bytes 60960 | tf_op jit(solution)/shard_map/all_to_all | solution.py:179
  650.9 4.5 all-to-all-start.10
  663.2 21.3 %all-to-all-done.10 = bf16[8,192,288]{1,2,0:T(8,128)(2,1)} async-done(((bf16[8,192,288]{1,2,0:T(8,128)(2,1)}), bf16[8,192,288]{1,2,0:T(8,128)(2,1)}, u32[]{:S(2)}, u32[]{:S(2)}) %all-to-all-start.10) | async-done | bytes 884768 | tf_op jit(solution)/shard_map/all_to_all | solution.py:179
  684.4 3.8 all-to-all-start.6
  700.1 10.5 %all-to-all-done.6 = bf16[8,72,768]{2,1,0:T(8,128)(2,1)S(1)} async-done(((bf16[8,72,768]{2,1,0:T(8,128)(2,1)}), bf16[8,72,768]{2,1,0:T(8,128)(2,1)S(1)}, u32[]{:S(2)}, u32[]{:S(2)}) %all-to-all-start.6) | async-done | bytes 884768 | tf_op jit(solution)/shard_map/all_to_all | solution.py:179
  (360 shorter events, 152.5 us)
Async XLA Ops:
  7.2 106.0 %copy-start = (bf16[95,64]{0,1:T(8,128)(2,1)S(1)}, bf16[95,64]{0,1:T(8,128)(2,1)}, u32[]{:S(2)}) copy-start(bf16[95,64]{0,1:T(8,128)(2,1)} %param.35) | copy-start | bytes 36484
  7.2 11.3 %copy-start.80 = (s32[8]{0:T(128)S(1)}, s32[8]{0:T(128)}, u32[]{:S(2)}) copy-start(s32[8]{0:T(128)} %param.20) | copy-start | bytes 100
  7.2 12.5 %copy-start.40 = (bf16[192,288]{1,0:T(8,128)(2,1)S(1)}, bf16[192,288]{1,0:T(8,128)(2,1)}, u32[]{:S(2)}) copy-start(bf16[192,288]{1,0:T(8,128)(2,1)} %param.23) | copy-start | bytes 331780
  7.2 13.3 %copy-start.78 = (bf16[192]{0:T(256)(128)(2,1)S(1)}, bf16[192]{0:T(256)(128)(2,1)}, u32[]{:S(2)}) copy-start(bf16[192]{0:T(256)(128)(2,1)} %param.25) | copy-start | bytes 1156
  7.2 13.3 %copy-start.79 = (bf16[192]{0:T(256)(128)(2,1)S(1)}, bf16[192]{0:T(256)(128)(2,1)}, u32[]{:S(2)}) copy-start(bf16[192]{0:T(256)(128)(2,1)} %param.24) | copy-start | bytes 1156
  7.3 70.7 %copy-start.72 = (bf16[192]{0:T(256)(128)(2,1)S(1)}, bf16[192]{0:T(256)(128)(2,1)}, u32[]{:S(2)}) copy-start(bf16[192]{0:T(256)(128)(2,1)} %param.21) | copy-start | bytes 1156
  7.3 70.7 %copy-start.73 = (bf16[192]{0:T(256)(128)(2,1)S(1)}, bf16[192]{0:T(256)(128)(2,1)}, u32[]{:S(2)}) copy-start(bf16[192]{0:T(256)(128)(2,1)} %param.22) | copy-start | bytes 1156
  7.3 70.7 %copy-start.74 = (bf16[192]{0:T(256)(128)(2,1)S(1)}, bf16[192]{0:T(256)(128)(2,1)}, u32[]{:S(2)}) copy-start(bf16[192]{0:T(256)(128)(2,1)} %param.27) | copy-start | bytes 1156
  7.3 70.6 %copy-start.75 = (bf16[192]{0:T(256)(128)(2,1)S(1)}, bf16[192]{0:T(256)(128)(2,1)}, u32[]{:S(2)}) copy-start(bf16[192]{0:T(256)(128)(2,1)} %param.28) | copy-start | bytes 1156
  7.3 70.6 %copy-start.76 = (bf16[192]{0:T(256)(128)(2,1)S(1)}, bf16[192]{0:T(256)(128)(2,1)}, u32[]{:S(2)}) copy-start(bf16[192]{0:T(256)(128)(2,1)} %param.29) | copy-start | bytes 1156
  7.3 70.6 %copy-start.77 = (bf16[192]{0:T(256)(128)(2,1)S(1)}, bf16[192]{0:T(256)(128)(2,1)}, u32[]{:S(2)}) copy-start(bf16[192]{0:T(256)(128)(2,1)} %param.33) | copy-start | bytes 1156
  7.3 70.6 %copy-start.71 = (bf16[768]{0:T(1024)(128)(2,1)S(1)}, bf16[768]{0:T(1024)(128)(2,1)}, u32[]{:S(2)}) copy-start(bf16[768]{0:T(1024)(128)(2,1)} %param.31) | copy-start | bytes 4612
  7.3 246.9 %all-gather.5.cloned.1.call-start = ((), (), s32[]{:S(2)}) async-start(), calls=%async_computation.15 | async-start | bytes 10948608 | tf_op jit(solution)/shard_map/all_gather | solution.py:363
  11.1 106.8 %copy-start.54 = (bf16[95,64]{0,1:T(8,128)(2,1)S(1)}, bf16[95,64]{0,1:T(8,128)(2,1)}, u32[]{:S(2)}) copy-start(bf16[95,64]{0,1:T(8,128)(2,1)} %param.34) | copy-start | bytes 36484
  11.2 65.2 %all-to-all-start.1 = ((bf16[8,72,768]{2,1,0:T(8,128)(2,1)}), bf16[8,72,768]{2,1,0:T(8,128)(2,1)S(1)}, u32[]{:S(2)}, u32[]{:S(2)}) async-start(bf16[8,72,768]{2,1,0:T(8,128)(2,1)} %param.18), calls=%async_computation.1 | async-start | bytes 1769472 | tf_op jit(solution)/shard_map/all_to_all | solution.py:291
  21.6 99.2 %copy-start.41 = (s32[48,48]{0,1:T(8,128)}, s32[48,48]{0,1:T(8,128)S(1)}, u32[]{:S(2)}) copy-start(s32[48,48]{0,1:T(8,128)S(1)} %get-tuple-element.150) | copy-start | bytes 27652
  21.6 99.2 %copy-start.43 = (s32[48,48]{0,1:T(8,128)}, s32[48,48]{0,1:T(8,128)S(1)}, u32[]{:S(2)}) copy-start(s32[48,48]{0,1:T(8,128)S(1)} %get-tuple-element.151) | copy-start | bytes 27652
  76.4 197.0 %copy-start.2 = (bf16[8,72,768]{2,1,0:T(8,128)(2,1)}, bf16[8,72,768]{2,1,0:T(8,128)(2,1)S(1)}, u32[]{:S(2)}) copy-start(bf16[8,72,768]{2,1,0:T(8,128)(2,1)S(1)} %all-to-all-done.1) | copy-start | bytes 2654212
  76.4 39.0 %collective-permute-start.1 = (bf16[576,768]{1,0:T(8,128)(2,1)S(1)}, bf16[576,768]{1,0:T(8,128)(2,1)}, u32[]{:S(2)}, u32[]{:S(2)}) collective-permute-start(bf16[576,768]{1,0:T(8,128)(2,1)S(1)} %bitcast.256), channel_id=1, source_target_pairs={{0,2},{1,3},{2,0},{3,1},{4,6},{5,7},{6,4},{7,5},{8,10},{9,11},{10,... | collective-permute-start | bytes 2654216 | tf_op jit(solution)/shard_map/ppermute | solution.py:189
  115.1 11.1 %collective-permute-start = (bf16[576,768]{1,0:T(8,128)(2,1)S(1)}, bf16[576,768]{1,0:T(8,128)(2,1)}, u32[]{:S(2)}, u32[]{:S(2)}) collective-permute-start(bf16[576,768]{1,0:T(8,128)(2,1)S(1)} %bitcast.257), channel_id=1, source_target_pairs={{0,1},{1,0},{2,3},{3,2},{4,5},{5,4},{6,7},{7,6},{8,9},{9,8},{10,11... | collective-permute-start | bytes 2654216 | tf_op jit(solution)/shard_map/ppermute | solution.py:189
  115.4 10.8 %collective-permute-start.2 = (bf16[576,768]{1,0:T(8,128)(2,1)}, bf16[576,768]{1,0:T(8,128)(2,1)}, u32[]{:S(2)}, u32[]{:S(2)}) collective-permute-start(bf16[576,768]{1,0:T(8,128)(2,1)} %collective-permute-done.1), channel_id=1, source_target_pairs={{0,1},{1,0},{2,3},{3,2},{4,5},{5,4},{6,7},{7,6},{8,9},{9,8},{10,11... | collective-permute-start | bytes 2654216 | tf_op jit(solution)/shard_map/ppermute | solution.py:189
  115.7 15.1 %copy-start.60 = (f32[768]{0:T(1024)}, f32[768]{0:T(1024)S(1)}, u32[]{:S(2)}) copy-start(f32[768]{0:T(1024)S(1)} %reshape.765) | copy-start | bytes 9220
  115.8 15.0 %copy-start.49 = (f32[768]{0:T(1024)}, f32[768]{0:T(1024)S(1)}, u32[]{:S(2)}) copy-start(f32[768]{0:T(1024)S(1)} %reshape.764) | copy-start | bytes 9220
  122.2 18.1 %all-to-all-start.2 = ((bf16[4,192,576]{2,1,0:T(8,128)(2,1)}), bf16[4,192,576]{2,1,0:T(8,128)(2,1)S(1)}, u32[]{:S(2)}, u32[]{:S(2)}) async-start(bf16[4,192,576]{2,1,0:T(8,128)(2,1)} %copy.151), calls=%async_computation.2 | async-start | bytes 1966080 | tf_op jit(solution)/shard_map/all_to_all | solution.py:179
  129.4 5.3 copy-start.36
  140.3 8.7 %copy-start.32 = (bf16[4,192,576]{2,1,0:T(8,128)(2,1)}, bf16[4,192,576]{2,1,0:T(8,128)(2,1)S(1)}, u32[]{:S(2)}) copy-start(bf16[4,192,576]{2,1,0:T(8,128)(2,1)S(1)} %all-to-all-done.2) | copy-start | bytes 2654212
  140.3 91.7 %all-to-all-start = ((bf16[8,72,768]{2,1,0:T(8,128)(2,1)}), bf16[8,72,768]{2,1,0:T(8,128)(2,1)}, u32[]{:S(2)}, u32[]{:S(2)}) async-start(bf16[8,72,768]{2,1,0:T(8,128)(2,1)} %param.19), calls=%async_computation | async-start | bytes 1769472 | tf_op jit(solution)/shard_map/all_to_all | solution.py:293
  172.4 5.3 copy-start.16
  185.5 5.2 copy-start.28
  232.0 19.3 %all-to-all-start.3 = ((bf16[8,4,72,1,192]{4,2,0,3,1:T(8,128)(2,1)}), bf16[8,4,72,1,192]{4,2,0,3,1:T(8,128)(2,1)S(1)}, u32[]{:S(2)}, u32[]{:S(2)}) async-start(bf16[8,4,72,1,192]{4,2,0,3,1:T(8,128)(2,1)} %copy.160), calls=%async_computation.3 | async-start | bytes 2359296 | tf_op jit(solution)/shard_map/all_to_all | solution.py:383
  235.5 475.1 %reduce-scatter.2.cloned.1.call-start = ((), (), s32[]{:S(2)}) async-start(), calls=%async_computation.14 | async-start | bytes 10948608 | tf_op jit(solution)/shard_map/reduce_scatter | solution.py:442
  236.3 37.1 %copy-start.57 = (f32[576]{0:T(1024)}, f32[576]{0:T(1024)S(1)}, u32[]{:S(2)}) copy-start(f32[576]{0:T(1024)S(1)} %fusion.86) | copy-start | bytes 6916
  267.7 5.7 copy-start.34
  286.5 8.7 %slice-start = ((s8[4718592]{0:T(1024)(128)(4,1)}), s8[4194304]{0:T(1024)(128)(4,1)S(1)}, s32[]{:S(2)}) async-start(s8[4718592]{0:T(1024)(128)(4,1)} %bitcast.267), calls=%async_computation.16 | async-start | bytes 8388608
  300.0 5.1 copy-start.23
  336.8 7.2 copy-start.5
  336.8 7.2 copy-start.52
  336.8 7.2 copy-start.58
  424.3 12.4 %all-to-all-start.11 = ((f32[32,1,192]{2,1,0:T(1,128)}), f32[32,1,192]{2,1,0:T(1,128)}, u32[]{:S(2)}, u32[]{:S(2)}) async-start(f32[32,1,192]{2,1,0:T(1,128)} %copy.206), calls=%async_computation.12 | async-start | bytes 65536 | tf_op jit(solution)/shard_map/all_to_all | solution.py:179
  431.7 9.3 %copy-start.59 = (f32[576]{0:T(1024)S(1)}, f32[576]{0:T(1024)}, u32[]{:S(2)}) copy-start(f32[576]{0:T(1024)} %copy-done.57) | copy-start | bytes 6916
  431.7 9.3 %copy-start.70 = (f32[768]{0:T(1024)S(1)}, f32[768]{0:T(1024)}, u32[]{:S(2)}) copy-start(f32[768]{0:T(1024)} %reshape.771) | copy-start | bytes 9220
  436.7 20.2 %all-to-all-start.4 = ((bf16[8,1,72,4,192]{4,2,1,0,3:T(8,128)(2,1)}), bf16[8,1,72,4,192]{4,2,1,0,3:T(8,128)(2,1)}, u32[]{:S(2)}, u32[]{:S(2)}) async-start(bf16[8,1,72,4,192]{4,2,1,0,3:T(8,128)(2,1)} %copy.168), calls=%async_computation.4 | async-start | bytes 2359296 | tf_op jit(solution)/shard_map/all_to_all | solution.py:420
  448.7 16.3 %copy-start.39 = (f32[8,4,72]{2,1,0:T(4,128)S(1)}, f32[8,4,72]{2,1,0:T(4,128)}, u32[]{:S(2)}) copy-start(f32[8,4,72]{2,1,0:T(4,128)} %copy-done.38) | copy-start | bytes 27652
  448.7 17.0 %copy-start.37 = (f32[8,4,72]{2,1,0:T(4,128)S(1)}, f32[8,4,72]{2,1,0:T(4,128)}, u32[]{:S(2)}) copy-start(f32[8,4,72]{2,1,0:T(4,128)} %copy-done.36) | copy-start | bytes 27652
  456.9 12.2 %copy-start.15 = (bf16[3,2304,96]{1,2,0:T(8,128)(2,1)S(1)}, bf16[3,2304,96]{1,2,0:T(8,128)(2,1)}, u32[]{:S(2)}) copy-start(bf16[3,2304,96]{1,2,0:T(8,128)(2,1)} %copy-done.14) | copy-start | bytes 3981316
  456.9 12.2 %copy-start.17 = (bf16[3,2304,64]{1,2,0:T(8,128)(2,1)S(1)}, bf16[3,2304,64]{1,2,0:T(8,128)(2,1)}, u32[]{:S(2)}) copy-start(bf16[3,2304,64]{1,2,0:T(8,128)(2,1)} %get-tuple-element.119) | copy-start | bytes 2654212
  456.9 41.7 %all-to-all-start.5 = ((bf16[8,72,768]{2,1,0:T(8,128)(2,1)}), bf16[8,72,768]{2,1,0:T(8,128)(2,1)S(1)}, u32[]{:S(2)}, u32[]{:S(2)}) async-start(bf16[8,72,768]{2,1,0:T(8,128)(2,1)} %bitcast.323), calls=%async_computation.5 | async-start | bytes 1769472 | tf_op jit(solution)/shard_map/all_to_all | solution.py:179
  471.3 10.2 %copy-start.18 = (f32[2304,192]{0,1:T(8,128)S(1)}, f32[2304,192]{0,1:T(8,128)}, u32[]{:S(2)}) copy-start(f32[2304,192]{0,1:T(8,128)} %copy.170) | copy-start | bytes 5308420
  498.6 52.9 %copy-start.26 = (bf16[8,72,768]{2,1,0:T(8,128)(2,1)}, bf16[8,72,768]{2,1,0:T(8,128)(2,1)S(1)}, u32[]{:S(2)}) copy-start(bf16[8,72,768]{2,1,0:T(8,128)(2,1)S(1)} %all-to-all-done.5) | copy-start | bytes 2654212
  499.2 97.7 %all-to-all-start.12 = ((f32[8,1,192]{2,1,0:T(1,128)}), f32[8,1,192]{2,1,0:T(1,128)}, u32[]{:S(2)}, u32[]{:S(2)}) async-start(f32[8,1,192]{2,1,0:T(1,128)} %broadcast_in_dim.114), calls=%async_computation.13 | async-start | bytes 16384 | tf_op jit(solution)/shard_map/all_to_all | solution.py:179
  565.2 7.0 copy-start.50
  565.2 7.0 copy-start.61
  584.1 26.2 %collective-permute-start.3 = (bf16[2,576,768]{2,1,0:T(8,128)(2,1)}, bf16[2,576,768]{2,1,0:T(8,128)(2,1)}, u32[]{:S(2)}, u32[]{:S(2)}) collective-permute-start(bf16[2,576,768]{2,1,0:T(8,128)(2,1)} %pad_maximum_fusion.7), channel_id=1, source_target_pairs={{0,1},{1,0},{2,3},{3,2},{4,5},{5,4},{6,7},{7,6},{8,9},{9,8},{10,11... | collective-permute-start | bytes 5308424 | tf_op jit(solution)/shard_map/ppermute | solution.py:189
  586.1 6.9 copy-start.22
  586.1 6.9 copy-start.31
  597.0 15.1 %all-to-all-start.7 = ((f32[32,1,476]{2,1,0:T(1,128)}), f32[32,1,476]{2,1,0:T(1,128)}, u32[]{:S(2)}, u32[]{:S(2)}) async-start(f32[32,1,476]{2,1,0:T(1,128)} %copy.192), calls=%async_computation.7 | async-start | bytes 131072 | tf_op jit(solution)/shard_map/all_to_all | solution.py:179
  612.1 18.6 %all-to-all-start.9 = ((bf16[4,192,576]{2,1,0:T(8,128)(2,1)}), bf16[4,192,576]{2,1,0:T(8,128)(2,1)}, u32[]{:S(2)}, u32[]{:S(2)}) async-start(bf16[4,192,576]{2,1,0:T(8,128)(2,1)} %bitcast.314), calls=%async_computation.9 | async-start | bytes 1966080 | tf_op jit(solution)/shard_map/all_to_all | solution.py:179
  618.6 36.9 %collective-permute-start.4 = (bf16[576,768]{1,0:T(8,128)(2,1)}, bf16[576,768]{1,0:T(8,128)(2,1)}, u32[]{:S(2)}, u32[]{:S(2)}) collective-permute-start(bf16[576,768]{1,0:T(8,128)(2,1)} %fusion.42), channel_id=1, source_target_pairs={{0,2},{1,3},{2,0},{3,1},{4,6},{5,7},{6,4},{7,5},{8,10},{9,11},{10,... | collective-permute-start | bytes 2654216 | tf_op jit(solution)/shard_map/ppermute | solution.py:189
  631.4 19.6 %all-to-all-start.8 = ((f32[32,1,476]{2,1,0:T(1,128)}), f32[32,1,476]{2,1,0:T(1,128)}, u32[]{:S(2)}, u32[]{:S(2)}) async-start(f32[32,1,476]{2,1,0:T(1,128)} %broadcast_in_dim.112), calls=%async_computation.8 | async-start | bytes 131072 | tf_op jit(solution)/shard_map/all_to_all | solution.py:179
  637.7 17.8 %copy-start.51 = (f32[768]{0:T(1024)S(1)}, f32[768]{0:T(1024)}, u32[]{:S(2)}) copy-start(f32[768]{0:T(1024)} %copy-done.49) | copy-start | bytes 9220
  650.9 33.5 %all-to-all-start.10 = ((bf16[8,192,288]{1,2,0:T(8,128)(2,1)}), bf16[8,192,288]{1,2,0:T(8,128)(2,1)}, u32[]{:S(2)}, u32[]{:S(2)}) async-start(bf16[8,192,288]{1,2,0:T(8,128)(2,1)} %bitcast.309), calls=%async_computation.10 | async-start | bytes 2359296 | tf_op jit(solution)/shard_map/all_to_all | solution.py:179
  684.4 30.5 %copy-start.27 = (bf16[8,72,768]{2,1,0:T(8,128)(2,1)S(1)}, bf16[8,72,768]{2,1,0:T(8,128)(2,1)}, u32[]{:S(2)}) copy-start(bf16[8,72,768]{2,1,0:T(8,128)(2,1)} %copy-done.26) | copy-start | bytes 2654212
  684.4 26.2 %all-to-all-start.6 = ((bf16[8,72,768]{2,1,0:T(8,128)(2,1)}), bf16[8,72,768]{2,1,0:T(8,128)(2,1)S(1)}, u32[]{:S(2)}, u32[]{:S(2)}) async-start(bf16[8,72,768]{2,1,0:T(8,128)(2,1)} %bitcast.71), calls=%async_computation.6 | async-start | bytes 1769472 | tf_op jit(solution)/shard_map/all_to_all | solution.py:179
  697.7 19.0 %copy-start.1 = (bf16[95,64]{0,1:T(8,128)(2,1)S(1)}, bf16[95,64]{0,1:T(8,128)(2,1)}, u32[]{:S(2)}) copy-start(bf16[95,64]{0,1:T(8,128)(2,1)} %param.35) | copy-start | bytes 36484
  (39 other events, 78.8 us)
Sparse Core Ops, SparseCore 0:
  11.3 117.1 all-gather.4
  421.8 151.1 reduce-scatter.1

commit v3 on v2

--- a/solution.py
+++ b/solution.py
@@ -138,6 +138,170 @@
         name="attend_backward",
         compiler_params=pltpu.CompilerParams(dimension_semantics=("arbitrary",)),
     )(q_aug, grads, lse, delta, k_aug, values, k_turn)
+
+
+def norm_parts(values):
+    center = values - jnp.mean(values, axis=-1, keepdims=True)
+    scale = lax.rsqrt(jnp.mean(center * center, axis=-1, keepdims=True) + 1e-06)
+    return center * scale, scale
+
+
+def feed_kernel(
+    mid_ref,
+    cot_ref,
+    mask_ref,
+    vec_ref,
+    shift_ref,
+    up_ref,
+    down_ref,
+    out_ref,
+    total_ref,
+    branch_ref,
+    sums_ref,
+    up_bias_ref,
+    up_grad_ref,
+    down_grad_ref,
+    normed_ref,
+    turned_ref,
+    down_in_ref,
+    down_turn_ref,
+    out_acc_ref,
+    in_acc_ref,
+    weight_ref,
+):
+    f32 = jnp.float32
+    bf16 = jnp.bfloat16
+    step = pl.program_id(0)
+    groups, heads, height, width = up_ref.shape
+    cols = weight_ref.shape[1] // groups
+    folds = width // cols
+    rows = height * folds
+    pieces, _, out_cols, _ = down_ref.shape
+
+    @pl.when(step == 0)
+    def _():
+        unit, _ = norm_parts(mid_ref[...])
+        normed = (unit * vec_ref[1:2] + vec_ref[2:3]).astype(bf16)
+        normed_ref[...] = normed
+        turned_ref[...] = normed.T
+        masked = mask_ref[...] * cot_ref[...].astype(f32)
+        down_in_ref[...] = masked.astype(bf16)
+        down_turn_ref[...] = masked.astype(bf16).T
+        out_acc_ref[...] = jnp.zeros_like(out_acc_ref)
+        in_acc_ref[...] = jnp.zeros_like(in_acc_ref)
+
+    for g in range(groups):
+        for h in range(heads):
+            for s in range(folds):
+                top = h * rows + s * height
+                weight_ref[top : top + height, g * cols : (g + 1) * cols] = up_ref[
+                    g, h, :, s * cols : (s + 1) * cols
+                ]
+    weight = weight_ref[...]
+    down = down_ref[...].reshape(pieces * out_cols, width)
+    hidden = mm(normed_ref[...], weight) + shift_ref[0]
+    share = 0.5 * (1.0 + lax.erf(hidden * (0.5**0.5)))
+    active = (hidden * share).astype(bf16)
+    slope = share + hidden * jnp.exp(-0.5 * hidden * hidden) * 0.3989422804014327
+    out_acc_ref[...] += mm_nt(active, down)
+    hidden_grad = (mm(down_in_ref[...], down) * slope).astype(bf16)
+    down_grad_ref[...] = (
+        mm(down_turn_ref[...], active).astype(bf16).reshape(pieces, 1, out_cols, width)
+    )
+    in_acc_ref[...] += mm_nt(hidden_grad, weight)
+    up_bias_ref[0] = jnp.sum(hidden_grad.astype(f32), axis=0, keepdims=True)
+    up_grad = mm(turned_ref[...], hidden_grad).astype(bf16)
+    for g in range(groups):
+        for h in range(heads):
+            for s in range(folds):
+                top = h * rows + s * height
+                up_grad_ref[g, h, :, s * cols : (s + 1) * cols] = up_grad[
+                    top : top + height, g * cols : (g + 1) * cols
+                ]
+
+    @pl.when(step == pl.num_programs(0) - 1)
+    def _():
+        middle = mid_ref[...]
+        mask = mask_ref[...]
+        cot = cot_ref[...].astype(f32)
+        out_ref[...] = (middle + mask * (out_acc_ref[...] + vec_ref[3:4])).astype(bf16)
+        unit, scale = norm_parts(middle)
+        grad_in = in_acc_ref[...]
+        inner = grad_in * vec_ref[1:2]
+        total = cot + scale * (
+            inner
+            - jnp.mean(inner, axis=-1, keepdims=True)
+            - unit * jnp.mean(inner * unit, axis=-1, keepdims=True)
+        )
+        branch = (mask * total).astype(bf16)
+        total_ref[...] = total
+        branch_ref[...] = branch
+        sums_ref[...] = jnp.concatenate(
+            [
+                jnp.sum(branch.astype(f32), axis=0, keepdims=True),
+                jnp.sum(grad_in * unit, axis=0, keepdims=True),
+                jnp.sum(grad_in, axis=0, keepdims=True),
+                jnp.sum(mask * cot, axis=0, keepdims=True),
+            ],
+            axis=0,
+        )
+
+
+def feed_forward(middle, cot, mask, vectors, shift, gathered, up_height, up_cols, out_cols):
+    tokens, width = middle.shape
+    groups, heads = gathered.shape[:2]
+    steps = shift.shape[0]
+    per_step = groups // steps
+    f32 = jnp.float32
+    bf16 = jnp.bfloat16
+
+    def whole(rows, cols):
+        return pl.BlockSpec((rows, cols), lambda c: (0, 0))
+
+    up_spec = (per_step, heads, up_height, width)
+    down_spec = (groups, 1, out_cols, width)
+    return pl.pallas_call(
+        feed_kernel,
+        grid=(steps,),
+        in_specs=[
+            whole(tokens, width),
+            whole(tokens, width),
+            whole(tokens, 1),
+            whole(vectors.shape[0], width),
+            pl.BlockSpec((1, 1, width), lambda c: (c, 0, 0)),
+            pl.BlockSpec(up_spec, lambda c: (c, 0, 0, 0)),
+            pl.BlockSpec(down_spec, lambda c: (0, c, 1, 0)),
+        ],
+        out_specs=[
+            whole(tokens, width),
+            whole(tokens, width),
+            whole(tokens, width),
+            whole(4, width),
+            pl.BlockSpec((1, 1, width), lambda c: (c, 0, 0)),
+            pl.BlockSpec(up_spec, lambda c: (c, 0, 0, 0)),
+            pl.BlockSpec(down_spec, lambda c: (0, c, 0, 0)),
+        ],
+        out_shape=[
+            jax.ShapeDtypeStruct((tokens, width), bf16),
+            jax.ShapeDtypeStruct((tokens, width), f32),
+            jax.ShapeDtypeStruct((tokens, width), bf16),
+            jax.ShapeDtypeStruct((4, width), f32),
+            jax.ShapeDtypeStruct((steps, 1, width), f32),
+            jax.ShapeDtypeStruct((groups, heads, up_height, width), bf16),
+            jax.ShapeDtypeStruct((groups, heads, out_cols, width), bf16),
+        ],
+        scratch_shapes=[
+            pltpu.VMEM((tokens, width), bf16),
+            pltpu.VMEM((width, tokens), bf16),
+            pltpu.VMEM((tokens, width), bf16),
+            pltpu.VMEM((width, tokens), bf16),
+            pltpu.VMEM((tokens, width), f32),
+            pltpu.VMEM((tokens, width), f32),
+            pltpu.VMEM((width, width), bf16),
+        ],
+        name="feed_forward",
+        compiler_params=pltpu.CompilerParams(dimension_semantics=("arbitrary",)),
+    )(middle, cot, mask, vectors, shift, gathered, gathered)
 
 
 def layer_norm(values, gain, shift):
@@ -275,6 +439,11 @@
         [norm1_gain, norm1_bias, proj_bias, norm2_gain, norm2_bias, fc2_bias, fc1_bias]
     )
     vectors_all = lax.all_gather(vectors, "ha", axis=0, tiled=False)
+    tokens_in = lax.all_to_all(patches, "ga", split_axis=0, concat_axis=1, tiled=True)[0]
+    tokens_in, triple_rows, vectors_all, packed = lax.optimization_barrier(
+        (tokens_in, triple_rows, vectors_all, packed)
+    )
+    cot_in = lax.all_to_all(cotangent, "ga", split_axis=0, concat_axis=1, tiled=True)[0]
     wide = model_width // head_groups
 
     def vector_at(slot, width):
@@ -288,9 +457,6 @@
     down_shift = vector_at(5, wide)
     up_shift = vector_at(6, 4 * wide)
 
-    tokens_in = lax.all_to_all(patches, "ga", split_axis=0, concat_axis=1, tiled=True)[0]
-    tokens_in, triple_rows = lax.optimization_barrier((tokens_in, triple_rows))
-    cot_in = lax.all_to_all(cotangent, "ga", split_axis=0, concat_axis=1, tiled=True)[0]
     triple_cut = triple_rows.reshape(group_width, 3, head_groups, group_width).transpose(2, 0, 1, 3)
     triple_own = exchange(
         triple_cut.reshape(head_groups, group_width, 3 * group_width), "ha"
@@ -363,16 +529,6 @@
     gathered = lax.all_gather(packed, BOTH, axis=0, tiled=False).reshape(
         group_count, head_groups, pack_rows, model_width
     )
-    up_full = (
-        unpack_up(gathered[:, :, :up_height], up_rows, up_cols)
-        .transpose(1, 2, 0, 3)
-        .reshape(model_width, hidden_width)
-    )
-    down_turn = (
-        gathered[:, :, up_height : up_height + out_cols]
-        .transpose(0, 2, 1, 3)
-        .reshape(model_width, hidden_width)
-    )
     proj_turn = (
         gathered[:, :, up_height + out_cols :]
         .reshape(group_count, head_groups, out_cols, group_width)
@@ -390,32 +546,72 @@
     att_tok = att_back.reshape(local_tokens, model_width)
     branch = contract_cols(att_tok, proj_turn) + proj_shift.astype(f32)
     middle = tokens32 + tok_mask * branch
-    normed2 = layer_norm(middle, second_gain.astype(f32), second_shift.astype(f32)).astype(bf16)
-    hidden = jnp.dot(normed2, up_full, preferred_element_type=f32) + up_shift.astype(f32)
-    activated = jax.nn.gelu(hidden, approximate=False).astype(bf16)
-    block_out = (
-        middle + tok_mask * (contract_cols(activated, down_turn) + down_shift.astype(f32))
-    ).astype(bf16)
-    out_back = exchange(block_out.reshape(group_count, block_len, model_width), "ga")
-
-    masked_cot = tok_mask * cot32
-    down_in = masked_cot.astype(bf16)
-    down_grad = contract_rows(down_in, activated).astype(bf16)
-    down_bias_grad = jnp.sum(masked_cot, axis=0)
-    act_grad = jnp.dot(down_in, down_turn, preferred_element_type=f32)
-    gelu_value, gelu_pull = jax.vjp(partial(jax.nn.gelu, approximate=False), hidden)
-    hidden_grad = gelu_pull(act_grad)[0].astype(bf16)
-    up_grad = contract_rows(normed2, hidden_grad).astype(bf16)
-    up_bias_grad = jnp.sum(hidden_grad.astype(f32), axis=0)
-    norm2_in = contract_cols(hidden_grad, up_full)
-    norm2_value, norm2_pull = jax.vjp(
-        layer_norm, middle, second_gain.astype(f32), second_shift.astype(f32)
-    )
-    mid_grad, second_gain_grad, second_shift_grad = norm2_pull(norm2_in)
-    mid_total = cot32 + mid_grad
-    branch_grad = (tok_mask * mid_total).astype(bf16)
+    steps = hidden_width // model_width
+    if out_cols % 16 == 0 and up_cols % 128 == 0 and up_height == out_cols and steps == head_groups:
+        norm_vectors = jnp.stack([proj_shift, second_gain, second_shift, down_shift]).astype(f32)
+        (
+            block_out,
+            mid_total,
+            branch_grad,
+            small_sums,
+            up_bias_grad,
+            up_packed,
+            down_packed,
+        ) = feed_forward(
+            middle,
+            cot_in,
+            tok_mask,
+            norm_vectors,
+            up_shift.astype(f32).reshape(steps, 1, model_width),
+            gathered,
+            up_height,
+            up_cols,
+            out_cols,
+        )
+        up_bias_grad = up_bias_grad.reshape(-1)
+        proj_bias_grad, second_gain_grad, second_shift_grad, down_bias_grad = small_sums
+    else:
+        up_full = (
+            unpack_up(gathered[:, :, :up_height], up_rows, up_cols)
+            .transpose(1, 2, 0, 3)
+            .reshape(model_width, hidden_width)
+        )
+        down_turn = (
+            gathered[:, :, up_height : up_height + out_cols]
+            .transpose(0, 2, 1, 3)
+            .reshape(model_width, hidden_width)
+        )
+        normed2 = layer_norm(middle, second_gain.astype(f32), second_shift.astype(f32)).astype(bf16)
+        hidden = jnp.dot(normed2, up_full, preferred_element_type=f32) + up_shift.astype(f32)
+        activated = jax.nn.gelu(hidden, approximate=False).astype(bf16)
+        block_out = (
+            middle + tok_mask * (contract_cols(activated, down_turn) + down_shift.astype(f32))
+        ).astype(bf16)
+        masked_cot = tok_mask * cot32
+        down_in = masked_cot.astype(bf16)
+        down_grad = contract_rows(down_in, activated).astype(bf16)
+        down_bias_grad = jnp.sum(masked_cot, axis=0)
+        act_grad = jnp.dot(down_in, down_turn, preferred_element_type=f32)
+        gelu_value, gelu_pull = jax.vjp(partial(jax.nn.gelu, approximate=False), hidden)
+        hidden_grad = gelu_pull(act_grad)[0].astype(bf16)
+        up_grad = contract_rows(normed2, hidden_grad).astype(bf16)
+        up_bias_grad = jnp.sum(hidden_grad.astype(f32), axis=0)
+        norm2_in = contract_cols(hidden_grad, up_full)
+        norm2_value, norm2_pull = jax.vjp(
+            layer_norm, middle, second_gain.astype(f32), second_shift.astype(f32)
+        )
+        mid_grad, second_gain_grad, second_shift_grad = norm2_pull(norm2_in)
+        mid_total = cot32 + mid_grad
+        branch_grad = (tok_mask * mid_total).astype(bf16)
+        up_packed = pack_up(
+            up_grad.reshape(head_groups, up_rows, group_count, up_cols).transpose(2, 0, 1, 3)
+        )
+        down_packed = down_grad.reshape(group_count, out_cols, head_groups, model_width).transpose(
+            0, 2, 1, 3
+        )
+        proj_bias_grad = jnp.sum(branch_grad.astype(f32), axis=0)
+
     proj_grad = contract_rows(branch_grad, att_tok).astype(bf16)
-    proj_bias_grad = jnp.sum(branch_grad.astype(f32), axis=0)
     att_grad_tok = jnp.dot(branch_grad, proj_turn, preferred_element_type=f32).astype(bf16)
     att_grad = lax.all_to_all(
         att_grad_tok.reshape(group_count, 1, block_len, head_groups, group_width),
@@ -424,15 +620,19 @@
         concat_axis=1,
         tiled=True,
     ).reshape(cap_tokens, group_width)
+    att_grad, block_out, early_in = lax.optimization_barrier(
+        (
+            att_grad,
+            block_out,
+            [proj_bias_grad, second_gain_grad, second_shift_grad, down_bias_grad, up_bias_grad],
+        )
+    )
+    out_back = exchange(block_out.reshape(group_count, block_len, model_width), "ga")
 
     grads_packed = jnp.concatenate(
         [
-            pack_up(
-                up_grad.reshape(head_groups, up_rows, group_count, up_cols).transpose(2, 0, 1, 3)
-            ),
-            down_grad.reshape(group_count, out_cols, head_groups, model_width).transpose(
-                0, 2, 1, 3
-            ),
+            up_packed,
+            down_packed,
             proj_grad.reshape(group_count, out_cols, head_groups, group_width)
             .transpose(0, 2, 1, 3)
             .reshape(group_count, head_groups, out_cols // head_groups, model_width),
@@ -464,9 +664,7 @@
             at += size
         return result
 
-    early = reduce_vectors(
-        [proj_bias_grad, second_gain_grad, second_shift_grad, down_bias_grad, up_bias_grad]
-    )
+    early = reduce_vectors(early_in)
 
     grad_heads = att_grad.reshape(cap_tokens, group_heads, HD)
     delta = (

time: 734 us -> 632 us (0.86)
  local copies, waits for them, and re-layouts: 204 us -> 129 us
  matrix products: 94.7 us -> 48.8 us
  Pallas kernels: 85.8 us -> 116 us
  waiting for transfers between devices: 91.4 us -> 112 us
  other arithmetic: 79.4 us -> 66.9 us
  blocking collectives: 87 us -> 77.2 us
  starting transfers between devices: 65.3 us -> 56.8 us
    reshape x5 -> x3, local copies, waits for them, and re-layouts: 39.3 us -> 6.04 us  [the longest x1 3.05 us: local(): grads_packed = jnp.concatenate([up_packed, down_packed, proj_grad.reshape...]
    all_to_all x0 -> x2, blocking collectives: none -> 31.1 us  [the longest x1 19 us: local(): lax.all_to_all(att_heads.reshape(group_count, head_groups, block_len, 1,...]
    pallas_call x0 -> x1, Pallas kernels: none -> 30 us  [feed_forward(): pl.pallas_call(feed_kernel, grid=(steps,), in_specs=[whole(tokens, width)...]
    all_gather x1, blocking collectives: 32.2 us -> 5.22 us  [local(): vectors_all = lax.all_gather(vectors, 'ha', axis=0, tiled=False)]
    dot_general x2 -> x0, matrix products: 24.1 us -> none  [the longest x1 21.1 us: local(): act_grad = jnp.dot(down_in, down_turn, preferred_element_type=f32)]
    transpose x3 -> x0, local copies, waits for them, and re-layouts: 16.4 us -> none  [the longest x1 9.3 us: pack_up(): jnp.swapaxes(cut, -3, -2).reshape(lead + (rows // fold, fold * width))]
    all_to_all x9 -> x8, waiting for transfers between devices: 71.9 us -> 86.6 us  [exchange(): return lax.all_to_all(values, axis, split_axis=0, concat_axis=0, tiled=True)]
    all_gather x1, blocking collectives: 54.8 us -> 40.9 us  [local(): triple_rows = lax.all_gather(qkv_weight, 'ga', axis=1, tiled=True)]
  transfers between devices with their start and end apart: 20 -> 18, of which waited for: 9 -> 8; matrix products, arithmetic and copies ran while one was open for 27% -> 33% of each run, Pallas kernels for 12% -> 14%
where the time goes in v3:
time: 632 us; the launch traced here: 624 us
  local copies, waits for them, and re-layouts  129 us (20%)
  Pallas kernels  116 us (18%)
  waiting for transfers between devices  112 us (18%)
  blocking collectives  77.2 us (12%)
  other arithmetic  66.9 us (11%)
  starting transfers between devices  56.8 us (9%)
  matrix products  48.8 us (8%)
  between operations  16.3 us (3%)
    all_to_all x8, waiting for transfers between devices, exchange(): return lax.all_to_all(values, axis, split_axis=0, concat_axis=0, tiled=True)  86.6 us
    pallas_call x1, Pallas kernels, attend_backward(): pl.pallas_call(backward_kernel, grid=(tokens // TBLK,), in_specs=[pl.Bloc...  48 us
    all_gather x1, blocking collectives, local(): triple_rows = lax.all_gather(qkv_weight, 'ga', axis=1, tiled=True)  40.9 us
    pallas_call x1, Pallas kernels, attend_forward(): pl.pallas_call(forward_kernel, grid=(tokens // TBLK,), in_specs=[pl.Block...  37.7 us
    all_to_all x8, starting transfers between devices, exchange(): return lax.all_to_all(values, axis, split_axis=0, concat_axis=0, tiled=True)  36.6 us
    pallas_call x1, Pallas kernels, feed_forward(): pl.pallas_call(feed_kernel, grid=(steps,), in_specs=[whole(tokens, width)...  30 us
    all_to_all x1, blocking collectives, local(): lax.all_to_all(att_heads.reshape(group_count, head_groups, block_len, 1,...  19 us
    unnamed x148, local copies, waits for them, and re-layouts  17.1 us
  transfers between devices with their start and end apart: 18, of which 8 were waited for; matrix products, arithmetic and copies ran while one was open for 33% of the time, Pallas kernels for 14%

profile of v3, /device:TPU:0, one launch (start us, length us, event | category | flops | bytes accessed | tf_op | source)
XLA Modules:
  0.0 623.5 jit_solution(9034405195623472266)
XLA Ops:
  7.3 7.5 %all-to-all-start = ((bf16[8,72,768]{2,1,0:T(8,128)(2,1)}), bf16[8,72,768]{2,1,0:T(8,128)(2,1)S(1)}, u32[]{:S(2)}, u32[]{:S(2)}) async-start(bf16[8,72,768]{2,1,0:T(8,128)(2,1)} %param.18), calls=%async_computation | async-start | bytes 1769472 | tf_op jit(solution)/shard_map/all_to_all | solution.py:442
  15.6 5.2 all-gather.2
  21.5 40.9 %all_gather.15 = bf16[192,2304]{0,1:T(8,128)(2,1)S(1)} all-gather(bf16[192,288]{0,1:T(8,128)(2,1)S(1)} %copy.254), channel_id=1, replica_groups=mesh['ga'=8,'ha'=4] {'ga'}, dimensions={1}, use_global_device_ids=true | all-gather | bytes 995328 | tf_op jit(solution)/shard_map/all_gather | solution.py:424
  75.4 9.9 %collective-permute-done.1 = bf16[576,768]{1,0:T(8,128)(2,1)} collective-permute-done((bf16[576,768]{1,0:T(8,128)(2,1)S(1)}, bf16[576,768]{1,0:T(8,128)(2,1)}, u32[]{:S(2)}, u32[]{:S(2)}) %collective-permute-start.1) | collective-permute-done | bytes 884768 | tf_op jit(solution)/shard_map/ppermute | solution.py:353
  88.6 3.7 all-to-all-start.1
  97.4 3.1 add_convert_fusion.1
  100.6 11.2 %all-to-all-done.1 = bf16[4,192,576]{2,1,0:T(8,128)(2,1)S(1)} async-done(((bf16[4,192,576]{2,1,0:T(8,128)(2,1)}), bf16[4,192,576]{2,1,0:T(8,128)(2,1)S(1)}, u32[]{:S(2)}, u32[]{:S(2)}) %all-to-all-start.1) | async-done | bytes 884768 | tf_op jit(solution)/shard_map/all_to_all | solution.py:343
  111.8 4.6 add_convert_fusion.2
  118.6 4.2 reshape_squeeze.6
  122.8 3.7 copy.262
  126.5 3.1 copy.260
  129.7 2.7 fusion.94
  138.2 3.0 copy.265
  145.4 5.8 copy.266.k_ref
  151.2 3.0 fusion.1
  154.2 3.5 pad_maximum_fusion.4.q_ref
  159.0 37.7 %attend_forward.1 = (bf16[2304,192]{1,0:T(8,128)(2,1)}, f32[3,1,2304]{2,1,0:T(1,128)}) custom-call(bf16[3,2304,256]{2,1,0:T(8,128)(2,1)} %pad_maximum_fusion.4.q_ref, bf16[3,2304,256]{2,1,0:T(8,128)(2,1)} %copy.266.k_ref, bf16[3,80,2304]{2,1,0:T(8,128)(2,1)} %maximum_maximum_fusion.v_ref), custom_call_target="tpu_custom_call" | custom-call | tf_op jit(solution)/shard_map/attend_forward/pallas_call | solution.py:51
  198.1 19.0 %all_to_all.93 = bf16[8,4,72,1,192]{4,2,0,3,1:T(8,128)(2,1)} all-to-all(bf16[8,4,72,1,192]{4,2,0,3,1:T(8,128)(2,1)S(1)} %copy.267), channel_id=1, replica_groups=mesh['ga'=8,'ha'=4] {'ha'}, dimensions={1} | all-to-all | bytes 1769472 | tf_op jit(solution)/shard_map/all_to_all | solution.py:539
  217.1 5.5 all-to-all-start.3
  235.2 3.2 copy.268
  238.4 3.2 reshape.678
  241.5 2.4 slice.132
  243.9 3.9 reshape.680
  247.8 2.8 copy.269
  250.6 3.8 reshape.681
  254.5 3.6 convert_add_fusion.mid_ref
  259.0 30.0 %feed_forward.1 = (bf16[576,768]{1,0:T(8,128)(2,1)}, f32[576,768]{1,0:T(8,128)}, bf16[576,768]{1,0:T(8,128)(2,1)}, f32[4,768]{1,0:T(4,128)}, f32[4,1,768]{2,1,0:...) custom-call(f32[576,768]{1,0:T(8,128)} %convert_add_fusion.mid_ref, ...), custom_call_target="tpu_custom_call" | custom-call | tf_op jit(solution)/shard_map/feed_forward/pallas_call | solution.py:263
  289.0 3.3 convolution_convert_fusion
  292.4 3.5 reshape.710
  297.3 3.1 reshape.711
  300.4 9.7 %pad_maximum_fusion = bf16[8,4,216,768]{3,2,1,0:T(8,128)(2,1)} fusion(bf16[8,4,24,768]{3,2,1,0:T(8,128)(2,1)S(1)} %reshape.711, bf16[8,4,96,768]{3,2,1,0:T(8,128)(2,1)} %get-tuple-element.61, bf16[8,4,96,768]{3,2,1,0:T(8,128)(2,1)} %get-tuple-element.60), kind=kLoop, calls=%fused_computation | loop fusion | flops 31850496 | bytes 21233664 | tf_op jit(solution)/shard_map/concatenate | solution.py:632
  311.3 3.0 convolution_convert_fusion.1
  314.3 2.9 reshape.683
  318.3 3.7 all-to-all-start.4
  322.1 15.7 %all-to-all-done.4 = bf16[8,1,72,4,192]{4,2,0,1,3:T(8,128)(2,1)S(1)} async-done(((bf16[8,1,72,4,192]{4,2,0,1,3:T(8,128)(2,1)}), bf16[8,1,72,4,192]{4,2,0,1,3:T(8,128)(2,1)S(1)}, u32[]{:S(2)}, u32[]{:S(2)}) %all-to-all-start.4) | async-done | bytes 884768 | tf_op jit(solution)/shard_map/all_to_all | solution.py:616
  339.5 12.1 %all_to_all.94 = f32[32,1,192]{2,1,0:T(1,128)S(1)} all-to-all(f32[32,1,192]{2,1,0:T(1,128)S(1)} %copy.309), channel_id=1, replica_groups=mesh['ga'=8,'ha'=4] {'ga','ha'}, dimensions={0} | all-to-all | bytes 49152 | tf_op jit(solution)/shard_map/all_to_all | solution.py:343
  351.6 4.2 all-to-all-start.5
  358.9 2.6 copy.279.v_ref
  361.5 2.6 maximum_bitcast_fusion.kt_ref
  369.8 24.5 %all-to-all-done.5 = bf16[8,72,768]{2,1,0:T(8,128)(2,1)} async-done(((bf16[8,72,768]{2,1,0:T(8,128)(2,1)}), bf16[8,72,768]{2,1,0:T(8,128)(2,1)}, u32[]{:S(2)}, u32[]{:S(2)}) %all-to-all-start.5) | async-done | bytes 884768 | tf_op jit(solution)/shard_map/all_to_all | solution.py:343
  394.9 5.5 all-to-all-start.12
  400.4 48.0 %attend_backward.1 = (f32[3,2304,64]{2,1,0:T(8,128)}, bf16[3,2304,96]{2,1,0:T(8,128)(2,1)}, bf16[2304,384]{1,0:T(8,128)(2,1)}) custom-call(bf16[3,2304,256]{2,1,0:T(8,128)(2,1)} %pad_maximum_fusion.4.q_ref, bf16[3,2304,64]{2,1,0:T(8,128)(2,1)} %bitcast.251, f32[3,1,2304]{2,1,0:T(1,128)} %get-tuple-element.55.lse_ref, f32[3,1,2304]{2,1,0:T(1,128)} %reshape.687.delta_ref, ...), custom_call_target="tpu_custom_call" | custom-call | tf_op jit(solution)/shard_map/attend_backward/pallas_call | solution.py:115
  448.4 2.8 fusion.89
  455.8 2.8 fusion.4
  458.6 4.5 copy.284
  463.0 4.6 convert_element_type.245
  467.7 2.3 copy.285
  470.0 8.9 %fusion.87 = (f32[768]{0:T(1024)}, f32[768]{0:T(1024)}, bf16[2304,768]{1,0:T(8,128)(2,1)S(1)}, bf16[2304,768]{1,0:T(8,128)(2,1)}) fusion(f32[2304]{0:T(1024)} %rsqrt.25, f32[2304]{0:T(1024)} %div.120, bf16[8,1,72,768]{3,2,1,0:T(8,128)(2,1)} %bitcast.238, bf16[8,1,72,768]{3,2,1,0:T(8,128)(2,1)} %bitcast.242, bf16[8,1,72,768]{3,2,1,0:T(8,128)(2,1)} %bitcast.246, ...), kind=kOutput, calls=%fused_computation.190 | convolution fusion | flops 2066741760 | bytes 14186496 | tf_op jit(solution)/shard_map/dot_general | solution.py:337
  484.8 3.4 fusion.25
  488.2 3.4 fusion.28
  495.2 5.5 all-to-all-start.7
  500.7 5.8 convolution_convert_fusion.2
  510.5 4.2 all-to-all-start.9
  519.9 9.2 %all-to-all-done.9 = bf16[4,192,576]{2,1,0:T(8,128)(2,1)} async-done(((bf16[4,192,576]{2,1,0:T(8,128)(2,1)}), bf16[4,192,576]{2,1,0:T(8,128)(2,1)}, u32[]{:S(2)}, u32[]{:S(2)}) %all-to-all-start.9) | async-done | bytes 884768 | tf_op jit(solution)/shard_map/all_to_all | solution.py:343
  529.8 5.2 all-to-all-start.8
  536.3 2.3 copy.300
  538.7 2.4 copy.301
  541.0 8.5 %all-to-all-done.8 = f32[32,1,476]{2,1,0:T(1,128)} async-done(((f32[32,1,476]{2,1,0:T(1,128)}), f32[32,1,476]{2,1,0:T(1,128)}, u32[]{:S(2)}, u32[]{:S(2)}) %all-to-all-start.8) | async-done | bytes 60960 | tf_op jit(solution)/shard_map/all_to_all | solution.py:343
  549.5 4.6 all-to-all-start.10
  554.2 2.6 fusion.8
  556.8 2.5 fusion.88
  560.5 22.6 %all-to-all-done.10 = bf16[8,192,288]{1,2,0:T(8,128)(2,1)} async-done(((bf16[8,192,288]{1,2,0:T(8,128)(2,1)}), bf16[8,192,288]{1,2,0:T(8,128)(2,1)}, u32[]{:S(2)}, u32[]{:S(2)}) %all-to-all-start.10) | async-done | bytes 884768 | tf_op jit(solution)/shard_map/all_to_all | solution.py:343
  583.1 3.6 all-to-all-start.6
  598.6 10.5 %all-to-all-done.6 = bf16[8,72,768]{2,1,0:T(8,128)(2,1)S(1)} async-done(((bf16[8,72,768]{2,1,0:T(8,128)(2,1)}), bf16[8,72,768]{2,1,0:T(8,128)(2,1)S(1)}, u32[]{:S(2)}, u32[]{:S(2)}) %all-to-all-start.6) | async-done | bytes 884768 | tf_op jit(solution)/shard_map/all_to_all | solution.py:343
  (304 shorter events, 110.1 us)
Async XLA Ops:
  7.2 64.6 %copy-start = (bf16[95,64]{0,1:T(8,128)(2,1)S(1)}, bf16[95,64]{0,1:T(8,128)(2,1)}, u32[]{:S(2)}) copy-start(bf16[95,64]{0,1:T(8,128)(2,1)} %param.34) | copy-start | bytes 36484
  7.2 7.6 %copy-start.32 = (bf16[192,288]{1,0:T(8,128)(2,1)S(1)}, bf16[192,288]{1,0:T(8,128)(2,1)}, u32[]{:S(2)}) copy-start(bf16[192,288]{1,0:T(8,128)(2,1)} %param.23) | copy-start | bytes 331780
  7.2 7.8 %copy-start.33 = (bf16[192,384]{1,0:T(8,128)(2,1)S(1)}, bf16[192,384]{1,0:T(8,128)(2,1)}, u32[]{:S(2)}) copy-start(bf16[192,384]{1,0:T(8,128)(2,1)} %param.30) | copy-start | bytes 442372
  7.2 7.9 %copy-start.47 = (bf16[192,96]{1,0:T(8,128)(2,1)S(1)}, bf16[192,96]{1,0:T(8,128)(2,1)}, u32[]{:S(2)}) copy-start(bf16[192,96]{1,0:T(8,128)(2,1)} %param.26) | copy-start | bytes 110596
  7.2 8.1 %copy-start.59 = (bf16[192]{0:T(256)(128)(2,1)S(1)}, bf16[192]{0:T(256)(128)(2,1)}, u32[]{:S(2)}) copy-start(bf16[192]{0:T(256)(128)(2,1)} %param.21) | copy-start | bytes 1156
  7.3 8.1 %copy-start.60 = (bf16[192]{0:T(256)(128)(2,1)S(1)}, bf16[192]{0:T(256)(128)(2,1)}, u32[]{:S(2)}) copy-start(bf16[192]{0:T(256)(128)(2,1)} %param.22) | copy-start | bytes 1156
  7.3 8.1 %copy-start.61 = (bf16[192]{0:T(256)(128)(2,1)S(1)}, bf16[192]{0:T(256)(128)(2,1)}, u32[]{:S(2)}) copy-start(bf16[192]{0:T(256)(128)(2,1)} %param.27) | copy-start | bytes 1156
  7.3 8.1 %copy-start.62 = (bf16[192]{0:T(256)(128)(2,1)S(1)}, bf16[192]{0:T(256)(128)(2,1)}, u32[]{:S(2)}) copy-start(bf16[192]{0:T(256)(128)(2,1)} %param.28) | copy-start | bytes 1156
  7.3 8.1 %copy-start.63 = (bf16[192]{0:T(256)(128)(2,1)S(1)}, bf16[192]{0:T(256)(128)(2,1)}, u32[]{:S(2)}) copy-start(bf16[192]{0:T(256)(128)(2,1)} %param.29) | copy-start | bytes 1156
  7.3 8.1 %copy-start.55 = (bf16[768]{0:T(1024)(128)(2,1)S(1)}, bf16[768]{0:T(1024)(128)(2,1)}, u32[]{:S(2)}) copy-start(bf16[768]{0:T(1024)(128)(2,1)} %param.31) | copy-start | bytes 4612
  7.3 8.1 %copy-start.64 = (bf16[192]{0:T(256)(128)(2,1)S(1)}, bf16[192]{0:T(256)(128)(2,1)}, u32[]{:S(2)}) copy-start(bf16[192]{0:T(256)(128)(2,1)} %param.33) | copy-start | bytes 1156
  7.3 13.5 %copy-start.34 = (bf16[768,96]{0,1:T(8,128)(2,1)S(1)}, bf16[768,96]{0,1:T(8,128)(2,1)}, u32[]{:S(2)}) copy-start(bf16[768,96]{0,1:T(8,128)(2,1)} %param.32) | copy-start | bytes 442372
  7.3 55.1 %all-to-all-start = ((bf16[8,72,768]{2,1,0:T(8,128)(2,1)}), bf16[8,72,768]{2,1,0:T(8,128)(2,1)S(1)}, u32[]{:S(2)}, u32[]{:S(2)}) async-start(bf16[8,72,768]{2,1,0:T(8,128)(2,1)} %param.18), calls=%async_computation | async-start | bytes 1769472 | tf_op jit(solution)/shard_map/all_to_all | solution.py:442
  14.8 47.7 %copy-start.67 = (s32[8]{0:T(128)S(1)}, s32[8]{0:T(128)}, u32[]{:S(2)}) copy-start(s32[8]{0:T(128)} %param.20) | copy-start | bytes 100
  14.8 51.5 %copy-start.65 = (bf16[192]{0:T(256)(128)(2,1)S(1)}, bf16[192]{0:T(256)(128)(2,1)}, u32[]{:S(2)}) copy-start(bf16[192]{0:T(256)(128)(2,1)} %param.25) | copy-start | bytes 1156
  14.8 51.5 %copy-start.66 = (bf16[192]{0:T(256)(128)(2,1)S(1)}, bf16[192]{0:T(256)(128)(2,1)}, u32[]{:S(2)}) copy-start(bf16[192]{0:T(256)(128)(2,1)} %param.24) | copy-start | bytes 1156
  14.8 226.7 %all-gather.5.cloned.1.call-start = ((), (), s32[]{:S(2)}) async-start(), calls=%async_computation.15 | async-start | bytes 10948608 | tf_op jit(solution)/shard_map/all_gather | solution.py:529
  20.8 65.6 %copy-start.43 = (bf16[4,1,1920]{2,0,1:T(4,128)(2,1)}, bf16[4,1,1920]{2,0,1:T(4,128)(2,1)S(1)}, u32[]{:S(2)}) copy-start(bf16[4,1,1920]{2,0,1:T(4,128)(2,1)S(1)} %copy.361) | copy-start | bytes 46084
  62.5 192.0 %copy-start.2 = (bf16[8,72,768]{2,1,0:T(8,128)(2,1)}, bf16[8,72,768]{2,1,0:T(8,128)(2,1)S(1)}, u32[]{:S(2)}) copy-start(bf16[8,72,768]{2,1,0:T(8,128)(2,1)S(1)} %all-to-all-done) | copy-start | bytes 2654212
  62.5 11.2 %copy-start.48 = (bf16[95,64]{0,1:T(8,128)(2,1)S(1)}, bf16[95,64]{0,1:T(8,128)(2,1)}, u32[]{:S(2)}) copy-start(bf16[95,64]{0,1:T(8,128)(2,1)} %param.35) | copy-start | bytes 36484
  67.3 2.6 copy-start.35
  67.3 2.6 copy-start.37
  67.3 18.0 %collective-permute-start.1 = (bf16[576,768]{1,0:T(8,128)(2,1)S(1)}, bf16[576,768]{1,0:T(8,128)(2,1)}, u32[]{:S(2)}, u32[]{:S(2)}) collective-permute-start(bf16[576,768]{1,0:T(8,128)(2,1)S(1)} %bitcast.215), channel_id=1, source_target_pairs={{0,2},{1,3},{2,0},{3,1},{4,6},{5,7},{6,4},{7,5},{8,10},{9,11},{10,... | collective-permute-start | bytes 2654216 | tf_op jit(solution)/shard_map/ppermute | solution.py:353
  75.4 16.9 %collective-permute-start = (bf16[576,768]{1,0:T(8,128)(2,1)S(1)}, bf16[576,768]{1,0:T(8,128)(2,1)}, u32[]{:S(2)}, u32[]{:S(2)}) collective-permute-start(bf16[576,768]{1,0:T(8,128)(2,1)S(1)} %bitcast.216), channel_id=1, source_target_pairs={{0,1},{1,0},{2,3},{3,2},{4,5},{5,4},{6,7},{7,6},{8,9},{9,8},{10,11... | collective-permute-start | bytes 2654216 | tf_op jit(solution)/shard_map/ppermute | solution.py:353
  85.3 7.0 %collective-permute-start.2 = (bf16[576,768]{1,0:T(8,128)(2,1)}, bf16[576,768]{1,0:T(8,128)(2,1)}, u32[]{:S(2)}, u32[]{:S(2)}) collective-permute-start(bf16[576,768]{1,0:T(8,128)(2,1)} %collective-permute-done.1), channel_id=1, source_target_pairs={{0,1},{1,0},{2,3},{3,2},{4,5},{5,4},{6,7},{7,6},{8,9},{9,8},{10,11... | collective-permute-start | bytes 2654216 | tf_op jit(solution)/shard_map/ppermute | solution.py:353
  87.1 9.7 %copy-start.44 = (f32[768]{0:T(1024)}, f32[768]{0:T(1024)S(1)}, u32[]{:S(2)}) copy-start(f32[768]{0:T(1024)S(1)} %reshape.728) | copy-start | bytes 9220
  87.2 9.6 %copy-start.49 = (f32[768]{0:T(1024)}, f32[768]{0:T(1024)S(1)}, u32[]{:S(2)}) copy-start(f32[768]{0:T(1024)S(1)} %reshape.729) | copy-start | bytes 9220
  88.6 23.1 %all-to-all-start.1 = ((bf16[4,192,576]{2,1,0:T(8,128)(2,1)}), bf16[4,192,576]{2,1,0:T(8,128)(2,1)S(1)}, u32[]{:S(2)}, u32[]{:S(2)}) async-start(bf16[4,192,576]{2,1,0:T(8,128)(2,1)} %copy.258), calls=%async_computation.1 | async-start | bytes 1966080 | tf_op jit(solution)/shard_map/all_to_all | solution.py:343
  94.5 2.2 copy-start.9
  94.5 2.2 copy-start.10
  94.5 2.2 copy-start.11
  111.8 4.6 copy-start.28
  138.2 5.2 copy-start.15
  145.4 5.8 copy-start.58
  151.2 3.0 copy-start.16
  154.2 3.6 copy-start.23
  154.2 3.6 copy-start.56
  154.2 3.6 copy-start.57
  217.1 40.9 %all-to-all-start.3 = ((bf16[8,72,768]{2,1,0:T(8,128)(2,1)}), bf16[8,72,768]{2,1,0:T(8,128)(2,1)S(1)}, u32[]{:S(2)}, u32[]{:S(2)}) async-start(bf16[8,72,768]{2,1,0:T(8,128)(2,1)} %param.19), calls=%async_computation.3 | async-start | bytes 1769472 | tf_op jit(solution)/shard_map/all_to_all | solution.py:446
  222.7 386.5 %reduce-scatter.2.cloned.1.call-start = ((), (), s32[]{:S(2)}) async-start(), calls=%async_computation.14 | async-start | bytes 10948608 | tf_op jit(solution)/shard_map/reduce_scatter | solution.py:642
  259.0 30.0 %copy-start.29 = (bf16[576,768]{1,0:T(8,128)(2,1)S(1)}, bf16[576,768]{1,0:T(8,128)(2,1)}, u32[]{:S(2)}) copy-start(bf16[576,768]{1,0:T(8,128)(2,1)} %reshape.678) | copy-start | bytes 2654212
  318.3 3.7 copy-start.52
  318.3 19.5 %all-to-all-start.4 = ((bf16[8,1,72,4,192]{4,2,0,1,3:T(8,128)(2,1)}), bf16[8,1,72,4,192]{4,2,0,1,3:T(8,128)(2,1)S(1)}, u32[]{:S(2)}, u32[]{:S(2)}) async-start(bf16[8,1,72,4,192]{4,2,0,1,3:T(8,128)(2,1)} %copy.273), calls=%async_computation.4 | async-start | bytes 2359296 | tf_op jit(solution)/shard_map/all_to_all | solution.py:616
  322.0 17.0 %copy-start.51 = (f32[4,1,768]{2,1,0:T(1,128)S(1)}, f32[4,1,768]{2,1,0:T(1,128)}, u32[]{:S(2)}) copy-start(f32[4,1,768]{2,1,0:T(1,128)} %get-tuple-element.50) | copy-start | bytes 36868
  338.9 17.0 %copy-start.21 = (bf16[2304,192]{1,0:T(8,128)(2,1)S(1)}, bf16[2304,192]{1,0:T(8,128)(2,1)}, u32[]{:S(2)}) copy-start(bf16[2304,192]{1,0:T(8,128)(2,1)} %get-tuple-element.45) | copy-start | bytes 2654212
  351.6 42.6 %all-to-all-start.5 = ((bf16[8,72,768]{2,1,0:T(8,128)(2,1)}), bf16[8,72,768]{2,1,0:T(8,128)(2,1)}, u32[]{:S(2)}, u32[]{:S(2)}) async-start(bf16[8,72,768]{2,1,0:T(8,128)(2,1)} %bitcast.272), calls=%async_computation.5 | async-start | bytes 1769472 | tf_op jit(solution)/shard_map/all_to_all | solution.py:343
  357.5 4.0 copy-start.14
  394.9 100.3 %all-to-all-start.12 = ((f32[8,1,192]{2,1,0:T(1,128)}), f32[8,1,192]{2,1,0:T(1,128)}, u32[]{:S(2)}, u32[]{:S(2)}) async-start(f32[8,1,192]{2,1,0:T(1,128)} %broadcast_in_dim.97), calls=%async_computation.13 | async-start | bytes 16384 | tf_op jit(solution)/shard_map/all_to_all | solution.py:343
  451.2 3.8 copy-start.7
  467.7 2.3 copy-start.45
  467.7 2.3 copy-start.50
  482.4 26.4 %collective-permute-start.3 = (bf16[2,576,768]{2,1,0:T(8,128)(2,1)}, bf16[2,576,768]{2,1,0:T(8,128)(2,1)}, u32[]{:S(2)}, u32[]{:S(2)}) collective-permute-start(bf16[2,576,768]{2,1,0:T(8,128)(2,1)} %pad_maximum_fusion.7), channel_id=1, source_target_pairs={{0,1},{1,0},{2,3},{3,2},{4,5},{5,4},{6,7},{7,6},{8,9},{9,8},{10,11... | collective-permute-start | bytes 5308424 | tf_op jit(solution)/shard_map/ppermute | solution.py:353
  484.8 6.9 %copy-start.26 = (bf16[2304,384]{1,0:T(8,128)(2,1)S(1)}, bf16[2304,384]{1,0:T(8,128)(2,1)}, u32[]{:S(2)}) copy-start(bf16[2304,384]{1,0:T(8,128)(2,1)} %get-tuple-element.59) | copy-start | bytes 5308420
  488.2 3.5 copy-start.20
  495.2 15.3 %all-to-all-start.7 = ((f32[32,1,476]{2,1,0:T(1,128)}), f32[32,1,476]{2,1,0:T(1,128)}, u32[]{:S(2)}, u32[]{:S(2)}) async-start(f32[32,1,476]{2,1,0:T(1,128)} %copy.298), calls=%async_computation.7 | async-start | bytes 131072 | tf_op jit(solution)/shard_map/all_to_all | solution.py:343
  510.5 18.6 %all-to-all-start.9 = ((bf16[4,192,576]{2,1,0:T(8,128)(2,1)}), bf16[4,192,576]{2,1,0:T(8,128)(2,1)}, u32[]{:S(2)}, u32[]{:S(2)}) async-start(bf16[4,192,576]{2,1,0:T(8,128)(2,1)} %bitcast.263), calls=%async_computation.9 | async-start | bytes 1966080 | tf_op jit(solution)/shard_map/all_to_all | solution.py:343
  517.0 37.1 %collective-permute-start.4 = (bf16[576,768]{1,0:T(8,128)(2,1)}, bf16[576,768]{1,0:T(8,128)(2,1)}, u32[]{:S(2)}, u32[]{:S(2)}) collective-permute-start(bf16[576,768]{1,0:T(8,128)(2,1)} %fusion.33), channel_id=1, source_target_pairs={{0,2},{1,3},{2,0},{3,1},{4,6},{5,7},{6,4},{7,5},{8,10},{9,11},{10,... | collective-permute-start | bytes 2654216 | tf_op jit(solution)/shard_map/ppermute | solution.py:353
  529.8 19.7 %all-to-all-start.8 = ((f32[32,1,476]{2,1,0:T(1,128)}), f32[32,1,476]{2,1,0:T(1,128)}, u32[]{:S(2)}, u32[]{:S(2)}) async-start(f32[32,1,476]{2,1,0:T(1,128)} %broadcast_in_dim.95), calls=%async_computation.8 | async-start | bytes 131072 | tf_op jit(solution)/shard_map/all_to_all | solution.py:343
  541.0 13.2 %copy-start.46 = (f32[768]{0:T(1024)S(1)}, f32[768]{0:T(1024)}, u32[]{:S(2)}) copy-start(f32[768]{0:T(1024)} %copy-done.44) | copy-start | bytes 9220
  549.5 33.5 %all-to-all-start.10 = ((bf16[8,192,288]{1,2,0:T(8,128)(2,1)}), bf16[8,192,288]{1,2,0:T(8,128)(2,1)}, u32[]{:S(2)}, u32[]{:S(2)}) async-start(bf16[8,192,288]{1,2,0:T(8,128)(2,1)} %bitcast.256), calls=%async_computation.10 | async-start | bytes 2359296 | tf_op jit(solution)/shard_map/all_to_all | solution.py:343
  554.2 2.6 copy-start.3
  556.8 2.5 copy-start.25
  583.1 26.1 %all-to-all-start.6 = ((bf16[8,72,768]{2,1,0:T(8,128)(2,1)}), bf16[8,72,768]{2,1,0:T(8,128)(2,1)S(1)}, u32[]{:S(2)}, u32[]{:S(2)}) async-start(bf16[8,72,768]{2,1,0:T(8,128)(2,1)} %bitcast.68), calls=%async_computation.6 | async-start | bytes 1769472 | tf_op jit(solution)/shard_map/all_to_all | solution.py:343
  613.4 3.1 copy-start.1
  (22 other events, 28.3 us)
Sparse Core Ops, SparseCore 0:
  62.6 93.5 all-gather.4
  310.2 157.3 reduce-scatter.1

commit v4 on v3

--- a/solution.py
+++ b/solution.py
@@ -462,7 +462,6 @@
         triple_cut.reshape(head_groups, group_width, 3 * group_width), "ha"
     ).reshape(model_width, 3 * group_width)
     tokens32 = tokens_in.astype(f32)
-    cot32 = cot_in.astype(f32)
     slot_index = jnp.arange(local_tokens, dtype=jnp.int32)
     grid_index = (
         slot_index // block_len * head_groups + head_index
@@ -524,6 +523,8 @@
         axis=1,
     )
     k_turn = jnp.concatenate([key_all, expand_all], axis=-1).swapaxes(1, 2)
+    q_aug, cot_in = lax.optimization_barrier((q_aug, cot_in))
+    cot32 = cot_in.astype(f32)
     att_heads, log_sums = attend_forward(q_aug, k_aug, v_aug)
 
     gathered = lax.all_gather(packed, BOTH, axis=0, tiled=False).reshape(
@@ -611,8 +612,10 @@
         )
         proj_bias_grad = jnp.sum(branch_grad.astype(f32), axis=0)
 
-    proj_grad = contract_rows(branch_grad, att_tok).astype(bf16)
     att_grad_tok = jnp.dot(branch_grad, proj_turn, preferred_element_type=f32).astype(bf16)
+    att_grad_tok, branch_turn, up_packed, down_packed = lax.optimization_barrier(
+        (att_grad_tok, branch_grad, up_packed, down_packed)
+    )
     att_grad = lax.all_to_all(
         att_grad_tok.reshape(group_count, 1, block_len, head_groups, group_width),
         "ha",
@@ -620,15 +623,10 @@
         concat_axis=1,
         tiled=True,
     ).reshape(cap_tokens, group_width)
-    att_grad, block_out, early_in = lax.optimization_barrier(
-        (
-            att_grad,
-            block_out,
-            [proj_bias_grad, second_gain_grad, second_shift_grad, down_bias_grad, up_bias_grad],
-        )
-    )
+    att_grad, block_out = lax.optimization_barrier((att_grad, block_out))
     out_back = exchange(block_out.reshape(group_count, block_len, model_width), "ga")
 
+    proj_grad = contract_rows(branch_turn, att_tok).astype(bf16)
     grads_packed = jnp.concatenate(
         [
             up_packed,
@@ -644,28 +642,6 @@
     down_own = grads_own[up_height : up_height + out_cols].T.astype(f32)
     proj_own = grads_own[up_height + out_cols :].reshape(out_cols, group_width).T.astype(f32)
 
-    def reduce_vectors(vectors_in):
-        stacked = jnp.concatenate(
-            [
-                vector.reshape(head_groups, group_count, -1)
-                .transpose(1, 0, 2)
-                .reshape(device_count, -1)
-                for vector in vectors_in
-            ],
-            axis=1,
-        )
-        part = jnp.sum(exchange(stacked[:, None], BOTH), axis=0)
-        own = spread(part, "ga")[:, 0]
-        result = []
-        at = 0
-        for vector in vectors_in:
-            size = vector.shape[0] // device_count
-            result.append(own[:, at : at + size].reshape(-1))
-            at += size
-        return result
-
-    early = reduce_vectors(early_in)
-
     grad_heads = att_grad.reshape(cap_tokens, group_heads, HD)
     delta = (
         jnp.sum(
@@ -675,9 +651,11 @@
         .transpose(1, 0)
         .reshape(group_heads, 1, cap_tokens)
     )
-    delta, out_back = lax.optimization_barrier((delta, out_back))
     query_part, line_sums, key_value_grad = attend_backward(
         q_aug, grad_heads.transpose(1, 0, 2), log_sums, delta, k_aug, value_all, k_turn
+    )
+    query_part, line_sums, key_value_grad, out_back = lax.optimization_barrier(
+        (query_part, line_sums, key_value_grad, out_back)
     )
     lines = line_sums.reshape(group_heads, SMAX, SMAX, 2 * SMAX)
     height_grad = lines[..., :SMAX]
@@ -687,8 +665,6 @@
         + jnp.einsum("hrwj,rjd->hrwd", height_grad, table_h, preferred_element_type=f32)
         + jnp.einsum("hrwj,wjd->hrwd", width_grad, table_w, preferred_element_type=f32)
     ).reshape(group_heads, cap_tokens, HD)
-    h_table_grad = jnp.einsum("hrwj,hrwd->rjd", height_grad, q_grid, preferred_element_type=f32)
-    w_table_grad = jnp.einsum("hrwj,hrwd->wjd", width_grad, q_grid, preferred_element_type=f32)
     mixed_grad = jnp.concatenate(
         [
             query_grad.astype(bf16).transpose(1, 0, 2).reshape(cap_tokens, group_width),
@@ -696,7 +672,13 @@
         ],
         axis=1,
     )
+    triple_part = contract_rows(normed_all, mixed_grad).astype(bf16)
+    mixed_grad, triple_part, height_grad, width_grad = lax.optimization_barrier(
+        (mixed_grad, triple_part, height_grad, width_grad)
+    )
     norm1_wide = contract_cols(mixed_grad, triple_own)
+    h_table_grad = jnp.einsum("hrwj,hrwd->rjd", height_grad, q_grid, preferred_element_type=f32)
+    w_table_grad = jnp.einsum("hrwj,hrwd->wjd", width_grad, q_grid, preferred_element_type=f32)
     norm1_part = (
         norm1_wide.astype(bf16)
         .reshape(group_count, head_groups, block_len, model_width)
@@ -704,7 +686,6 @@
         .reshape(head_groups, local_tokens, model_width)
     )
     norm1_in = scatter_heads(norm1_part)
-    triple_part = contract_rows(normed_all, mixed_grad).astype(bf16)
     triple_rows_grad = (
         exchange(triple_part.reshape(head_groups, group_width, 3 * group_width), "ha")
         .reshape(head_groups, group_width, 3, group_width)
@@ -719,38 +700,45 @@
     first_gain_grad = jnp.sum(norm1_wide * unit, axis=0)
     first_shift_grad = jnp.sum(norm1_wide, axis=0)
     mixed_float = mixed_grad.astype(f32)
-    zero_wide = jnp.zeros((model_width,), f32)
-
-    def own_slot(vector):
-        return lax.dynamic_update_slice(zero_wide, vector, (head_index * group_width,))
-
-    query_bias_grad = own_slot(jnp.sum(mixed_float[:, :group_width], axis=0))
-    value_bias_grad = own_slot(jnp.sum(mixed_float[:, 2 * group_width :], axis=0))
     height_rel = jnp.einsum("qkj,qkd->jd", matrix, h_table_grad, precision=exact_mode)
     width_rel = jnp.einsum("qkj,qkd->jd", matrix, w_table_grad, precision=exact_mode)
     rel_flat = jnp.concatenate([height_rel, width_rel]).reshape(-1)
     rel_size = rel_flat.shape[0]
-    chunk = -(-rel_size // device_count)
-    rel_flat = jnp.pad(rel_flat, (0, chunk * device_count - rel_size))
-    piece = model_width // device_count
-    last_vectors = [first_gain_grad, first_shift_grad, query_bias_grad, value_bias_grad]
-    stacked = jnp.concatenate(
+    grouped = [
+        first_gain_grad,
+        first_shift_grad,
+        proj_bias_grad,
+        second_gain_grad,
+        second_shift_grad,
+        down_bias_grad,
+        up_bias_grad,
+    ]
+    small = jnp.concatenate(
+        [vector.reshape(head_groups, -1) for vector in grouped]
+        + [rel_flat.reshape(head_groups, -1)],
+        axis=1,
+    )
+    small = small + swap(small, 1)
+    small = small + swap(small, 2)
+    own_part = lax.dynamic_index_in_dim(small, head_index, 0, False)
+    own_size = own_part.shape[0] - rel_size // head_groups
+    last_part = jnp.concatenate(
         [
-            vector.reshape(head_groups, group_count, piece)
-            .transpose(1, 0, 2)
-            .reshape(device_count, piece)
-            for vector in last_vectors
+            own_part[:own_size],
+            jnp.sum(mixed_float[:, :group_width], axis=0),
+            jnp.sum(mixed_float[:, 2 * group_width :], axis=0),
+            small[:, own_size:].reshape(-1),
         ]
-        + [rel_flat.reshape(device_count, chunk)],
-        axis=1,
-    )
-    last_part = jnp.sum(exchange(stacked[:, None], BOTH), axis=0)
-    last_all = spread(last_part, BOTH)[:, 0].reshape(group_count, head_groups, -1)
-    last_here = lax.dynamic_index_in_dim(last_all, head_index, 1, False)
-    late = [last_here[:, i * piece : (i + 1) * piece].reshape(-1) for i in range(4)]
-    rel_sum = (
-        last_all[:, :, 4 * piece :].reshape(-1)[:rel_size].reshape(2, 2 * SMAX - 1, HD)
-    )
+    )
+    last_size = last_part.shape[0]
+    last_part = jnp.pad(last_part, (0, -last_size % 128)).reshape(-1, 128)
+    last_sum = jnp.sum(spread(last_part, "ga"), axis=0).reshape(-1)[:last_size]
+    rel_sum = last_sum[last_size - rel_size :].reshape(2, 2 * SMAX - 1, HD)
+    late = []
+    at = 0
+    for size in [group_width] * 6 + [hidden_width // head_groups] + [group_width] * 2:
+        late.append(last_sum[at : at + size])
+        at += size
 
     norm1_value, norm1_pull = jax.vjp(lambda tokens: layer_norm(tokens, gain32, shift32), tokens32)
     input_grad = (mid_total + norm1_pull(norm1_in)[0]).astype(bf16)
@@ -761,16 +749,16 @@
         late[0],
         late[1],
         triple_grad,
+        late[7],
+        late[8],
+        proj_own,
         late[2],
         late[3],
-        proj_own,
-        early[0],
-        early[1],
-        early[2],
+        late[4],
         up_own,
-        early[4],
+        late[6],
         down_own,
-        early[3],
+        late[5],
         rel_sum[0],
         rel_sum[1],
     )

time: 632 us -> 587 us (0.929)
  waiting for transfers between devices: 112 us -> 73.6 us
  blocking collectives: 77.2 us -> 62.8 us
  local copies, waits for them, and re-layouts: 129 us -> 139 us
  starting transfers between devices: 56.8 us -> 50 us
    all_to_all x8 -> x6, waiting for transfers between devices: 86.6 us -> 45.9 us  [exchange(): return lax.all_to_all(values, axis, split_axis=0, concat_axis=0, tiled=True)]
    all_to_all x2 -> x1, blocking collectives: 31.1 us -> 18.3 us  [local(): lax.all_to_all(att_grad_tok.reshape(group_count, 1, block_len, head_group...]
    all_to_all x1, waiting for transfers between devices: 15.7 us -> 3.43 us  [local(): lax.all_to_all(att_heads.reshape(group_count, head_groups, block_len, 1,...]
    all_to_all x8 -> x6, starting transfers between devices: 36.6 us -> 26.7 us  [exchange(): return lax.all_to_all(values, axis, split_axis=0, concat_axis=0, tiled=True)]
    ppermute x5 -> x7, waiting for transfers between devices: 9.9 us -> 18.5 us  [swap(): return lax.ppermute(values, 'ha', pairs)]
    unnamed x148 -> x142, local copies, waits for them, and re-layouts: 17.1 us -> 13.9 us
  transfers between devices with their start and end apart: 18 -> 18, of which waited for: 8 -> 10; matrix products, arithmetic and copies ran while one was open for 33% -> 35% of each run, Pallas kernels for 14% -> 15%
where the time goes in v4:
time: 587 us; the launch traced here: 576 us
  local copies, waits for them, and re-layouts  139 us (24%)
  Pallas kernels  116 us (20%)
  waiting for transfers between devices  73.6 us (13%)
  other arithmetic  72.9 us (12%)
  blocking collectives  62.8 us (11%)
  starting transfers between devices  50 us (9%)
  matrix products  45.8 us (8%)
  between operations  16.1 us (3%)
    pallas_call x1, Pallas kernels, attend_backward(): pl.pallas_call(backward_kernel, grid=(tokens // TBLK,), in_specs=[pl.Bloc...  48.1 us
    all_to_all x6, waiting for transfers between devices, exchange(): return lax.all_to_all(values, axis, split_axis=0, concat_axis=0, tiled=True)  45.9 us
    all_gather x1, blocking collectives, local(): triple_rows = lax.all_gather(qkv_weight, 'ga', axis=1, tiled=True)  39.3 us
    pallas_call x1, Pallas kernels, attend_forward(): pl.pallas_call(forward_kernel, grid=(tokens // TBLK,), in_specs=[pl.Block...  37.7 us
    pallas_call x1, Pallas kernels, feed_forward(): pl.pallas_call(feed_kernel, grid=(steps,), in_specs=[whole(tokens, width)...  30.2 us
    all_to_all x6, starting transfers between devices, exchange(): return lax.all_to_all(values, axis, split_axis=0, concat_axis=0, tiled=True)  26.7 us
    ppermute x7, waiting for transfers between devices, swap(): return lax.ppermute(values, 'ha', pairs)  18.5 us
    all_to_all x1, blocking collectives, local(): lax.all_to_all(att_grad_tok.reshape(group_count, 1, block_len, head_group...  18.3 us
  transfers between devices with their start and end apart: 18, of which 10 were waited for; matrix products, arithmetic and copies ran while one was open for 35% of the time, Pallas kernels for 15%

profile of v4, /device:TPU:0, one launch (start us, length us, event | category | flops | bytes accessed | tf_op | source)
XLA Modules:
  0.0 576.3 jit_solution(11071802012357809997)
XLA Ops:
  7.3 7.5 %all-to-all-start = ((bf16[8,72,768]{2,1,0:T(8,128)(2,1)}), bf16[8,72,768]{2,1,0:T(8,128)(2,1)S(1)}, u32[]{:S(2)}, u32[]{:S(2)}) async-start(bf16[8,72,768]{2,1,0:T(8,128)(2,1)} %param.18), calls=%async_computation | async-start | bytes 1769472 | tf_op jit(solution)/shard_map/all_to_all | solution.py:442
  17.3 5.2 all-gather.2
  23.3 39.3 %all_gather.15 = bf16[192,2304]{0,1:T(8,128)(2,1)S(1)} all-gather(bf16[192,288]{0,1:T(8,128)(2,1)S(1)} %copy.316), channel_id=1, replica_groups=mesh['ga'=8,'ha'=4] {'ga'}, dimensions={1}, use_global_device_ids=true | all-gather | bytes 995328 | tf_op jit(solution)/shard_map/all_gather | solution.py:424
  76.2 10.1 %collective-permute-done.1 = bf16[576,768]{1,0:T(8,128)(2,1)} collective-permute-done((bf16[576,768]{1,0:T(8,128)(2,1)S(1)}, bf16[576,768]{1,0:T(8,128)(2,1)}, u32[]{:S(2)}, u32[]{:S(2)}) %collective-permute-start.1) | collective-permute-done | bytes 884768 | tf_op jit(solution)/shard_map/ppermute | solution.py:353
  90.8 4.2 all-to-all-start.1
  100.1 3.1 add_convert_fusion.1
  103.2 8.6 %all-to-all-done.1 = bf16[4,192,576]{2,1,0:T(8,128)(2,1)} async-done(((bf16[4,192,576]{2,1,0:T(8,128)(2,1)}), bf16[4,192,576]{2,1,0:T(8,128)(2,1)}, u32[]{:S(2)}, u32[]{:S(2)}) %all-to-all-start.1) | async-done | bytes 884768 | tf_op jit(solution)/shard_map/all_to_all | solution.py:343
  111.7 5.7 all-to-all-start.2
  117.5 5.6 add_convert_fusion.2
  125.2 5.2 reshape_squeeze.3
  130.4 5.2 copy.324
  135.6 4.6 copy.322
  140.3 2.7 fusion.82
  148.7 2.6 copy.327
  151.4 2.8 fusion.1
  154.2 3.5 pad_maximum_fusion.4.q_ref
  157.7 5.8 %all-to-all-done.2 = bf16[8,72,768]{2,1,0:T(8,128)(2,1)} async-done(((bf16[8,72,768]{2,1,0:T(8,128)(2,1)}), bf16[8,72,768]{2,1,0:T(8,128)(2,1)}, u32[]{:S(2)}, u32[]{:S(2)}) %all-to-all-start.2) | async-done | bytes 884768 | tf_op jit(solution)/shard_map/all_to_all | solution.py:446
  167.8 6.0 %copy.328.k_ref = bf16[3,2304,256]{2,1,0:T(8,128)(2,1)} copy(bf16[3,2304,256]{1,2,0:T(8,128)(2,1)} %pad_maximum_fusion.5) | data formatting | bytes 7077888 | tf_op jit(solution)/shard_map/concatenate | solution.py:516
  173.8 2.4 maximum_maximum_fusion.v_ref
  176.2 37.7 %attend_forward.1 = (bf16[2304,192]{1,0:T(8,128)(2,1)}, f32[3,1,2304]{2,1,0:T(1,128)}) custom-call(bf16[3,2304,256]{2,1,0:T(8,128)(2,1)} %pad_maximum_fusion.4.q_ref, bf16[3,2304,256]{2,1,0:T(8,128)(2,1)} %copy.328.k_ref, bf16[3,80,2304]{2,1,0:T(8,128)(2,1)} %maximum_maximum_fusion.v_ref), custom_call_target="tpu_custom_call" | custom-call | tf_op jit(solution)/shard_map/attend_forward/pallas_call | solution.py:51
  214.0 2.4 copy.329
  216.4 4.3 all-to-all-start.3
  233.1 3.4 all-to-all-done.3
  236.5 3.2 copy.330
  239.8 3.2 reshape.601
  242.9 2.4 slice.148
  245.3 3.9 reshape.603
  249.2 2.8 copy.331
  252.1 3.8 reshape.604
  255.9 3.6 convert_add_fusion.mid_ref
  259.5 30.2 %feed_forward.1 = (bf16[576,768]{1,0:T(8,128)(2,1)}, f32[576,768]{1,0:T(8,128)}, bf16[576,768]{1,0:T(8,128)(2,1)}, f32[4,768]{1,0:T(4,128)}, f32[4,1,768]{2,1,0:...) custom-call(f32[576,768]{1,0:T(8,128)} %convert_add_fusion.mid_ref, ...), custom_call_target="tpu_custom_call" | custom-call | tf_op jit(solution)/shard_map/feed_forward/pallas_call | solution.py:263
  289.7 2.5 convolution_convert_fusion.1
  294.4 4.4 reshape.624
  298.8 2.8 copy.403
  301.6 4.1 reshape.625
  305.7 9.6 %pad_maximum_fusion = bf16[8,4,216,768]{3,2,1,0:T(8,128)(2,1)} fusion(bf16[8,4,24,768]{3,2,1,0:T(8,128)(2,1)} %reshape.625, bf16[8,4,96,768]{3,2,1,0:T(8,128)(2,1)} %get-tuple-element.79, bf16[8,4,96,768]{3,2,1,0:T(8,128)(2,1)} %get-tuple-element.78), kind=kLoop, calls=%fused_computation | loop fusion | flops 31850496 | bytes 21233664 | tf_op jit(solution)/shard_map/concatenate | solution.py:630
  318.8 18.3 %all_to_all.78 = bf16[8,1,72,4,192]{4,2,0,1,3:T(8,128)(2,1)S(1)} all-to-all(bf16[8,1,72,4,192]{4,2,0,1,3:T(8,128)(2,1)S(1)} %copy.335), channel_id=1, replica_groups=mesh['ga'=8,'ha'=4] {'ha'}, dimensions={3} | all-to-all | bytes 1769472 | tf_op jit(solution)/shard_map/all_to_all | solution.py:619
  338.2 4.4 all-to-all-start.5
  342.6 2.5 copy.339
  348.9 3.3 maximum_bitcast_fusion.kt_ref
  352.2 2.8 add_convert_fusion
  357.3 2.6 copy.338
  362.4 48.1 %attend_backward.1 = (f32[3,2304,64]{2,1,0:T(8,128)}, bf16[3,2304,96]{2,1,0:T(8,128)(2,1)}, bf16[2304,384]{1,0:T(8,128)(2,1)}) custom-call(bf16[3,2304,256]{2,1,0:T(8,128)(2,1)} %pad_maximum_fusion.4.q_ref, bf16[3,2304,64]{2,1,0:T(8,128)(2,1)} %bitcast.242, f32[3,1,2304]{2,1,0:T(1,128)} %get-tuple-element.62.lse_ref, f32[3,1,2304]{2,1,0:T(1,128)} %reshape.609.delta_ref, ...), custom_call_target="tpu_custom_call" | custom-call | tf_op jit(solution)/shard_map/attend_backward/pallas_call | solution.py:115
  410.5 2.8 fusion.79
  418.7 2.8 fusion.4
  421.5 4.5 copy.346
  425.9 4.7 convert_element_type.245
  432.9 3.3 pad_maximum_fusion.6
  436.3 6.5 %convolution_convert_fusion.2 = bf16[768,576]{0,1:T(8,128)(2,1)} fusion(bf16[2304,768]{1,0:T(8,128)(2,1)S(1)} %copy-done.23, bf16[2304,384]{1,0:T(8,128)(2,1)} %get-tuple-element.71, bf16[2304,192]{1,0:T(8,128)(2,1)S(1)} %copy-done.22), kind=kOutput, calls=%fused_computation.51 | convolution fusion | flops 2044182528 | bytes 7077888 | tf_op jit(solution)/shard_map/dot_general | solution.py:331
  442.7 5.8 %fusion.77 = (f32[768]{0:T(1024)}, f32[768]{0:T(1024)}, bf16[2304,768]{1,0:T(8,128)(2,1)S(1)}) fusion(f32[2304]{0:T(1024)S(1)} %copy-done.41, f32[2304]{0:T(1024)S(1)} %copy-done.43, bf16[8,1,72,768]{3,2,1,0:T(8,128)(2,1)S(1)} %bitcast.218, bf16[8,1,72,768]{3,2,1,0:T(8,128)(2,1)S(1)} %bitcast.223, bf16[8,1,72,768]{3,2,1,0:T(8,128)(2,1)S(1)} %bitcast.228, ...), kind=kOutput, calls=%fused_computation.185 | convolution fusion | flops 2056124928 | bytes 10641408 | tf_op jit(solution)/shard_map/dot_general | solution.py:337
  456.3 2.6 copy.357
  458.9 4.3 all-to-all-start.8
  466.0 3.4 fusion.19
  469.5 3.4 fusion.22
  477.3 2.4 collective-permute-done.6
  484.0 5.9 %all-to-all-start.7 = ((f32[8,113,128]{2,1,0:T(8,128)}), f32[8,113,128]{2,1,0:T(8,128)}, u32[]{:S(2)}, u32[]{:S(2)}) async-start(f32[8,113,128]{2,1,0:T(8,128)} %broadcast_in_dim.81), calls=%async_computation.7 | async-start | bytes 983040 | tf_op jit(solution)/shard_map/all_to_all | solution.py:343
  498.8 4.7 all-to-all-done.7
  503.5 4.4 all-to-all-start.9
  507.9 5.4 collective-permute-done.4
  513.3 2.5 fusion.8
  515.9 2.5 fusion.78
  519.5 16.5 %all-to-all-done.9 = bf16[8,192,288]{1,2,0:T(8,128)(2,1)} async-done(((bf16[8,192,288]{1,2,0:T(8,128)(2,1)}), bf16[8,192,288]{1,2,0:T(8,128)(2,1)}, u32[]{:S(2)}, u32[]{:S(2)}) %all-to-all-start.9) | async-done | bytes 884768 | tf_op jit(solution)/shard_map/all_to_all | solution.py:343
  536.1 3.6 all-to-all-start.6
  545.8 16.1 %all-to-all-done.6 = bf16[8,72,768]{2,1,0:T(8,128)(2,1)S(1)} async-done(((bf16[8,72,768]{2,1,0:T(8,128)(2,1)}), bf16[8,72,768]{2,1,0:T(8,128)(2,1)S(1)}, u32[]{:S(2)}, u32[]{:S(2)}) %all-to-all-start.6) | async-done | bytes 884768 | tf_op jit(solution)/shard_map/all_to_all | solution.py:343
  (273 shorter events, 115.6 us)
Async XLA Ops:
  7.2 65.3 %copy-start = (bf16[95,64]{0,1:T(8,128)(2,1)S(1)}, bf16[95,64]{0,1:T(8,128)(2,1)}, u32[]{:S(2)}) copy-start(bf16[95,64]{0,1:T(8,128)(2,1)} %param.34) | copy-start | bytes 36484
  7.2 9.7 %copy-start.44 = (bf16[192,96]{1,0:T(8,128)(2,1)S(1)}, bf16[192,96]{1,0:T(8,128)(2,1)}, u32[]{:S(2)}) copy-start(bf16[192,96]{1,0:T(8,128)(2,1)} %param.26) | copy-start | bytes 110596
  7.2 9.9 %copy-start.56 = (bf16[192]{0:T(256)(128)(2,1)S(1)}, bf16[192]{0:T(256)(128)(2,1)}, u32[]{:S(2)}) copy-start(bf16[192]{0:T(256)(128)(2,1)} %param.21) | copy-start | bytes 1156
  7.2 9.9 %copy-start.57 = (bf16[192]{0:T(256)(128)(2,1)S(1)}, bf16[192]{0:T(256)(128)(2,1)}, u32[]{:S(2)}) copy-start(bf16[192]{0:T(256)(128)(2,1)} %param.22) | copy-start | bytes 1156
  7.2 9.9 %copy-start.58 = (bf16[192]{0:T(256)(128)(2,1)S(1)}, bf16[192]{0:T(256)(128)(2,1)}, u32[]{:S(2)}) copy-start(bf16[192]{0:T(256)(128)(2,1)} %param.27) | copy-start | bytes 1156
  7.2 9.9 %copy-start.59 = (bf16[192]{0:T(256)(128)(2,1)S(1)}, bf16[192]{0:T(256)(128)(2,1)}, u32[]{:S(2)}) copy-start(bf16[192]{0:T(256)(128)(2,1)} %param.28) | copy-start | bytes 1156
  7.3 9.9 %copy-start.60 = (bf16[192]{0:T(256)(128)(2,1)S(1)}, bf16[192]{0:T(256)(128)(2,1)}, u32[]{:S(2)}) copy-start(bf16[192]{0:T(256)(128)(2,1)} %param.29) | copy-start | bytes 1156
  7.3 9.9 %copy-start.55 = (bf16[768]{0:T(1024)(128)(2,1)S(1)}, bf16[768]{0:T(1024)(128)(2,1)}, u32[]{:S(2)}) copy-start(bf16[768]{0:T(1024)(128)(2,1)} %param.31) | copy-start | bytes 4612
  7.3 9.9 %copy-start.61 = (bf16[192]{0:T(256)(128)(2,1)S(1)}, bf16[192]{0:T(256)(128)(2,1)}, u32[]{:S(2)}) copy-start(bf16[192]{0:T(256)(128)(2,1)} %param.33) | copy-start | bytes 1156
  7.3 15.3 %copy-start.29 = (bf16[768,96]{0,1:T(8,128)(2,1)S(1)}, bf16[768,96]{0,1:T(8,128)(2,1)}, u32[]{:S(2)}) copy-start(bf16[768,96]{0,1:T(8,128)(2,1)} %param.32) | copy-start | bytes 442372
  7.3 55.3 %all-to-all-start = ((bf16[8,72,768]{2,1,0:T(8,128)(2,1)}), bf16[8,72,768]{2,1,0:T(8,128)(2,1)S(1)}, u32[]{:S(2)}, u32[]{:S(2)}) async-start(bf16[8,72,768]{2,1,0:T(8,128)(2,1)} %param.18), calls=%async_computation | async-start | bytes 1769472 | tf_op jit(solution)/shard_map/all_to_all | solution.py:442
  14.8 47.9 %copy-start.65 = (s32[8]{0:T(128)S(1)}, s32[8]{0:T(128)}, u32[]{:S(2)}) copy-start(s32[8]{0:T(128)} %param.20) | copy-start | bytes 100
  14.8 51.6 %copy-start.62 = (bf16[192]{0:T(256)(128)(2,1)S(1)}, bf16[192]{0:T(256)(128)(2,1)}, u32[]{:S(2)}) copy-start(bf16[192]{0:T(256)(128)(2,1)} %param.25) | copy-start | bytes 1156
  14.8 51.6 %copy-start.63 = (bf16[192]{0:T(256)(128)(2,1)S(1)}, bf16[192]{0:T(256)(128)(2,1)}, u32[]{:S(2)}) copy-start(bf16[192]{0:T(256)(128)(2,1)} %param.24) | copy-start | bytes 1156
  14.8 228.2 %all-gather.5.cloned.1.call-start = ((), (), s32[]{:S(2)}) async-start(), calls=%async_computation.12 | async-start | bytes 10948608 | tf_op jit(solution)/shard_map/all_gather | solution.py:530
  22.6 64.8 %copy-start.40 = (bf16[4,1,1920]{2,0,1:T(4,128)(2,1)}, bf16[4,1,1920]{2,0,1:T(4,128)(2,1)S(1)}, u32[]{:S(2)}) copy-start(bf16[4,1,1920]{2,0,1:T(4,128)(2,1)S(1)} %copy.404) | copy-start | bytes 46084
  23.3 51.0 %copy-start.47 = (bf16[95,64]{0,1:T(8,128)(2,1)S(1)}, bf16[95,64]{0,1:T(8,128)(2,1)}, u32[]{:S(2)}) copy-start(bf16[95,64]{0,1:T(8,128)(2,1)} %param.35) | copy-start | bytes 36484
  62.6 193.2 %copy-start.2 = (bf16[8,72,768]{2,1,0:T(8,128)(2,1)}, bf16[8,72,768]{2,1,0:T(8,128)(2,1)S(1)}, u32[]{:S(2)}) copy-start(bf16[8,72,768]{2,1,0:T(8,128)(2,1)S(1)} %all-to-all-done) | copy-start | bytes 2654212
  68.0 2.6 copy-start.32
  68.1 2.6 copy-start.34
  68.1 18.2 %collective-permute-start.1 = (bf16[576,768]{1,0:T(8,128)(2,1)S(1)}, bf16[576,768]{1,0:T(8,128)(2,1)}, u32[]{:S(2)}, u32[]{:S(2)}) collective-permute-start(bf16[576,768]{1,0:T(8,128)(2,1)S(1)} %bitcast.202), channel_id=1, source_target_pairs={{0,2},{1,3},{2,0},{3,1},{4,6},{5,7},{6,4},{7,5},{8,10},{9,11},{10,... | collective-permute-start | bytes 2654216 | tf_op jit(solution)/shard_map/ppermute | solution.py:353
  76.2 18.8 %collective-permute-start = (bf16[576,768]{1,0:T(8,128)(2,1)S(1)}, bf16[576,768]{1,0:T(8,128)(2,1)}, u32[]{:S(2)}, u32[]{:S(2)}) collective-permute-start(bf16[576,768]{1,0:T(8,128)(2,1)S(1)} %bitcast.203), channel_id=1, source_target_pairs={{0,1},{1,0},{2,3},{3,2},{4,5},{5,4},{6,7},{7,6},{8,9},{9,8},{10,11... | collective-permute-start | bytes 2654216 | tf_op jit(solution)/shard_map/ppermute | solution.py:353
  86.3 8.7 %collective-permute-start.2 = (bf16[576,768]{1,0:T(8,128)(2,1)}, bf16[576,768]{1,0:T(8,128)(2,1)}, u32[]{:S(2)}, u32[]{:S(2)}) collective-permute-start(bf16[576,768]{1,0:T(8,128)(2,1)} %collective-permute-done.1), channel_id=1, source_target_pairs={{0,1},{1,0},{2,3},{3,2},{4,5},{5,4},{6,7},{7,6},{8,9},{9,8},{10,11... | collective-permute-start | bytes 2654216 | tf_op jit(solution)/shard_map/ppermute | solution.py:353
  90.8 21.0 %all-to-all-start.1 = ((bf16[4,192,576]{2,1,0:T(8,128)(2,1)}), bf16[4,192,576]{2,1,0:T(8,128)(2,1)}, u32[]{:S(2)}, u32[]{:S(2)}) async-start(bf16[4,192,576]{2,1,0:T(8,128)(2,1)} %copy.320), calls=%async_computation.1 | async-start | bytes 1966080 | tf_op jit(solution)/shard_map/all_to_all | solution.py:343
  111.7 51.8 %all-to-all-start.2 = ((bf16[8,72,768]{2,1,0:T(8,128)(2,1)}), bf16[8,72,768]{2,1,0:T(8,128)(2,1)}, u32[]{:S(2)}, u32[]{:S(2)}) async-start(bf16[8,72,768]{2,1,0:T(8,128)(2,1)} %param.19), calls=%async_computation.2 | async-start | bytes 1769472 | tf_op jit(solution)/shard_map/all_to_all | solution.py:446
  151.4 2.8 copy-start.18
  216.4 20.2 %all-to-all-start.3 = ((bf16[8,4,72,1,192]{4,2,0,3,1:T(8,128)(2,1)}), bf16[8,4,72,1,192]{4,2,0,3,1:T(8,128)(2,1)}, u32[]{:S(2)}, u32[]{:S(2)}) async-start(bf16[8,4,72,1,192]{4,2,0,3,1:T(8,128)(2,1)} %copy.329), calls=%async_computation.3 | async-start | bytes 2359296 | tf_op jit(solution)/shard_map/all_to_all | solution.py:540
  220.6 341.3 %reduce-scatter.2.cloned.1.call-start = ((), (), s32[]{:S(2)}) async-start(), calls=%async_computation.11 | async-start | bytes 10948608 | tf_op jit(solution)/shard_map/reduce_scatter | solution.py:640
  289.7 2.6 copy-start.27
  289.7 2.6 copy-start.64
  338.2 9.0 %copy-start.25 = (bf16[3,2304,64]{1,2,0:T(8,128)(2,1)S(1)}, bf16[3,2304,64]{1,2,0:T(8,128)(2,1)}, u32[]{:S(2)}) copy-start(bf16[3,2304,64]{1,2,0:T(8,128)(2,1)} %get-tuple-element.221) | copy-start | bytes 2654212
  338.2 72.3 %all-to-all-start.5 = ((bf16[8,72,768]{2,1,0:T(8,128)(2,1)}), bf16[8,72,768]{2,1,0:T(8,128)(2,1)}, u32[]{:S(2)}, u32[]{:S(2)}) async-start(bf16[8,72,768]{2,1,0:T(8,128)(2,1)} %bitcast.259), calls=%async_computation.5 | async-start | bytes 1769472 | tf_op jit(solution)/shard_map/all_to_all | solution.py:343
  348.8 3.3 copy-start.6
  348.8 3.3 copy-start.31
  348.8 3.3 copy-start.41
  348.8 3.3 copy-start.42
  348.9 3.3 copy-start.46
  432.9 3.3 copy-start.22
  432.9 3.3 copy-start.23
  436.2 6.5 %copy-start.14 = (bf16[2304,576]{1,0:T(8,128)(2,1)}, bf16[2304,576]{1,0:T(8,128)(2,1)S(1)}, u32[]{:S(2)}) copy-start(bf16[2304,576]{1,0:T(8,128)(2,1)S(1)} %pad_maximum_fusion.6) | copy-start | bytes 7962628
  436.3 6.5 %copy-start.43 = (f32[2304]{0:T(1024)S(1)}, f32[2304]{0:T(1024)}, u32[]{:S(2)}) copy-start(f32[2304]{0:T(1024)} %div.115) | copy-start | bytes 27652
  448.8 2.4 copy-start.7
  448.9 2.3 copy-start.52
  451.2 11.9 %copy-start.10 = (bf16[3,48,48,64]{3,2,0,1:T(8,128)(2,1)S(1)}, bf16[3,48,48,64]{3,2,0,1:T(8,128)(2,1)}, u32[]{:S(2)}) copy-start(bf16[3,48,48,64]{3,2,0,1:T(8,128)(2,1)} %copy.322) | copy-start | bytes 2654212
  451.2 11.9 %copy-start.17 = (bf16[3,48,48,48]{3,2,0,1:T(8,128)(2,1)S(1)}, bf16[3,48,48,48]{3,2,0,1:T(8,128)(2,1)}, u32[]{:S(2)}) copy-start(bf16[3,48,48,48]{3,2,0,1:T(8,128)(2,1)} %copy.374) | copy-start | bytes 1990660
  451.2 29.4 %collective-permute-start.3 = (bf16[2,576,768]{2,1,0:T(8,128)(2,1)}, bf16[2,576,768]{2,1,0:T(8,128)(2,1)}, u32[]{:S(2)}, u32[]{:S(2)}) collective-permute-start(bf16[2,576,768]{2,1,0:T(8,128)(2,1)} %pad_maximum_fusion.7), channel_id=1, source_target_pairs={{0,1},{1,0},{2,3},{3,2},{4,5},{5,4},{6,7},{7,6},{8,9},{9,8},{10,11... | collective-permute-start | bytes 5308424 | tf_op jit(solution)/shard_map/ppermute | solution.py:353
  458.9 23.4 %all-to-all-start.8 = ((bf16[4,192,576]{2,1,0:T(8,128)(2,1)}), bf16[4,192,576]{2,1,0:T(8,128)(2,1)}, u32[]{:S(2)}, u32[]{:S(2)}) async-start(bf16[4,192,576]{2,1,0:T(8,128)(2,1)} %bitcast.253), calls=%async_computation.8 | async-start | bytes 1966080 | tf_op jit(solution)/shard_map/all_to_all | solution.py:343
  469.4 3.8 copy-start.54
  469.4 3.9 copy-start.53
  469.5 4.0 copy-start.48
  469.5 4.0 copy-start.49
  469.5 3.9 copy-start.50
  469.5 3.9 copy-start.51
  469.5 4.5 copy-start.15
  473.5 1.4 collective-permute-start.5
  475.0 4.7 collective-permute-start.6
  484.0 19.5 %all-to-all-start.7 = ((f32[8,113,128]{2,1,0:T(8,128)}), f32[8,113,128]{2,1,0:T(8,128)}, u32[]{:S(2)}, u32[]{:S(2)}) async-start(f32[8,113,128]{2,1,0:T(8,128)} %broadcast_in_dim.81), calls=%async_computation.7 | async-start | bytes 983040 | tf_op jit(solution)/shard_map/all_to_all | solution.py:343
  489.9 4.0 copy-start.3
  492.2 21.1 %collective-permute-start.4 = (bf16[576,768]{1,0:T(8,128)(2,1)}, bf16[576,768]{1,0:T(8,128)(2,1)}, u32[]{:S(2)}, u32[]{:S(2)}) collective-permute-start(bf16[576,768]{1,0:T(8,128)(2,1)} %fusion.27), channel_id=1, source_target_pairs={{0,2},{1,3},{2,0},{3,1},{4,6},{5,7},{6,4},{7,5},{8,10},{9,11},{10,... | collective-permute-start | bytes 2654216 | tf_op jit(solution)/shard_map/ppermute | solution.py:353
  503.5 32.6 %all-to-all-start.9 = ((bf16[8,192,288]{1,2,0:T(8,128)(2,1)}), bf16[8,192,288]{1,2,0:T(8,128)(2,1)}, u32[]{:S(2)}, u32[]{:S(2)}) async-start(bf16[8,192,288]{1,2,0:T(8,128)(2,1)} %bitcast.247), calls=%async_computation.9 | async-start | bytes 2359296 | tf_op jit(solution)/shard_map/all_to_all | solution.py:343
  507.9 7.9 %copy-start.4 = (bf16[8,72,768]{2,1,0:T(8,128)(2,1)S(1)}, bf16[8,72,768]{2,1,0:T(8,128)(2,1)}, u32[]{:S(2)}) copy-start(bf16[8,72,768]{2,1,0:T(8,128)(2,1)} %copy-done.2) | copy-start | bytes 2654212
  515.9 2.5 copy-start.26
  536.1 25.9 %all-to-all-start.6 = ((bf16[8,72,768]{2,1,0:T(8,128)(2,1)}), bf16[8,72,768]{2,1,0:T(8,128)(2,1)S(1)}, u32[]{:S(2)}, u32[]{:S(2)}) async-start(bf16[8,72,768]{2,1,0:T(8,128)(2,1)} %bitcast.68), calls=%async_computation.6 | async-start | bytes 1769472 | tf_op jit(solution)/shard_map/all_to_all | solution.py:343
  563.9 5.4 copy-start.1
  (20 other events, 27.9 us)
Sparse Core Ops, SparseCore 0:
  62.8 107.6 all-gather.4
  315.4 139.9 reduce-scatter.1

commit v5 on v4

--- a/solution.py
+++ b/solution.py
@@ -30,114 +30,166 @@
     return lax.dot_general(left, right, NT, preferred_element_type=jnp.float32)
 
 
-def forward_kernel(q_ref, k_ref, v_ref, out_ref, lse_ref):
-    heads = q_ref.shape[0]
-    dim = 64
+def query_rows(mixed_ref, rel_ref, head):
+    start = pl.multiple_of(pl.program_id(0) * TBLK, TBLK)
+    rows = mixed_ref[pl.ds(start, TBLK), head * HD : (head + 1) * HD]
+    return jnp.concatenate([rows * jnp.asarray(HD**-0.5, rows.dtype), rel_ref[head]], axis=1)
+
+
+def forward_kernel(mixed_ref, rel_ref, lines_ref, out_ref, lse_ref, k_ref, v_ref):
+    heads = rel_ref.shape[0]
+    tokens = mixed_ref.shape[0]
+    width = heads * HD
+    bf16 = jnp.bfloat16
+
+    @pl.when(pl.program_id(0) == 0)
+    def _():
+        lines = lines_ref[...]
+        for h in range(heads):
+            keys = mixed_ref[:, width + h * HD : width + (h + 1) * HD]
+            values = mixed_ref[:, 2 * width + h * HD : 2 * width + (h + 1) * HD]
+            k_ref[h] = jnp.concatenate([keys, lines, lines], axis=1)
+            v_ref[h, :HD] = values.T
+            v_ref[h, HD:] = jnp.ones((16, tokens), bf16)
+
     outs = []
     for h in range(heads):
-        scores = mm_nt(k_ref[h], q_ref[h])
+        scores = mm_nt(k_ref[h], query_rows(mixed_ref, rel_ref, h))
         top = jnp.max(scores, axis=0, keepdims=True)
-        expo = jnp.exp(scores - top).astype(jnp.bfloat16)
+        expo = jnp.exp(scores - top).astype(bf16)
         mixed = mm(v_ref[h], expo)
-        total = mixed[dim : dim + 1]
-        outs.append((mixed[:dim] / total).T.astype(jnp.bfloat16))
+        total = mixed[HD : HD + 1]
+        outs.append((mixed[:HD] / total).T.astype(bf16))
         lse_ref[h] = top + jnp.log(total)
     out_ref[...] = jnp.concatenate(outs, axis=1)
 
 
-def attend_forward(q_aug, k_aug, v_aug):
-    heads, tokens, depth = q_aug.shape
-    dim = 64
+def attend_forward(mixed, rel, lines):
+    heads, tokens, depth = rel.shape
     return pl.pallas_call(
         forward_kernel,
         grid=(tokens // TBLK,),
         in_specs=[
+            pl.BlockSpec(mixed.shape, lambda t: (0, 0)),
             pl.BlockSpec((heads, TBLK, depth), lambda t: (0, t, 0)),
-            pl.BlockSpec((heads, tokens, depth), lambda t: (0, 0, 0)),
-            pl.BlockSpec((heads, v_aug.shape[1], tokens), lambda t: (0, 0, 0)),
+            pl.BlockSpec(lines.shape, lambda t: (0, 0)),
         ],
         out_specs=[
-            pl.BlockSpec((TBLK, heads * dim), lambda t: (t, 0)),
+            pl.BlockSpec((TBLK, heads * HD), lambda t: (t, 0)),
             pl.BlockSpec((heads, 1, TBLK), lambda t: (0, 0, t)),
         ],
         out_shape=[
-            jax.ShapeDtypeStruct((tokens, heads * dim), jnp.bfloat16),
+            jax.ShapeDtypeStruct((tokens, heads * HD), jnp.bfloat16),
             jax.ShapeDtypeStruct((heads, 1, tokens), jnp.float32),
+        ],
+        scratch_shapes=[
+            pltpu.VMEM((heads, tokens, HD + depth), jnp.bfloat16),
+            pltpu.VMEM((heads, HD + 16, tokens), jnp.bfloat16),
         ],
         name="attend_forward",
         compiler_params=pltpu.CompilerParams(dimension_semantics=("arbitrary",)),
-    )(q_aug, k_aug, v_aug)
+    )(mixed, rel, lines)
 
 
 def backward_kernel(
-    q_ref, g_ref, lse_ref, delta_ref, k_ref, v_ref, kt_ref, dq_ref, line_ref, out_ref, dkv_ref
+    mixed_ref,
+    rel_ref,
+    lines_ref,
+    g_ref,
+    att_ref,
+    lse_ref,
+    dq_ref,
+    rows_ref,
+    cols_ref,
+    out_ref,
+    dkv_ref,
+    k_ref,
+    v_ref,
+    kt_ref,
 ):
-    heads, tokens, depth = k_ref.shape
-    dim = 64
-    blk = q_ref.shape[1]
+    heads = rel_ref.shape[0]
+    tokens = mixed_ref.shape[0]
+    width = heads * HD
+    bf16 = jnp.bfloat16
+    f32 = jnp.float32
 
     @pl.when(pl.program_id(0) == 0)
     def _():
         dkv_ref[...] = jnp.zeros_like(dkv_ref)
-
+        lines = lines_ref[...]
+        for h in range(heads):
+            keys = mixed_ref[:, width + h * HD : width + (h + 1) * HD]
+            k_ref[h] = jnp.concatenate([keys, lines, lines], axis=1)
+            v_ref[h] = mixed_ref[:, 2 * width + h * HD : 2 * width + (h + 1) * HD]
+            kt_ref[h] = jnp.concatenate([keys, lines], axis=1).T
+
+    zero = jnp.zeros((TBLK, HD), bf16)
+    query_grads = []
     for h in range(heads):
-        q_here = q_ref[h]
-        g_here = g_ref[h]
-        zero = jnp.zeros((blk, dim), jnp.bfloat16)
+        q_here = query_rows(mixed_ref, rel_ref, h)
+        g_here = g_ref[:, h * HD : (h + 1) * HD]
+        weighed = g_here.astype(f32) * att_ref[:, h * HD : (h + 1) * HD].astype(f32)
+        delta = jnp.sum(weighed.T, axis=0, keepdims=True)
         g_wide = jnp.concatenate([g_here, zero], axis=1)
-        q_wide = jnp.concatenate([zero, q_here[:, :dim]], axis=1)
+        q_wide = jnp.concatenate([zero, q_here[:, :HD]], axis=1)
         lse = lse_ref[h]
-        delta = delta_ref[h]
         total = None
         for c in range(tokens // UBLK):
             span = pl.ds(c * UBLK, UBLK)
             scores = mm_nt(k_ref[h, span, :], q_here)
             probs = jnp.exp(scores - lse)
             pgrad = mm_nt(v_ref[h, span, :], g_here)
-            sgrad = (probs * (pgrad - delta)).astype(jnp.bfloat16)
-            dkv_ref[h, span, :] += mm(probs.astype(jnp.bfloat16), g_wide) + mm(sgrad, q_wide)
+            sgrad = (probs * (pgrad - delta)).astype(bf16)
+            dkv_ref[h, span, :] += mm(probs.astype(bf16), g_wide) + mm(sgrad, q_wide)
             part = mm(kt_ref[h, :, span], sgrad)
             total = part if total is None else total + part
-        dq_ref[h] = total[:dim].T
-        line_ref[h] = total[dim:].T.astype(jnp.bfloat16)
+        query_grads.append(total[:HD].T)
+        rows_ref[h] = total[HD : HD + SMAX].T.astype(bf16)
+        cols_ref[h] = total[HD + SMAX :].T.astype(bf16)
+    dq_ref[...] = HD**-0.5 * jnp.concatenate(query_grads, axis=1)
 
     @pl.when(pl.program_id(0) == pl.num_programs(0) - 1)
     def _():
-        keys = [dkv_ref[h, :, dim:] for h in range(heads)]
-        values = [dkv_ref[h, :, :dim] for h in range(heads)]
-        out_ref[...] = jnp.concatenate(keys + values, axis=1).astype(jnp.bfloat16)
-
-
-def attend_backward(q_aug, grads, lse, delta, k_aug, values, k_turn):
-    heads, tokens, depth = q_aug.shape
-    dim = 64
-    lines = k_turn.shape[1] - dim
+        keys = [dkv_ref[h, :, HD:] for h in range(heads)]
+        values = [dkv_ref[h, :, :HD] for h in range(heads)]
+        out_ref[...] = jnp.concatenate(keys + values, axis=1).astype(bf16)
+
+
+def attend_backward(mixed, rel, lines, grads, attended, lse):
+    heads, tokens, depth = rel.shape
+    width = heads * HD
     return pl.pallas_call(
         backward_kernel,
         grid=(tokens // TBLK,),
         in_specs=[
+            pl.BlockSpec(mixed.shape, lambda t: (0, 0)),
             pl.BlockSpec((heads, TBLK, depth), lambda t: (0, t, 0)),
-            pl.BlockSpec((heads, TBLK, dim), lambda t: (0, t, 0)),
+            pl.BlockSpec(lines.shape, lambda t: (0, 0)),
+            pl.BlockSpec((TBLK, width), lambda t: (t, 0)),
+            pl.BlockSpec((TBLK, width), lambda t: (t, 0)),
             pl.BlockSpec((heads, 1, TBLK), lambda t: (0, 0, t)),
-            pl.BlockSpec((heads, 1, TBLK), lambda t: (0, 0, t)),
-            pl.BlockSpec((heads, tokens, depth), lambda t: (0, 0, 0)),
-            pl.BlockSpec((heads, tokens, dim), lambda t: (0, 0, 0)),
-            pl.BlockSpec((heads, dim + lines, tokens), lambda t: (0, 0, 0)),
         ],
         out_specs=[
-            pl.BlockSpec((heads, TBLK, dim), lambda t: (0, t, 0)),
-            pl.BlockSpec((heads, TBLK, lines), lambda t: (0, t, 0)),
-            pl.BlockSpec((tokens, 2 * heads * dim), lambda t: (0, 0)),
-        ],
-        scratch_shapes=[pltpu.VMEM((heads, tokens, 2 * dim), jnp.float32)],
+            pl.BlockSpec((TBLK, width), lambda t: (t, 0)),
+            pl.BlockSpec((heads, TBLK, SMAX), lambda t: (0, t, 0)),
+            pl.BlockSpec((heads, TBLK, SMAX), lambda t: (0, t, 0)),
+            pl.BlockSpec((tokens, 2 * width), lambda t: (0, 0)),
+        ],
         out_shape=[
-            jax.ShapeDtypeStruct((heads, tokens, dim), jnp.float32),
-            jax.ShapeDtypeStruct((heads, tokens, lines), jnp.bfloat16),
-            jax.ShapeDtypeStruct((tokens, 2 * heads * dim), jnp.bfloat16),
+            jax.ShapeDtypeStruct((tokens, width), jnp.float32),
+            jax.ShapeDtypeStruct((heads, tokens, SMAX), jnp.bfloat16),
+            jax.ShapeDtypeStruct((heads, tokens, SMAX), jnp.bfloat16),
+            jax.ShapeDtypeStruct((tokens, 2 * width), jnp.bfloat16),
+        ],
+        scratch_shapes=[
+            pltpu.VMEM((heads, tokens, 2 * HD), jnp.float32),
+            pltpu.VMEM((heads, tokens, HD + depth), jnp.bfloat16),
+            pltpu.VMEM((heads, tokens, HD), jnp.bfloat16),
+            pltpu.VMEM((heads, HD + 2 * SMAX, tokens), jnp.bfloat16),
         ],
         name="attend_backward",
         compiler_params=pltpu.CompilerParams(dimension_semantics=("arbitrary",)),
-    )(q_aug, grads, lse, delta, k_aug, values, k_turn)
+    )(mixed, rel, lines, grads, attended, lse)
 
 
 def norm_parts(values):
@@ -353,13 +405,17 @@
     return lax.ppermute(values, "ha", pairs)
 
 
-def gather_heads(values):
+def gather_heads(values, beside):
     me = lax.axis_index("ha")
     far = swap(values, 2)
     near = swap(values, 1)
+    far, near, beside = lax.optimization_barrier((far, near, beside))
     corner = swap(far, 1)
     blocks = jnp.stack([values, near, far, corner])
-    return [lax.dynamic_index_in_dim(blocks, jnp.bitwise_xor(me, i), 0, False) for i in range(4)]
+    ordered = [
+        lax.dynamic_index_in_dim(blocks, jnp.bitwise_xor(me, i), 0, False) for i in range(4)
+    ]
+    return ordered, beside
 
 
 def scatter_heads(parts):
@@ -486,9 +542,10 @@
         bf16
     )
 
+    blocks_all, triple_own = gather_heads(tokens_in, triple_own)
     tokens_all = (
         jnp.stack(
-            [block.reshape(group_count, block_len, model_width) for block in gather_heads(tokens_in)],
+            [block.reshape(group_count, block_len, model_width) for block in blocks_all],
             axis=1,
         )
         .reshape(cap_tokens, model_width)
@@ -499,10 +556,9 @@
     normed_all = layer_norm(tokens_all, gain32, shift32).astype(bf16)
     bias_own = jnp.concatenate([query_bias, jnp.zeros_like(query_bias), value_bias]).astype(f32)
     mixed = (jnp.dot(normed_all, triple_own, preferred_element_type=f32) + bias_own).astype(bf16)
-    by_head = mixed.reshape(cap_tokens, 3, group_heads, HD).transpose(1, 2, 0, 3)
-    q_all, key_all, value_all = by_head[0], by_head[1], by_head[2]
-
-    q_grid = q_all.reshape(group_heads, SMAX, SMAX, HD)
+    q_grid = (
+        mixed[:, :group_width].reshape(SMAX, SMAX, group_heads, HD).transpose(2, 0, 1, 3)
+    )
     rel_h = jnp.einsum("hrwd,rkd->hrwk", q_grid, table_h, preferred_element_type=f32)
     rel_w = jnp.einsum("hrwd,wkd->hrwk", q_grid, table_w, preferred_element_type=f32)
     rel_both = jnp.concatenate([rel_h, rel_w], axis=-1).reshape(
@@ -511,25 +567,14 @@
     rel_upper = lax.reduce_precision(rel_both, 8, 7)
     rel_lower = jnp.where(line_valid, rel_both - rel_upper, 0.0).astype(bf16)
     rel_upper = jnp.where(line_valid, rel_upper, -1e30).astype(bf16)
-    q_aug = jnp.concatenate([q_all * jnp.asarray(HD**-0.5, bf16), rel_upper, rel_lower], axis=-1)
-    expand_all = jnp.broadcast_to(expand, (group_heads,) + expand.shape)
-    k_aug = jnp.concatenate([key_all, expand_all, expand_all], axis=-1)
-    v_aug = jnp.concatenate(
-        [
-            value_all.swapaxes(1, 2),
-            jnp.ones((group_heads, 1, cap_tokens), bf16),
-            jnp.zeros((group_heads, 15, cap_tokens), bf16),
-        ],
-        axis=1,
-    )
-    k_turn = jnp.concatenate([key_all, expand_all], axis=-1).swapaxes(1, 2)
-    q_aug, cot_in = lax.optimization_barrier((q_aug, cot_in))
+    rel_split = jnp.concatenate([rel_upper, rel_lower], axis=-1)
+    rel_split, cot_in = lax.optimization_barrier((rel_split, cot_in))
     cot32 = cot_in.astype(f32)
-    att_heads, log_sums = attend_forward(q_aug, k_aug, v_aug)
-
-    gathered = lax.all_gather(packed, BOTH, axis=0, tiled=False).reshape(
-        group_count, head_groups, pack_rows, model_width
-    )
+    att_heads, log_sums = attend_forward(mixed, rel_split, expand)
+
+    gathered = lax.all_gather(packed, BOTH, axis=0, tiled=False)
+    att_heads, gathered = lax.optimization_barrier((att_heads, gathered))
+    gathered = gathered.reshape(group_count, head_groups, pack_rows, model_width)
     proj_turn = (
         gathered[:, :, up_height + out_cols :]
         .reshape(group_count, head_groups, out_cols, group_width)
@@ -642,32 +687,26 @@
     down_own = grads_own[up_height : up_height + out_cols].T.astype(f32)
     proj_own = grads_own[up_height + out_cols :].reshape(out_cols, group_width).T.astype(f32)
 
-    grad_heads = att_grad.reshape(cap_tokens, group_heads, HD)
-    delta = (
-        jnp.sum(
-            grad_heads.astype(f32) * att_heads.reshape(cap_tokens, group_heads, HD).astype(f32),
-            axis=-1,
-        )
-        .transpose(1, 0)
-        .reshape(group_heads, 1, cap_tokens)
-    )
-    query_part, line_sums, key_value_grad = attend_backward(
-        q_aug, grad_heads.transpose(1, 0, 2), log_sums, delta, k_aug, value_all, k_turn
-    )
-    query_part, line_sums, key_value_grad, out_back = lax.optimization_barrier(
-        (query_part, line_sums, key_value_grad, out_back)
-    )
-    lines = line_sums.reshape(group_heads, SMAX, SMAX, 2 * SMAX)
-    height_grad = lines[..., :SMAX]
-    width_grad = lines[..., SMAX:]
+    query_part, height_grad, width_grad, key_value_grad = attend_backward(
+        mixed, rel_split, expand, att_grad, att_heads, log_sums
+    )
+    query_part, height_grad, width_grad, key_value_grad, out_back = lax.optimization_barrier(
+        (query_part, height_grad, width_grad, key_value_grad, out_back)
+    )
+    height_grad = height_grad.reshape(group_heads, SMAX, SMAX, SMAX)
+    width_grad = width_grad.reshape(group_heads, SMAX, SMAX, SMAX)
     query_grad = (
-        HD**-0.5 * query_part.reshape(group_heads, SMAX, SMAX, HD)
-        + jnp.einsum("hrwj,rjd->hrwd", height_grad, table_h, preferred_element_type=f32)
-        + jnp.einsum("hrwj,wjd->hrwd", width_grad, table_w, preferred_element_type=f32)
-    ).reshape(group_heads, cap_tokens, HD)
+        query_part
+        + jnp.einsum(
+            "hrwj,rjd->rwhd", height_grad, table_h, preferred_element_type=f32
+        ).reshape(cap_tokens, group_width)
+        + jnp.einsum(
+            "hrwj,wjd->rwhd", width_grad, table_w, preferred_element_type=f32
+        ).reshape(cap_tokens, group_width)
+    )
     mixed_grad = jnp.concatenate(
         [
-            query_grad.astype(bf16).transpose(1, 0, 2).reshape(cap_tokens, group_width),
+            query_grad.astype(bf16),
             key_value_grad,
         ],
         axis=1,

time: 587 us -> 526 us (0.90)
  local copies, waits for them, and re-layouts: 139 us -> 98.1 us
  other arithmetic: 72.9 us -> 58.2 us
  matrix products: 45.8 us -> 37.8 us
    reshape x3 -> x6, local copies, waits for them, and re-layouts: 5.53 us -> 27.3 us  [the longest x4 20.7 us: local(): query_grad = query_part + jnp.einsum('hrwj,rjd->rwhd', height_grad, table...]
    all_to_all x6, waiting for transfers between devices: 45.9 us -> 62.4 us  [exchange(): return lax.all_to_all(values, axis, split_axis=0, concat_axis=0, tiled=True)]
    another operation x3 -> x0, local copies, waits for them, and re-layouts: 15 us -> none  [local(): q_grid = q_all.reshape(group_heads, SMAX, SMAX, HD)]
    convert_element_type x3 -> x0, local copies, waits for them, and re-layouts: 11.7 us -> none  [the longest x2 9.12 us: local(): query_grad.astype(bf16).transpose(1, 0, 2).reshape(cap_tokens, group_width)]
    ppermute x7, waiting for transfers between devices: 18.5 us -> 8.75 us  [swap(): return lax.ppermute(values, 'ha', pairs)]
    concatenate x3 -> x0, local copies, waits for them, and re-layouts: 7.12 us -> none  [the longest x1 5.95 us: local(): k_aug = jnp.concatenate([key_all, expand_all, expand_all], axis=-1)]
    concatenate x4 -> x2, other arithmetic: 11.3 us -> 4.71 us  [the longest x1 3.34 us: local(): rel_split = jnp.concatenate([rel_upper, rel_lower], axis=-1)]
    unnamed x142 -> x152, local copies, waits for them, and re-layouts: 13.9 us -> 9.48 us
  transfers between devices with their start and end apart: 18 -> 18, of which waited for: 10 -> 7; matrix products, arithmetic and copies ran while one was open for 35% -> 28% of each run, Pallas kernels for 15% -> 17%
where the time goes in v5:
time: 526 us; the launch traced here: 516 us
  Pallas kernels  120 us (23%)
  local copies, waits for them, and re-layouts  98.1 us (19%)
  waiting for transfers between devices  71.2 us (14%)
  blocking collectives  65.4 us (12%)
  other arithmetic  58.2 us (11%)
  starting transfers between devices  49.3 us (9%)
  matrix products  37.8 us (7%)
  between operations  16.5 us (3%)
    all_to_all x6, waiting for transfers between devices, exchange(): return lax.all_to_all(values, axis, split_axis=0, concat_axis=0, tiled=True)  62.4 us
    pallas_call x1, Pallas kernels, attend_backward(): pl.pallas_call(backward_kernel, grid=(tokens // TBLK,), in_specs=[pl.Bloc...  49.6 us
    all_gather x1, blocking collectives, local(): triple_rows = lax.all_gather(qkv_weight, 'ga', axis=1, tiled=True)  40.9 us
    pallas_call x1, Pallas kernels, attend_forward(): pl.pallas_call(forward_kernel, grid=(tokens // TBLK,), in_specs=[pl.Block...  39.7 us
    pallas_call x1, Pallas kernels, feed_forward(): pl.pallas_call(feed_kernel, grid=(steps,), in_specs=[whole(tokens, width)...  30.2 us
    all_to_all x6, starting transfers between devices, exchange(): return lax.all_to_all(values, axis, split_axis=0, concat_axis=0, tiled=True)  27.7 us
    reshape x4, local copies, waits for them, and re-layouts, local(): query_grad = query_part + jnp.einsum('hrwj,rjd->rwhd', height_grad, table...  20.7 us
    all_to_all x1, blocking collectives, local(): lax.all_to_all(att_grad_tok.reshape(group_count, 1, block_len, head_group...  19.2 us
  transfers between devices with their start and end apart: 18, of which 7 were waited for; matrix products, arithmetic and copies ran while one was open for 28% of the time, Pallas kernels for 17%

profile of v5, /device:TPU:0, one launch (start us, length us, event | category | flops | bytes accessed | tf_op | source)
XLA Modules:
  0.0 516.0 jit_solution(3788253270312800833)
XLA Ops:
  7.3 7.5 %all-to-all-start = ((bf16[8,72,768]{2,1,0:T(8,128)(2,1)}), bf16[8,72,768]{2,1,0:T(8,128)(2,1)S(1)}, u32[]{:S(2)}, u32[]{:S(2)}) async-start(bf16[8,72,768]{2,1,0:T(8,128)(2,1)} %param.18), calls=%async_computation | async-start | bytes 1769472 | tf_op jit(solution)/shard_map/all_to_all | solution.py:498
  15.6 5.2 %all-gather.2 = bf16[4,1,1920]{2,1,0:T(2,128)(2,1)S(1)} all-gather(bf16[1,1,1920]{2,1,0:T(2,128)(2,1)S(1)} %reshape.541), channel_id=2, replica_groups=mesh['ga'=8,'ha'=4] {'ha'}, dimensions={0}, use_global_device_ids=true | all-gather | bytes 19200 | tf_op jit(solution)/shard_map/all_gather | solution.py:497
  21.6 40.9 %all_gather.15 = bf16[192,2304]{0,1:T(8,128)(2,1)S(1)} all-gather(bf16[192,288]{0,1:T(8,128)(2,1)S(1)} %copy.284), channel_id=1, replica_groups=mesh['ga'=8,'ha'=4] {'ga'}, dimensions={1}, use_global_device_ids=true | all-gather | bytes 995328 | tf_op jit(solution)/shard_map/all_gather | solution.py:480
  70.7 3.5 all-to-all-start.1
  75.6 1.8 fusion.30
  77.4 1.9 convolution_convert_fusion.3
  79.3 24.7 %all-to-all-done.1 = bf16[4,192,576]{2,1,0:T(8,128)(2,1)S(1)} async-done(((bf16[4,192,576]{2,1,0:T(8,128)(2,1)}), bf16[4,192,576]{2,1,0:T(8,128)(2,1)S(1)}, u32[]{:S(2)}, u32[]{:S(2)}) %all-to-all-start.1) | async-done | bytes 884768 | tf_op jit(solution)/shard_map/all_to_all | solution.py:395
  104.0 4.2 all-to-all-start.2
  108.3 2.2 fusion.36.lines_ref
  116.2 2.4 multiply_reduce_fusion.1
  119.3 3.5 add_convert_fusion
  122.8 3.1 add_convert_fusion.1.mixed_ref
  128.7 4.3 reshape.555
  133.1 2.1 copy.335
  141.0 3.3 pad_maximum_fusion.4.rel_ref
  144.3 39.7 %attend_forward.1 = (bf16[2304,192]{1,0:T(8,128)(2,1)}, f32[3,1,2304]{2,1,0:T(1,128)}) custom-call(bf16[2304,576]{1,0:T(8,128)(2,1)} %copy-done.6, bf16[3,2304,192]{2,1,0:T(8,128)(2,1)} %pad_maximum_fusion.4.rel_ref, bf16[2304,96]{1,0:T(8,128)(2,1)} %fusion.36.lines_ref), custom_call_target="tpu_custom_call" | custom-call | tf_op jit(solution)/shard_map/attend_forward/pallas_call | solution.py:69
  184.0 2.4 copy.297
  186.4 4.3 all-to-all-start.3
  191.4 1.8 fusion.61.mask_ref
  195.6 2.4 slice.130
  198.0 3.9 reshape.506
  201.9 2.8 copy.299
  204.7 3.8 reshape.507
  208.5 3.2 copy.298
  211.7 3.2 reshape.504
  214.9 3.6 convert_add_fusion.mid_ref
  218.5 30.2 %feed_forward.1 = (bf16[576,768]{1,0:T(8,128)(2,1)}, f32[576,768]{1,0:T(8,128)}, bf16[576,768]{1,0:T(8,128)(2,1)}, f32[4,768]{1,0:T(4,128)}, f32[4,1,768]{2,1,0:...) custom-call(f32[576,768]{1,0:T(8,128)} %convert_add_fusion.mid_ref, ...), custom_call_target="tpu_custom_call" | custom-call | tf_op jit(solution)/shard_map/feed_forward/pallas_call | solution.py:315
  248.7 2.5 convolution_convert_fusion.1
  251.3 2.1 convolution_convert_fusion
  253.4 4.4 reshape.527
  257.8 2.9 copy.384
  260.7 3.9 reshape.528
  264.6 9.6 %pad_maximum_fusion = bf16[8,4,216,768]{3,2,1,0:T(8,128)(2,1)} fusion(bf16[8,4,24,768]{3,2,1,0:T(8,128)(2,1)} %reshape.528, bf16[8,4,96,768]{3,2,1,0:T(8,128)(2,1)} %get-tuple-element.93, bf16[8,4,96,768]{3,2,1,0:T(8,128)(2,1)} %get-tuple-element.92), kind=kLoop, calls=%fused_computation | loop fusion | flops 31850496 | bytes 21233664 | tf_op jit(solution)/shard_map/concatenate | solution.py:675
  274.2 2.0 reshape.509
  277.7 19.2 %all_to_all.78 = bf16[8,1,72,4,192]{4,2,0,1,3:T(8,128)(2,1)S(1)} all-to-all(bf16[8,1,72,4,192]{4,2,0,1,3:T(8,128)(2,1)S(1)} %copy.303), channel_id=1, replica_groups=mesh['ga'=8,'ha'=4] {'ha'}, dimensions={3} | all-to-all | bytes 1769472 | tf_op jit(solution)/shard_map/all_to_all | solution.py:664
  298.0 6.1 %all-to-all-start.5 = ((bf16[8,72,768]{2,1,0:T(8,128)(2,1)}), bf16[8,72,768]{2,1,0:T(8,128)(2,1)S(1)}, u32[]{:S(2)}, u32[]{:S(2)}) async-start(bf16[8,72,768]{2,1,0:T(8,128)(2,1)} %bitcast.228), calls=%async_computation.5 | async-start | bytes 1769472 | tf_op jit(solution)/shard_map/all_to_all | solution.py:395
  304.1 49.6 %attend_backward.1 = (f32[2304,192]{1,0:T(8,128)}, bf16[3,2304,48]{2,1,0:T(8,128)(2,1)}, bf16[3,2304,48]{2,1,0:T(8,128)(2,1)}, bf16[2304,384]{1,0:T(8,128)(2,1)}) custom-call(bf16[2304,576]{1,0:T(8,128)(2,1)} %copy-done.6, bf16[3,2304,192]{2,1,0:T(8,128)(2,1)} %pad_maximum_fusion.4.rel_ref, bf16[2304,96]{1,0:T(8,128)(2,1)} %fusion.36.lines_ref, ...), custom_call_target="tpu_custom_call" | custom-call | tf_op jit(solution)/shard_map/attend_backward/pallas_call | solution.py:161
  353.8 2.3 copy.308
  357.2 4.0 copy.337
  361.2 6.5 %reshape.557 = f32[2304,192]{1,0:T(8,128)} reshape(f32[48,48,3,64]{3,2,1,0:T(4,128)} %copy.337) | data formatting | bytes 3538944 | tf_op jit(solution)/shard_map/reshape | solution.py:705
  367.7 2.1 convolution_bitcast_fusion
  369.8 4.0 copy.336
  373.8 6.2 %reshape.556 = f32[2304,192]{1,0:T(8,128)} reshape(f32[48,48,3,64]{3,2,1,0:T(4,128)} %copy.336) | data formatting | bytes 3538944 | tf_op jit(solution)/shard_map/reshape | solution.py:702
  380.0 3.6 add_convert_fusion.2
  385.7 3.0 convolution_convert_fusion.2
  389.0 4.1 fusion.92
  398.2 4.5 all-to-all-start.8
  402.7 2.6 fusion.27
  406.3 3.4 fusion.37
  409.7 3.4 fusion.40
  415.2 1.9 collective-permute-start.6
  417.5 2.9 collective-permute-done.6
  424.7 5.5 %all-to-all-start.7 = ((f32[8,113,128]{2,1,0:T(8,128)}), f32[8,113,128]{2,1,0:T(8,128)}, u32[]{:S(2)}, u32[]{:S(2)}) async-start(f32[8,113,128]{2,1,0:T(8,128)} %broadcast_in_dim.63), calls=%async_computation.7 | async-start | bytes 983040 | tf_op jit(solution)/shard_map/all_to_all | solution.py:395
  430.3 2.3 fusion.45
  434.3 2.3 copy.321
  436.6 2.4 copy.322
  439.0 4.9 all-to-all-done.7
  443.9 4.5 all-to-all-start.9
  448.5 5.3 %collective-permute-done.4 = bf16[576,768]{1,0:T(8,128)(2,1)} collective-permute-done((bf16[576,768]{1,0:T(8,128)(2,1)}, bf16[576,768]{1,0:T(8,128)(2,1)}, u32[]{:S(2)}, u32[]{:S(2)}) %collective-permute-start.4) | collective-permute-done | bytes 884768 | tf_op jit(solution)/shard_map/ppermute | solution.py:405
  453.8 2.5 fusion.7
  456.4 2.5 fusion.93
  460.0 16.7 %all-to-all-done.9 = bf16[8,192,288]{1,2,0:T(8,128)(2,1)} async-done(((bf16[8,192,288]{1,2,0:T(8,128)(2,1)}), bf16[8,192,288]{1,2,0:T(8,128)(2,1)}, u32[]{:S(2)}, u32[]{:S(2)}) %all-to-all-start.9) | async-done | bytes 884768 | tf_op jit(solution)/shard_map/all_to_all | solution.py:395
  476.7 3.6 all-to-all-start.6
  486.4 16.1 %all-to-all-done.6 = bf16[8,72,768]{2,1,0:T(8,128)(2,1)S(1)} async-done(((bf16[8,72,768]{2,1,0:T(8,128)(2,1)}), bf16[8,72,768]{2,1,0:T(8,128)(2,1)S(1)}, u32[]{:S(2)}, u32[]{:S(2)}) %all-to-all-start.6) | async-done | bytes 884768 | tf_op jit(solution)/shard_map/all_to_all | solution.py:395
  (265 shorter events, 61.9 us)
Async XLA Ops:
  7.2 68.4 %copy-start = (bf16[95,64]{0,1:T(8,128)(2,1)S(1)}, bf16[95,64]{0,1:T(8,128)(2,1)}, u32[]{:S(2)}) copy-start(bf16[95,64]{0,1:T(8,128)(2,1)} %param.34) | copy-start | bytes 36484
  7.2 7.6 %copy-start.34 = (bf16[192,288]{1,0:T(8,128)(2,1)S(1)}, bf16[192,288]{1,0:T(8,128)(2,1)}, u32[]{:S(2)}) copy-start(bf16[192,288]{1,0:T(8,128)(2,1)} %param.23) | copy-start | bytes 331780
  7.2 7.8 %copy-start.35 = (bf16[192,384]{1,0:T(8,128)(2,1)S(1)}, bf16[192,384]{1,0:T(8,128)(2,1)}, u32[]{:S(2)}) copy-start(bf16[192,384]{1,0:T(8,128)(2,1)} %param.30) | copy-start | bytes 442372
  7.2 7.9 %copy-start.49 = (bf16[192,96]{1,0:T(8,128)(2,1)S(1)}, bf16[192,96]{1,0:T(8,128)(2,1)}, u32[]{:S(2)}) copy-start(bf16[192,96]{1,0:T(8,128)(2,1)} %param.26) | copy-start | bytes 110596
  7.2 8.1 %copy-start.61 = (bf16[192]{0:T(256)(128)(2,1)S(1)}, bf16[192]{0:T(256)(128)(2,1)}, u32[]{:S(2)}) copy-start(bf16[192]{0:T(256)(128)(2,1)} %param.21) | copy-start | bytes 1156
  7.3 8.1 %copy-start.62 = (bf16[192]{0:T(256)(128)(2,1)S(1)}, bf16[192]{0:T(256)(128)(2,1)}, u32[]{:S(2)}) copy-start(bf16[192]{0:T(256)(128)(2,1)} %param.22) | copy-start | bytes 1156
  7.3 8.1 %copy-start.63 = (bf16[192]{0:T(256)(128)(2,1)S(1)}, bf16[192]{0:T(256)(128)(2,1)}, u32[]{:S(2)}) copy-start(bf16[192]{0:T(256)(128)(2,1)} %param.27) | copy-start | bytes 1156
  7.3 8.1 %copy-start.64 = (bf16[192]{0:T(256)(128)(2,1)S(1)}, bf16[192]{0:T(256)(128)(2,1)}, u32[]{:S(2)}) copy-start(bf16[192]{0:T(256)(128)(2,1)} %param.28) | copy-start | bytes 1156
  7.3 8.1 %copy-start.65 = (bf16[192]{0:T(256)(128)(2,1)S(1)}, bf16[192]{0:T(256)(128)(2,1)}, u32[]{:S(2)}) copy-start(bf16[192]{0:T(256)(128)(2,1)} %param.29) | copy-start | bytes 1156
  7.3 8.1 %copy-start.59 = (bf16[768]{0:T(1024)(128)(2,1)S(1)}, bf16[768]{0:T(1024)(128)(2,1)}, u32[]{:S(2)}) copy-start(bf16[768]{0:T(1024)(128)(2,1)} %param.31) | copy-start | bytes 4612
  7.3 8.1 %copy-start.66 = (bf16[192]{0:T(256)(128)(2,1)S(1)}, bf16[192]{0:T(256)(128)(2,1)}, u32[]{:S(2)}) copy-start(bf16[192]{0:T(256)(128)(2,1)} %param.33) | copy-start | bytes 1156
  7.3 13.5 %copy-start.36 = (bf16[768,96]{0,1:T(8,128)(2,1)S(1)}, bf16[768,96]{0,1:T(8,128)(2,1)}, u32[]{:S(2)}) copy-start(bf16[768,96]{0,1:T(8,128)(2,1)} %param.32) | copy-start | bytes 442372
  7.3 55.1 %all-to-all-start = ((bf16[8,72,768]{2,1,0:T(8,128)(2,1)}), bf16[8,72,768]{2,1,0:T(8,128)(2,1)S(1)}, u32[]{:S(2)}, u32[]{:S(2)}) async-start(bf16[8,72,768]{2,1,0:T(8,128)(2,1)} %param.18), calls=%async_computation | async-start | bytes 1769472 | tf_op jit(solution)/shard_map/all_to_all | solution.py:498
  14.8 47.7 %copy-start.70 = (s32[8]{0:T(128)S(1)}, s32[8]{0:T(128)}, u32[]{:S(2)}) copy-start(s32[8]{0:T(128)} %param.20) | copy-start | bytes 100
  14.8 50.3 %copy-start.67 = (bf16[192]{0:T(256)(128)(2,1)S(1)}, bf16[192]{0:T(256)(128)(2,1)}, u32[]{:S(2)}) copy-start(bf16[192]{0:T(256)(128)(2,1)} %param.25) | copy-start | bytes 1156
  14.8 50.3 %copy-start.68 = (bf16[192]{0:T(256)(128)(2,1)S(1)}, bf16[192]{0:T(256)(128)(2,1)}, u32[]{:S(2)}) copy-start(bf16[192]{0:T(256)(128)(2,1)} %param.24) | copy-start | bytes 1156
  14.8 169.2 %all-gather.5.cloned.1.call-start = ((), (), s32[]{:S(2)}) async-start(), calls=%async_computation.12 | async-start | bytes 10948608 | tf_op jit(solution)/shard_map/all_gather | solution.py:575
  20.8 89.7 %copy-start.45 = (bf16[4,1,1920]{2,0,1:T(4,128)(2,1)}, bf16[4,1,1920]{2,0,1:T(4,128)(2,1)S(1)}, u32[]{:S(2)}) copy-start(bf16[4,1,1920]{2,0,1:T(4,128)(2,1)S(1)} %copy.385) | copy-start | bytes 46084
  62.5 152.4 %copy-start.2 = (bf16[8,72,768]{2,1,0:T(8,128)(2,1)}, bf16[8,72,768]{2,1,0:T(8,128)(2,1)S(1)}, u32[]{:S(2)}) copy-start(bf16[8,72,768]{2,1,0:T(8,128)(2,1)S(1)} %all-to-all-done) | copy-start | bytes 2654212
  66.7 7.5 %copy-start.37 = (s32[48,48]{0,1:T(8,128)}, s32[48,48]{0,1:T(8,128)S(1)}, u32[]{:S(2)}) copy-start(s32[48,48]{0,1:T(8,128)S(1)} %get-tuple-element.257) | copy-start | bytes 27652
  66.7 7.5 %copy-start.39 = (s32[48,48]{0,1:T(8,128)}, s32[48,48]{0,1:T(8,128)S(1)}, u32[]{:S(2)}) copy-start(s32[48,48]{0,1:T(8,128)S(1)} %get-tuple-element.258) | copy-start | bytes 27652
  66.7 41.5 %collective-permute-start = (bf16[576,768]{1,0:T(8,128)(2,1)S(1)}, bf16[576,768]{1,0:T(8,128)(2,1)}, u32[]{:S(2)}, u32[]{:S(2)}) collective-permute-start(bf16[576,768]{1,0:T(8,128)(2,1)S(1)} %bitcast.178), channel_id=1, source_target_pairs={{0,2},{1,3},{2,0},{3,1},{4,6},{5,7},{6,4},{7,5},{8,10},{9,11},{10,... | collective-permute-start | bytes 2654216 | tf_op jit(solution)/shard_map/ppermute | solution.py:405
  68.3 39.9 %collective-permute-start.1 = (bf16[576,768]{1,0:T(8,128)(2,1)S(1)}, bf16[576,768]{1,0:T(8,128)(2,1)}, u32[]{:S(2)}, u32[]{:S(2)}) collective-permute-start(bf16[576,768]{1,0:T(8,128)(2,1)S(1)} %bitcast.179), channel_id=1, source_target_pairs={{0,1},{1,0},{2,3},{3,2},{4,5},{5,4},{6,7},{7,6},{8,9},{9,8},{10,11... | collective-permute-start | bytes 2654216 | tf_op jit(solution)/shard_map/ppermute | solution.py:405
  69.2 5.0 copy-start.41
  69.3 5.0 copy-start.43
  70.7 33.2 %all-to-all-start.1 = ((bf16[4,192,576]{2,1,0:T(8,128)(2,1)}), bf16[4,192,576]{2,1,0:T(8,128)(2,1)S(1)}, u32[]{:S(2)}, u32[]{:S(2)}) async-start(bf16[4,192,576]{2,1,0:T(8,128)(2,1)} %copy.288), calls=%async_computation.1 | async-start | bytes 1966080 | tf_op jit(solution)/shard_map/all_to_all | solution.py:395
  74.2 3.2 copy-start.50
  104.0 8.6 %copy-start.30 = (bf16[4,192,576]{2,1,0:T(8,128)(2,1)}, bf16[4,192,576]{2,1,0:T(8,128)(2,1)S(1)}, u32[]{:S(2)}) copy-start(bf16[4,192,576]{2,1,0:T(8,128)(2,1)S(1)} %all-to-all-done.1) | copy-start | bytes 2654212
  104.0 40.4 %all-to-all-start.2 = ((bf16[8,72,768]{2,1,0:T(8,128)(2,1)}), bf16[8,72,768]{2,1,0:T(8,128)(2,1)}, u32[]{:S(2)}, u32[]{:S(2)}) async-start(bf16[8,72,768]{2,1,0:T(8,128)(2,1)} %param.19), calls=%async_computation.2 | async-start | bytes 1769472 | tf_op jit(solution)/shard_map/all_to_all | solution.py:502
  108.2 4.3 collective-permute-start.2
  114.4 4.9 copy-start.9
  114.4 4.8 copy-start.11
  114.5 4.8 copy-start.13
  119.3 3.5 copy-start.31
  119.3 3.5 copy-start.58
  122.8 3.1 copy-start.24
  186.4 6.9 %copy-start.51 = (f32[4,192]{1,0:T(4,128)S(1)}, f32[4,192]{1,0:T(4,128)}, u32[]{:S(2)}) copy-start(f32[4,192]{1,0:T(4,128)} %get-tuple-element.248) | copy-start | bytes 9220
  186.4 7.0 %copy-start.57 = (bf16[4,192]{1,0:T(4,128)(2,1)S(1)}, bf16[4,192]{1,0:T(4,128)(2,1)}, u32[]{:S(2)}) copy-start(bf16[4,192]{1,0:T(4,128)(2,1)} %get-tuple-element.247) | copy-start | bytes 4612
  186.4 7.0 %copy-start.56 = (bf16[4,192]{1,0:T(4,128)(2,1)S(1)}, bf16[4,192]{1,0:T(4,128)(2,1)}, u32[]{:S(2)}) copy-start(bf16[4,192]{1,0:T(4,128)(2,1)} %get-tuple-element.251) | copy-start | bytes 4612
  186.4 7.1 %copy-start.55 = (bf16[4,192]{1,0:T(4,128)(2,1)S(1)}, bf16[4,192]{1,0:T(4,128)(2,1)}, u32[]{:S(2)}) copy-start(bf16[4,192]{1,0:T(4,128)(2,1)} %get-tuple-element.250) | copy-start | bytes 4612
  186.4 7.2 %copy-start.54 = (bf16[4,192]{1,0:T(4,128)(2,1)S(1)}, bf16[4,192]{1,0:T(4,128)(2,1)}, u32[]{:S(2)}) copy-start(bf16[4,192]{1,0:T(4,128)(2,1)} %get-tuple-element.249) | copy-start | bytes 4612
  186.4 22.1 %all-to-all-start.3 = ((bf16[8,4,72,1,192]{4,2,0,3,1:T(8,128)(2,1)}), bf16[8,4,72,1,192]{4,2,0,3,1:T(8,128)(2,1)}, u32[]{:S(2)}, u32[]{:S(2)}) async-start(bf16[8,4,72,1,192]{4,2,0,3,1:T(8,128)(2,1)} %copy.297), calls=%async_computation.3 | async-start | bytes 2359296 | tf_op jit(solution)/shard_map/all_to_all | solution.py:585
  190.7 311.8 %reduce-scatter.2.cloned.1.call-start = ((), (), s32[]{:S(2)}) async-start(), calls=%async_computation.11 | async-start | bytes 10948608 | tf_op jit(solution)/shard_map/reduce_scatter | solution.py:685
  298.0 55.7 %all-to-all-start.5 = ((bf16[8,72,768]{2,1,0:T(8,128)(2,1)}), bf16[8,72,768]{2,1,0:T(8,128)(2,1)S(1)}, u32[]{:S(2)}, u32[]{:S(2)}) async-start(bf16[8,72,768]{2,1,0:T(8,128)(2,1)} %bitcast.228), calls=%async_computation.5 | async-start | bytes 1769472 | tf_op jit(solution)/shard_map/all_to_all | solution.py:395
  361.2 6.5 %copy-start.21 = (bf16[48,48,64,1]{2,1,3,0:T(8,128)(2,1)S(1)}, bf16[48,48,64,1]{2,1,3,0:T(8,128)(2,1)}, u32[]{:S(2)}) copy-start(bf16[48,48,64,1]{2,1,3,0:T(8,128)(2,1)} %fusion.30) | copy-start | bytes 884740
  380.0 3.6 copy-start.29
  385.7 3.1 copy-start.14
  385.7 3.1 copy-start.16
  385.7 3.3 copy-start.32
  385.7 3.3 copy-start.47
  385.7 3.3 copy-start.48
  396.5 24.8 %collective-permute-start.3 = (bf16[2,576,768]{2,1,0:T(8,128)(2,1)}, bf16[2,576,768]{2,1,0:T(8,128)(2,1)}, u32[]{:S(2)}, u32[]{:S(2)}) collective-permute-start(bf16[2,576,768]{2,1,0:T(8,128)(2,1)} %pad_maximum_fusion.6), channel_id=1, source_target_pairs={{0,1},{1,0},{2,3},{3,2},{4,5},{5,4},{6,7},{7,6},{8,9},{9,8},{10,11... | collective-permute-start | bytes 5308424 | tf_op jit(solution)/shard_map/ppermute | solution.py:405
  398.2 24.8 %all-to-all-start.8 = ((bf16[4,192,576]{2,1,0:T(8,128)(2,1)}), bf16[4,192,576]{2,1,0:T(8,128)(2,1)}, u32[]{:S(2)}, u32[]{:S(2)}) async-start(bf16[4,192,576]{2,1,0:T(8,128)(2,1)} %bitcast.223), calls=%async_computation.8 | async-start | bytes 1966080 | tf_op jit(solution)/shard_map/all_to_all | solution.py:395
  409.7 4.5 copy-start.18
  413.7 1.5 collective-permute-start.5
  415.2 5.2 %collective-permute-start.6 = (f32[4,4960]{1,0:T(4,128)S(1)}, f32[4,4960]{1,0:T(4,128)S(1)}, u32[]{:S(2)}, u32[]{:S(2)}) collective-permute-start(f32[4,4960]{1,0:T(4,128)S(1)} %add.329), channel_id=1, source_target_pairs={{0,2},{1,3},{2,0},{3,1},{4,6},{5,7},{6,4},{7,5},{8,10},{9,11},{10,... | collective-permute-start | bytes 238088 | tf_op jit(solution)/shard_map/ppermute | solution.py:405
  424.7 19.2 %all-to-all-start.7 = ((f32[8,113,128]{2,1,0:T(8,128)}), f32[8,113,128]{2,1,0:T(8,128)}, u32[]{:S(2)}, u32[]{:S(2)}) async-start(f32[8,113,128]{2,1,0:T(8,128)} %broadcast_in_dim.63), calls=%async_computation.7 | async-start | bytes 983040 | tf_op jit(solution)/shard_map/all_to_all | solution.py:395
  430.3 3.8 copy-start.3
  432.6 21.2 %collective-permute-start.4 = (bf16[576,768]{1,0:T(8,128)(2,1)}, bf16[576,768]{1,0:T(8,128)(2,1)}, u32[]{:S(2)}, u32[]{:S(2)}) collective-permute-start(bf16[576,768]{1,0:T(8,128)(2,1)} %fusion.45), channel_id=1, source_target_pairs={{0,2},{1,3},{2,0},{3,1},{4,6},{5,7},{6,4},{7,5},{8,10},{9,11},{10,... | collective-permute-start | bytes 2654216 | tf_op jit(solution)/shard_map/ppermute | solution.py:405
  439.0 14.8 %copy-start.46 = (f32[768]{0:T(1024)S(1)}, f32[768]{0:T(1024)}, u32[]{:S(2)}) copy-start(f32[768]{0:T(1024)} %reshape.532) | copy-start | bytes 9220
  443.9 32.7 %all-to-all-start.9 = ((bf16[8,192,288]{1,2,0:T(8,128)(2,1)}), bf16[8,192,288]{1,2,0:T(8,128)(2,1)}, u32[]{:S(2)}, u32[]{:S(2)}) async-start(bf16[8,192,288]{1,2,0:T(8,128)(2,1)} %bitcast.219), calls=%async_computation.9 | async-start | bytes 2359296 | tf_op jit(solution)/shard_map/all_to_all | solution.py:395
  448.5 7.8 %copy-start.4 = (bf16[8,72,768]{2,1,0:T(8,128)(2,1)S(1)}, bf16[8,72,768]{2,1,0:T(8,128)(2,1)}, u32[]{:S(2)}) copy-start(bf16[8,72,768]{2,1,0:T(8,128)(2,1)} %copy-done.2) | copy-start | bytes 2654212
  476.7 25.9 %all-to-all-start.6 = ((bf16[8,72,768]{2,1,0:T(8,128)(2,1)}), bf16[8,72,768]{2,1,0:T(8,128)(2,1)S(1)}, u32[]{:S(2)}, u32[]{:S(2)}) async-start(bf16[8,72,768]{2,1,0:T(8,128)(2,1)} %bitcast.56), calls=%async_computation.6 | async-start | bytes 1769472 | tf_op jit(solution)/shard_map/all_to_all | solution.py:395
  485.6 21.2 %copy-start.27 = (bf16[8,72,768]{2,1,0:T(8,128)(2,1)S(1)}, bf16[8,72,768]{2,1,0:T(8,128)(2,1)}, u32[]{:S(2)}) copy-start(bf16[8,72,768]{2,1,0:T(8,128)(2,1)} %copy-done.26) | copy-start | bytes 2654212
  (25 other events, 46.6 us)
Sparse Core Ops, SparseCore 0:
  62.6 97.5 all-gather.4
  274.3 145.4 reduce-scatter.1

commit v6 on v5

--- a/solution.py
+++ b/solution.py
@@ -299,7 +299,7 @@
         )
 
 
-def feed_forward(middle, cot, mask, vectors, shift, gathered, up_height, up_cols, out_cols):
+def feed_forward(middle, cot, mask, vectors, shift, gathered, up_height, out_cols):
     tokens, width = middle.shape
     groups, heads = gathered.shape[:2]
     steps = shift.shape[0]
@@ -416,6 +416,18 @@
         lax.dynamic_index_in_dim(blocks, jnp.bitwise_xor(me, i), 0, False) for i in range(4)
     ]
     return ordered, beside
+
+
+def exchange_heads(parts):
+    me = lax.axis_index("ha")
+    arrived = [
+        swap(lax.dynamic_index_in_dim(parts, jnp.bitwise_xor(me, i), 0, False), i)
+        for i in range(1, 4)
+    ]
+    blocks = jnp.stack([lax.dynamic_index_in_dim(parts, me, 0, False)] + arrived)
+    return jnp.stack(
+        [lax.dynamic_index_in_dim(blocks, jnp.bitwise_xor(me, i), 0, False) for i in range(4)]
+    )
 
 
 def scatter_heads(parts):
@@ -480,21 +492,29 @@
     triple_rows = lax.all_gather(qkv_weight, "ga", axis=1, tiled=True)
     up_rows, up_cols = fc1_weight.shape
     out_cols = fc2_weight.shape[1]
+    up_height = up_rows * up_cols // model_width
+    out_share = out_cols // head_groups
+    pack_rows = up_height + out_cols + out_share
+
+    vectors = jnp.concatenate(
+        [norm1_gain, norm1_bias, proj_bias, norm2_gain, norm2_bias, fc2_bias, fc1_bias]
+    )
+    vector_size = vectors.shape[0]
+    vectors_all = lax.all_gather(
+        jnp.concatenate([vectors, proj_weight.T.reshape(-1)]), "ha", axis=0, tiled=False
+    )
+    proj_rows = vectors_all[:, vector_size:].reshape(head_groups, head_groups, -1)
+    proj_mine = lax.dynamic_index_in_dim(proj_rows, head_index, 1, False)
     packed = jnp.concatenate(
         [
             pack_up(fc1_weight),
             fc2_weight.T,
-            proj_weight.T.reshape(out_cols // head_groups, model_width),
+            proj_mine.reshape(head_groups, out_share, group_width)
+            .transpose(1, 0, 2)
+            .reshape(out_share, model_width),
         ],
         axis=0,
     )
-    pack_rows = packed.shape[0]
-    up_height = up_rows * up_cols // model_width
-
-    vectors = jnp.concatenate(
-        [norm1_gain, norm1_bias, proj_bias, norm2_gain, norm2_bias, fc2_bias, fc1_bias]
-    )
-    vectors_all = lax.all_gather(vectors, "ha", axis=0, tiled=False)
     tokens_in = lax.all_to_all(patches, "ga", split_axis=0, concat_axis=1, tiled=True)[0]
     tokens_in, triple_rows, vectors_all, packed = lax.optimization_barrier(
         (tokens_in, triple_rows, vectors_all, packed)
@@ -575,12 +595,7 @@
     gathered = lax.all_gather(packed, BOTH, axis=0, tiled=False)
     att_heads, gathered = lax.optimization_barrier((att_heads, gathered))
     gathered = gathered.reshape(group_count, head_groups, pack_rows, model_width)
-    proj_turn = (
-        gathered[:, :, up_height + out_cols :]
-        .reshape(group_count, head_groups, out_cols, group_width)
-        .transpose(0, 2, 1, 3)
-        .reshape(model_width, model_width)
-    )
+    proj_turn = gathered[:, :, up_height + out_cols :].reshape(model_width, model_width)
 
     att_back = lax.all_to_all(
         att_heads.reshape(group_count, head_groups, block_len, 1, group_width),
@@ -611,7 +626,6 @@
             up_shift.astype(f32).reshape(steps, 1, model_width),
             gathered,
             up_height,
-            up_cols,
             out_cols,
         )
         up_bias_grad = up_bias_grad.reshape(-1)
@@ -638,12 +652,12 @@
         down_grad = contract_rows(down_in, activated).astype(bf16)
         down_bias_grad = jnp.sum(masked_cot, axis=0)
         act_grad = jnp.dot(down_in, down_turn, preferred_element_type=f32)
-        gelu_value, gelu_pull = jax.vjp(partial(jax.nn.gelu, approximate=False), hidden)
+        _, gelu_pull = jax.vjp(partial(jax.nn.gelu, approximate=False), hidden)
         hidden_grad = gelu_pull(act_grad)[0].astype(bf16)
         up_grad = contract_rows(normed2, hidden_grad).astype(bf16)
         up_bias_grad = jnp.sum(hidden_grad.astype(f32), axis=0)
         norm2_in = contract_cols(hidden_grad, up_full)
-        norm2_value, norm2_pull = jax.vjp(
+        _, norm2_pull = jax.vjp(
             layer_norm, middle, second_gain.astype(f32), second_shift.astype(f32)
         )
         mid_grad, second_gain_grad, second_shift_grad = norm2_pull(norm2_in)
@@ -676,16 +690,22 @@
         [
             up_packed,
             down_packed,
-            proj_grad.reshape(group_count, out_cols, head_groups, group_width)
-            .transpose(0, 2, 1, 3)
-            .reshape(group_count, head_groups, out_cols // head_groups, model_width),
+            proj_grad.reshape(group_count, head_groups, out_share, model_width),
         ],
         axis=2,
     ).reshape(device_count * pack_rows, model_width)
     grads_own = lax.psum_scatter(grads_packed, BOTH, scatter_dimension=0, tiled=True)
     up_own = unpack_up(grads_own[:up_height], up_rows, up_cols).astype(f32)
     down_own = grads_own[up_height : up_height + out_cols].T.astype(f32)
-    proj_own = grads_own[up_height + out_cols :].reshape(out_cols, group_width).T.astype(f32)
+    proj_own = (
+        exchange_heads(
+            grads_own[up_height + out_cols :]
+            .reshape(out_share, head_groups, group_width)
+            .transpose(1, 0, 2)
+        )
+        .reshape(out_cols, group_width)
+        .T.astype(f32)
+    )
 
     query_part, height_grad, width_grad, key_value_grad = attend_backward(
         mixed, rel_split, expand, att_grad, att_heads, log_sums
@@ -698,10 +718,10 @@
     query_grad = (
         query_part
         + jnp.einsum(
-            "hrwj,rjd->rwhd", height_grad, table_h, preferred_element_type=f32
+            "hrwj,rjd->rwhd", height_grad, table_h, preferred_element_type=bf16
         ).reshape(cap_tokens, group_width)
         + jnp.einsum(
-            "hrwj,wjd->rwhd", width_grad, table_w, preferred_element_type=f32
+            "hrwj,wjd->rwhd", width_grad, table_w, preferred_element_type=bf16
         ).reshape(cap_tokens, group_width)
     )
     mixed_grad = jnp.concatenate(
@@ -779,7 +799,7 @@
         late.append(last_sum[at : at + size])
         at += size
 
-    norm1_value, norm1_pull = jax.vjp(lambda tokens: layer_norm(tokens, gain32, shift32), tokens32)
+    _, norm1_pull = jax.vjp(lambda tokens: layer_norm(tokens, gain32, shift32), tokens32)
     input_grad = (mid_total + norm1_pull(norm1_in)[0]).astype(bf16)
     in_back = exchange(input_grad.reshape(group_count, block_len, model_width), "ga")
     return (

time: 526 us -> 521 us (level)
  waiting for transfers between devices: 71.2 us -> 79.4 us
  local copies, waits for them, and re-layouts: 98.1 us -> 90.5 us
    reshape x11 -> x4, local copies, waits for them, and re-layouts: 42.5 us -> 0.43 us  [the longest x1 0.12 us: local(): proj_weight.T.reshape(-1)]
    convert_element_type x2 -> x4, local copies, waits for them, and re-layouts: 0.83 us -> 20.7 us  [local(): query_part + jnp.einsum('hrwj,rjd->rwhd', height_grad, table_h, preferred...]
    reshape x1, local copies, waits for them, and re-layouts: 4.34 us -> 15 us  [local(): mixed[:, :group_width].reshape(SMAX, SMAX, group_heads, HD)]
    all_to_all x1, waiting for transfers between devices: 0.01 us -> 9.46 us  [local(): lax.all_to_all(att_heads.reshape(group_count, head_groups, block_len, 1,...]
    unnamed x152 -> x161, local copies, waits for them, and re-layouts: 9.48 us -> 11.8 us
  transfers between devices with their start and end apart: 18 -> 21, of which waited for: 7 -> 8; matrix products, arithmetic and copies ran while one was open for 28% -> 29% of each run, Pallas kernels for 17% -> 17%
where the time goes in v6:
time: 521 us; the launch traced here: 511 us
  Pallas kernels  119 us (23%)
  local copies, waits for them, and re-layouts  90.5 us (17%)
  waiting for transfers between devices  79.4 us (15%)
  blocking collectives  63.9 us (12%)
  other arithmetic  53.2 us (10%)
  starting transfers between devices  52.1 us (10%)
  matrix products  36.6 us (7%)
  between operations  16.7 us (3%)
    all_to_all x6, waiting for transfers between devices, exchange(): return lax.all_to_all(values, axis, split_axis=0, concat_axis=0, tiled=True)  61.6 us
    pallas_call x1, Pallas kernels, attend_backward(): pl.pallas_call(backward_kernel, grid=(tokens // TBLK,), in_specs=[pl.Bloc...  49.7 us
    all_gather x1, blocking collectives, local(): triple_rows = lax.all_gather(qkv_weight, 'ga', axis=1, tiled=True)  39.6 us
    pallas_call x1, Pallas kernels, attend_forward(): pl.pallas_call(forward_kernel, grid=(tokens // TBLK,), in_specs=[pl.Block...  39.4 us
    pallas_call x1, Pallas kernels, feed_forward(): pl.pallas_call(feed_kernel, grid=(steps,), in_specs=[whole(tokens, width)...  29.8 us
    all_to_all x6, starting transfers between devices, exchange(): return lax.all_to_all(values, axis, split_axis=0, concat_axis=0, tiled=True)  28.1 us
    convert_element_type x4, local copies, waits for them, and re-layouts, local(): query_part + jnp.einsum('hrwj,rjd->rwhd', height_grad, table_h, preferred...  20.7 us
    all_to_all x1, blocking collectives, local(): lax.all_to_all(att_grad_tok.reshape(group_count, 1, block_len, head_group...  18.3 us
  transfers between devices with their start and end apart: 21, of which 8 were waited for; matrix products, arithmetic and copies ran while one was open for 29% of the time, Pallas kernels for 17%

profile of v6, /device:TPU:0, one launch (start us, length us, event | category | flops | bytes accessed | tf_op | source)
XLA Modules:
  0.0 511.3 jit_solution(14564543563011209564)
XLA Ops:
  7.3 7.5 %all-to-all-start = ((bf16[8,72,768]{2,1,0:T(8,128)(2,1)}), bf16[8,72,768]{2,1,0:T(8,128)(2,1)S(1)}, u32[]{:S(2)}, u32[]{:S(2)}) async-start(bf16[8,72,768]{2,1,0:T(8,128)(2,1)} %param.18), calls=%async_computation | async-start | bytes 1769472 | tf_op jit(solution)/shard_map/all_to_all | solution.py:518
  15.3 6.1 %all-gather.2 = bf16[4,1,20352]{2,1,0:T(2,128)(2,1)S(1)} all-gather(bf16[1,1,20352]{2,1,0:T(2,128)(2,1)S(1)} %reshape.557), channel_id=2, replica_groups=mesh['ga'=8,'ha'=4] {'ha'}, dimensions={0}, use_global_device_ids=true | all-gather | bytes 203520 | tf_op jit(solution)/shard_map/all_gather | solution.py:503
  22.9 39.6 %all_gather.15 = bf16[192,2304]{0,1:T(8,128)(2,1)S(1)} all-gather(bf16[192,288]{0,1:T(8,128)(2,1)S(1)} %copy.280), channel_id=1, replica_groups=mesh['ga'=8,'ha'=4] {'ga'}, dimensions={1}, use_global_device_ids=true | all-gather | bytes 995328 | tf_op jit(solution)/shard_map/all_gather | solution.py:492
  66.8 1.8 collective-permute-start
  71.0 3.5 all-to-all-start.1
  75.9 1.8 fusion.33
  77.7 1.9 convolution_convert_fusion.3
  79.6 24.2 %all-to-all-done.1 = bf16[4,192,576]{2,1,0:T(8,128)(2,1)S(1)} async-done(((bf16[4,192,576]{2,1,0:T(8,128)(2,1)}), bf16[4,192,576]{2,1,0:T(8,128)(2,1)S(1)}, u32[]{:S(2)}, u32[]{:S(2)}) %all-to-all-start.1) | async-done | bytes 884768 | tf_op jit(solution)/shard_map/all_to_all | solution.py:395
  103.8 4.2 all-to-all-start.2
  108.1 2.2 fusion.39.lines_ref
  116.1 2.4 multiply_reduce_fusion.1
  119.2 3.5 add_convert_fusion
  122.7 3.1 add_convert_fusion.1.mixed_ref
  125.9 1.7 copy-done.6
  128.7 15.0 %reshape.571 = bf16[48,48,3,64]{3,2,1,0:T(4,128)(2,1)S(1)} reshape(bf16[2304,192]{1,0:T(8,128)(2,1)} %slice.134) | data formatting | bytes 1769472 | tf_op jit(solution)/shard_map/reshape | solution.py:580
  143.7 2.1 copy.331
  151.6 3.4 pad_maximum_fusion.4.rel_ref
  155.0 39.4 %attend_forward.1 = (bf16[2304,192]{1,0:T(8,128)(2,1)}, f32[3,1,2304]{2,1,0:T(1,128)}) custom-call(bf16[2304,576]{1,0:T(8,128)(2,1)} %copy-done.6, bf16[3,2304,192]{2,1,0:T(8,128)(2,1)} %pad_maximum_fusion.4.rel_ref, bf16[2304,96]{1,0:T(8,128)(2,1)} %fusion.39.lines_ref), custom_call_target="tpu_custom_call" | custom-call | tf_op jit(solution)/shard_map/attend_forward/pallas_call | solution.py:69
  194.4 2.3 copy.295
  196.7 4.3 all-to-all-start.3
  201.8 1.8 fusion.64.mask_ref
  206.0 2.4 slice.135
  208.4 9.5 %all-to-all-done.3 = bf16[8,4,72,1,192]{4,2,0,3,1:T(8,128)(2,1)} async-done(((bf16[8,4,72,1,192]{4,2,0,3,1:T(8,128)(2,1)}), bf16[8,4,72,1,192]{4,2,0,3,1:T(8,128)(2,1)}, u32[]{:S(2)}, u32[]{:S(2)}) %all-to-all-start.3) | async-done | bytes 884768 | tf_op jit(solution)/shard_map/all_to_all | solution.py:600
  217.8 3.2 copy.296
  221.0 3.6 reshape.521
  224.6 3.7 convert_add_fusion.mid_ref
  228.2 29.8 %feed_forward.1 = (bf16[576,768]{1,0:T(8,128)(2,1)}, f32[576,768]{1,0:T(8,128)}, bf16[576,768]{1,0:T(8,128)(2,1)}, f32[4,768]{1,0:T(4,128)}, f32[4,1,768]{2,1,0:...) custom-call(f32[576,768]{1,0:T(8,128)} %convert_add_fusion.mid_ref, ...), custom_call_target="tpu_custom_call" | custom-call | tf_op jit(solution)/shard_map/feed_forward/pallas_call | solution.py:315
  258.1 2.5 convolution_convert_fusion.1
  263.2 5.0 pad_maximum_fusion
  268.3 2.0 reshape.525
  271.7 18.3 %all_to_all.78 = bf16[8,1,72,4,192]{4,2,0,1,3:T(8,128)(2,1)S(1)} all-to-all(bf16[8,1,72,4,192]{4,2,0,1,3:T(8,128)(2,1)S(1)} %copy.300), channel_id=1, replica_groups=mesh['ga'=8,'ha'=4] {'ha'}, dimensions={3} | all-to-all | bytes 1769472 | tf_op jit(solution)/shard_map/all_to_all | solution.py:678
  291.1 6.1 %all-to-all-start.5 = ((bf16[8,72,768]{2,1,0:T(8,128)(2,1)}), bf16[8,72,768]{2,1,0:T(8,128)(2,1)S(1)}, u32[]{:S(2)}, u32[]{:S(2)}) async-start(bf16[8,72,768]{2,1,0:T(8,128)(2,1)} %bitcast.242), calls=%async_computation.5 | async-start | bytes 1769472 | tf_op jit(solution)/shard_map/all_to_all | solution.py:395
  297.2 49.7 %attend_backward.1 = (f32[2304,192]{1,0:T(8,128)}, bf16[3,2304,48]{2,1,0:T(8,128)(2,1)}, bf16[3,2304,48]{2,1,0:T(8,128)(2,1)}, bf16[2304,384]{1,0:T(8,128)(2,1)}) custom-call(bf16[2304,576]{1,0:T(8,128)(2,1)} %copy-done.6, bf16[3,2304,192]{2,1,0:T(8,128)(2,1)} %pad_maximum_fusion.4.rel_ref, bf16[2304,96]{1,0:T(8,128)(2,1)} %fusion.39.lines_ref, ...), custom_call_target="tpu_custom_call" | custom-call | tf_op jit(solution)/shard_map/attend_backward/pallas_call | solution.py:161
  346.9 2.4 copy.305
  350.7 3.9 copy.333
  354.6 6.4 %reshape.573 = f32[2304,192]{1,0:T(8,128)} reshape(f32[48,48,3,64]{3,2,1,0:T(4,128)} %copy.333) | data formatting | bytes 3538944 | tf_op jit(solution)/shard_map/convert_element_type | solution.py:719
  361.0 2.1 convert_bitcast_fusion.1
  363.1 4.0 copy.332
  367.1 6.4 %reshape.572 = f32[2304,192]{1,0:T(8,128)} reshape(f32[48,48,3,64]{3,2,1,0:T(4,128)} %copy.332) | data formatting | bytes 3538944 | tf_op jit(solution)/shard_map/convert_element_type | solution.py:719
  373.5 3.6 add_convert_fusion.2
  379.2 3.0 convolution_convert_fusion.2
  382.5 4.1 fusion.95
  387.0 1.7 copy-done.5
  391.8 4.5 all-to-all-start.8
  396.3 2.4 fusion.30
  399.6 3.4 fusion.40
  403.1 3.4 fusion.43
  408.6 1.9 collective-permute-start.6
  410.8 2.4 collective-permute-done.6
  414.2 1.7 convert_element_type.238
  417.6 5.9 %all-to-all-start.7 = ((f32[8,113,128]{2,1,0:T(8,128)}), f32[8,113,128]{2,1,0:T(8,128)}, u32[]{:S(2)}, u32[]{:S(2)}) async-start(f32[8,113,128]{2,1,0:T(8,128)} %broadcast_in_dim.63), calls=%async_computation.7 | async-start | bytes 983040 | tf_op jit(solution)/shard_map/all_to_all | solution.py:395
  423.5 2.3 fusion.48
  425.9 1.7 collective-permute-start.4
  427.8 2.3 copy.318
  430.1 2.4 copy.319
  432.5 4.6 all-to-all-done.7
  437.1 4.5 all-to-all-start.9
  441.7 5.3 %collective-permute-done.4 = bf16[576,768]{1,0:T(8,128)(2,1)} collective-permute-done((bf16[576,768]{1,0:T(8,128)(2,1)}, bf16[576,768]{1,0:T(8,128)(2,1)}, u32[]{:S(2)}, u32[]{:S(2)}) %collective-permute-start.4) | collective-permute-done | bytes 884768 | tf_op jit(solution)/shard_map/ppermute | solution.py:405
  447.0 2.5 fusion.7
  449.5 2.5 fusion.96
  453.2 16.7 %all-to-all-done.9 = bf16[8,192,288]{1,2,0:T(8,128)(2,1)} async-done(((bf16[8,192,288]{1,2,0:T(8,128)(2,1)}), bf16[8,192,288]{1,2,0:T(8,128)(2,1)}, u32[]{:S(2)}, u32[]{:S(2)}) %all-to-all-start.9) | async-done | bytes 884768 | tf_op jit(solution)/shard_map/all_to_all | solution.py:395
  469.8 3.6 all-to-all-start.6
  479.6 16.1 %all-to-all-done.6 = bf16[8,72,768]{2,1,0:T(8,128)(2,1)S(1)} async-done(((bf16[8,72,768]{2,1,0:T(8,128)(2,1)}), bf16[8,72,768]{2,1,0:T(8,128)(2,1)S(1)}, u32[]{:S(2)}, u32[]{:S(2)}) %all-to-all-start.6) | async-done | bytes 884768 | tf_op jit(solution)/shard_map/all_to_all | solution.py:395
  498.7 1.7 convert_bitcast_fusion.2
  (284 shorter events, 57.5 us)
Async XLA Ops:
  7.2 68.7 %copy-start = (bf16[95,64]{0,1:T(8,128)(2,1)S(1)}, bf16[95,64]{0,1:T(8,128)(2,1)}, u32[]{:S(2)}) copy-start(bf16[95,64]{0,1:T(8,128)(2,1)} %param.34) | copy-start | bytes 36484
  7.2 7.6 %copy-start.51 = (bf16[192,96]{1,0:T(8,128)(2,1)S(1)}, bf16[192,96]{1,0:T(8,128)(2,1)}, u32[]{:S(2)}) copy-start(bf16[192,96]{1,0:T(8,128)(2,1)} %param.26) | copy-start | bytes 110596
  7.2 7.8 %copy-start.65 = (bf16[192]{0:T(256)(128)(2,1)S(1)}, bf16[192]{0:T(256)(128)(2,1)}, u32[]{:S(2)}) copy-start(bf16[192]{0:T(256)(128)(2,1)} %param.21) | copy-start | bytes 1156
  7.2 7.8 %copy-start.66 = (bf16[192]{0:T(256)(128)(2,1)S(1)}, bf16[192]{0:T(256)(128)(2,1)}, u32[]{:S(2)}) copy-start(bf16[192]{0:T(256)(128)(2,1)} %param.22) | copy-start | bytes 1156
  7.2 7.8 %copy-start.67 = (bf16[192]{0:T(256)(128)(2,1)S(1)}, bf16[192]{0:T(256)(128)(2,1)}, u32[]{:S(2)}) copy-start(bf16[192]{0:T(256)(128)(2,1)} %param.27) | copy-start | bytes 1156
  7.3 7.8 %copy-start.68 = (bf16[192]{0:T(256)(128)(2,1)S(1)}, bf16[192]{0:T(256)(128)(2,1)}, u32[]{:S(2)}) copy-start(bf16[192]{0:T(256)(128)(2,1)} %param.28) | copy-start | bytes 1156
  7.3 7.8 %copy-start.69 = (bf16[192]{0:T(256)(128)(2,1)S(1)}, bf16[192]{0:T(256)(128)(2,1)}, u32[]{:S(2)}) copy-start(bf16[192]{0:T(256)(128)(2,1)} %param.29) | copy-start | bytes 1156
  7.3 7.8 %copy-start.61 = (bf16[768]{0:T(1024)(128)(2,1)S(1)}, bf16[768]{0:T(1024)(128)(2,1)}, u32[]{:S(2)}) copy-start(bf16[768]{0:T(1024)(128)(2,1)} %param.31) | copy-start | bytes 4612
  7.3 7.8 %copy-start.70 = (bf16[192]{0:T(256)(128)(2,1)S(1)}, bf16[192]{0:T(256)(128)(2,1)}, u32[]{:S(2)}) copy-start(bf16[192]{0:T(256)(128)(2,1)} %param.33) | copy-start | bytes 1156
  7.3 14.6 %copy-start.37 = (bf16[192,384]{1,0:T(8,128)(2,1)S(1)}, bf16[192,384]{1,0:T(8,128)(2,1)}, u32[]{:S(2)}) copy-start(bf16[192,384]{1,0:T(8,128)(2,1)} %param.30) | copy-start | bytes 442372
  7.3 14.7 %copy-start.38 = (bf16[192,288]{1,0:T(8,128)(2,1)S(1)}, bf16[192,288]{1,0:T(8,128)(2,1)}, u32[]{:S(2)}) copy-start(bf16[192,288]{1,0:T(8,128)(2,1)} %param.23) | copy-start | bytes 331780
  7.3 55.2 %all-to-all-start = ((bf16[8,72,768]{2,1,0:T(8,128)(2,1)}), bf16[8,72,768]{2,1,0:T(8,128)(2,1)S(1)}, u32[]{:S(2)}, u32[]{:S(2)}) async-start(bf16[8,72,768]{2,1,0:T(8,128)(2,1)} %param.18), calls=%async_computation | async-start | bytes 1769472 | tf_op jit(solution)/shard_map/all_to_all | solution.py:518
  14.8 7.4 %copy-start.39 = (bf16[768,96]{0,1:T(8,128)(2,1)S(1)}, bf16[768,96]{0,1:T(8,128)(2,1)}, u32[]{:S(2)}) copy-start(bf16[768,96]{0,1:T(8,128)(2,1)} %param.32) | copy-start | bytes 442372
  14.8 179.6 %all-gather.5.cloned.1.call-start = ((), (), s32[]{:S(2)}) async-start(), calls=%async_computation.12 | async-start | bytes 10948608 | tf_op jit(solution)/shard_map/all_gather | solution.py:595
  21.5 88.9 %copy-start.36 = (bf16[4,1,20352]{2,0,1:T(4,128)(2,1)}, bf16[4,1,20352]{2,0,1:T(4,128)(2,1)S(1)}, u32[]{:S(2)}) copy-start(bf16[4,1,20352]{2,0,1:T(4,128)(2,1)S(1)} %copy.389) | copy-start | bytes 488452
  21.6 41.0 %copy-start.72 = (s32[8]{0:T(128)S(1)}, s32[8]{0:T(128)}, u32[]{:S(2)}) copy-start(s32[8]{0:T(128)} %param.20) | copy-start | bytes 100
  21.6 43.5 %copy-start.63 = (bf16[192]{0:T(256)(128)(2,1)S(1)}, bf16[192]{0:T(256)(128)(2,1)}, u32[]{:S(2)}) copy-start(bf16[192]{0:T(256)(128)(2,1)} %param.25) | copy-start | bytes 1156
  21.6 43.5 %copy-start.64 = (bf16[192]{0:T(256)(128)(2,1)S(1)}, bf16[192]{0:T(256)(128)(2,1)}, u32[]{:S(2)}) copy-start(bf16[192]{0:T(256)(128)(2,1)} %param.24) | copy-start | bytes 1156
  62.5 162.1 %copy-start.2 = (bf16[8,72,768]{2,1,0:T(8,128)(2,1)}, bf16[8,72,768]{2,1,0:T(8,128)(2,1)S(1)}, u32[]{:S(2)}) copy-start(bf16[8,72,768]{2,1,0:T(8,128)(2,1)S(1)} %all-to-all-done) | copy-start | bytes 2654212
  66.8 7.8 %copy-start.40 = (s32[48,48]{0,1:T(8,128)}, s32[48,48]{0,1:T(8,128)S(1)}, u32[]{:S(2)}) copy-start(s32[48,48]{0,1:T(8,128)S(1)} %get-tuple-element.265) | copy-start | bytes 27652
  66.8 7.8 %copy-start.42 = (s32[48,48]{0,1:T(8,128)}, s32[48,48]{0,1:T(8,128)S(1)}, u32[]{:S(2)}) copy-start(s32[48,48]{0,1:T(8,128)S(1)} %get-tuple-element.266) | copy-start | bytes 27652
  66.8 41.3 %collective-permute-start = (bf16[576,768]{1,0:T(8,128)(2,1)S(1)}, bf16[576,768]{1,0:T(8,128)(2,1)}, u32[]{:S(2)}, u32[]{:S(2)}) collective-permute-start(bf16[576,768]{1,0:T(8,128)(2,1)S(1)} %bitcast.191), channel_id=1, source_target_pairs={{0,2},{1,3},{2,0},{3,1},{4,6},{5,7},{6,4},{7,5},{8,10},{9,11},{10,... | collective-permute-start | bytes 2654216 | tf_op jit(solution)/shard_map/ppermute | solution.py:405
  68.6 39.5 %collective-permute-start.1 = (bf16[576,768]{1,0:T(8,128)(2,1)S(1)}, bf16[576,768]{1,0:T(8,128)(2,1)}, u32[]{:S(2)}, u32[]{:S(2)}) collective-permute-start(bf16[576,768]{1,0:T(8,128)(2,1)S(1)} %bitcast.192), channel_id=1, source_target_pairs={{0,1},{1,0},{2,3},{3,2},{4,5},{5,4},{6,7},{7,6},{8,9},{9,8},{10,11... | collective-permute-start | bytes 2654216 | tf_op jit(solution)/shard_map/ppermute | solution.py:405
  69.5 5.0 copy-start.44
  69.6 5.0 copy-start.46
  71.0 32.8 %all-to-all-start.1 = ((bf16[4,192,576]{2,1,0:T(8,128)(2,1)}), bf16[4,192,576]{2,1,0:T(8,128)(2,1)S(1)}, u32[]{:S(2)}, u32[]{:S(2)}) async-start(bf16[4,192,576]{2,1,0:T(8,128)(2,1)} %copy.286), calls=%async_computation.1 | async-start | bytes 1966080 | tf_op jit(solution)/shard_map/all_to_all | solution.py:395
  103.8 8.6 %copy-start.32 = (bf16[4,192,576]{2,1,0:T(8,128)(2,1)}, bf16[4,192,576]{2,1,0:T(8,128)(2,1)S(1)}, u32[]{:S(2)}) copy-start(bf16[4,192,576]{2,1,0:T(8,128)(2,1)S(1)} %all-to-all-done.1) | copy-start | bytes 2654212
  103.8 51.2 %all-to-all-start.2 = ((bf16[8,72,768]{2,1,0:T(8,128)(2,1)}), bf16[8,72,768]{2,1,0:T(8,128)(2,1)}, u32[]{:S(2)}, u32[]{:S(2)}) async-start(bf16[8,72,768]{2,1,0:T(8,128)(2,1)} %param.19), calls=%async_computation.2 | async-start | bytes 1769472 | tf_op jit(solution)/shard_map/all_to_all | solution.py:522
  108.1 4.3 collective-permute-start.2
  114.3 4.9 copy-start.9
  114.3 4.8 copy-start.11
  114.3 4.8 copy-start.13
  119.2 3.5 copy-start.33
  119.2 3.5 copy-start.60
  196.7 6.9 %copy-start.53 = (f32[4,192]{1,0:T(4,128)S(1)}, f32[4,192]{1,0:T(4,128)}, u32[]{:S(2)}) copy-start(f32[4,192]{1,0:T(4,128)} %get-tuple-element.238) | copy-start | bytes 9220
  196.7 7.0 %copy-start.59 = (bf16[4,192]{1,0:T(4,128)(2,1)S(1)}, bf16[4,192]{1,0:T(4,128)(2,1)}, u32[]{:S(2)}) copy-start(bf16[4,192]{1,0:T(4,128)(2,1)} %get-tuple-element.237) | copy-start | bytes 4612
  196.7 7.0 %copy-start.58 = (bf16[4,192]{1,0:T(4,128)(2,1)S(1)}, bf16[4,192]{1,0:T(4,128)(2,1)}, u32[]{:S(2)}) copy-start(bf16[4,192]{1,0:T(4,128)(2,1)} %get-tuple-element.241) | copy-start | bytes 4612
  196.7 7.1 %copy-start.57 = (bf16[4,192]{1,0:T(4,128)(2,1)S(1)}, bf16[4,192]{1,0:T(4,128)(2,1)}, u32[]{:S(2)}) copy-start(bf16[4,192]{1,0:T(4,128)(2,1)} %get-tuple-element.240) | copy-start | bytes 4612
  196.7 7.2 %copy-start.56 = (bf16[4,192]{1,0:T(4,128)(2,1)S(1)}, bf16[4,192]{1,0:T(4,128)(2,1)}, u32[]{:S(2)}) copy-start(bf16[4,192]{1,0:T(4,128)(2,1)} %get-tuple-element.239) | copy-start | bytes 4612
  196.7 21.1 %all-to-all-start.3 = ((bf16[8,4,72,1,192]{4,2,0,3,1:T(8,128)(2,1)}), bf16[8,4,72,1,192]{4,2,0,3,1:T(8,128)(2,1)}, u32[]{:S(2)}, u32[]{:S(2)}) async-start(bf16[8,4,72,1,192]{4,2,0,3,1:T(8,128)(2,1)} %copy.295), calls=%async_computation.3 | async-start | bytes 2359296 | tf_op jit(solution)/shard_map/all_to_all | solution.py:600
  201.1 294.6 %reduce-scatter.2.cloned.1.call-start = ((), (), s32[]{:S(2)}) async-start(), calls=%async_computation.11 | async-start | bytes 10948608 | tf_op jit(solution)/shard_map/reduce_scatter | solution.py:697
  258.1 3.7 copy-start.25
  291.1 55.8 %all-to-all-start.5 = ((bf16[8,72,768]{2,1,0:T(8,128)(2,1)}), bf16[8,72,768]{2,1,0:T(8,128)(2,1)S(1)}, u32[]{:S(2)}, u32[]{:S(2)}) async-start(bf16[8,72,768]{2,1,0:T(8,128)(2,1)} %bitcast.242), calls=%async_computation.5 | async-start | bytes 1769472 | tf_op jit(solution)/shard_map/all_to_all | solution.py:395
  354.6 6.4 %copy-start.21 = (bf16[48,48,64,1]{2,1,3,0:T(8,128)(2,1)S(1)}, bf16[48,48,64,1]{2,1,3,0:T(8,128)(2,1)}, u32[]{:S(2)}) copy-start(bf16[48,48,64,1]{2,1,3,0:T(8,128)(2,1)} %fusion.33) | copy-start | bytes 884740
  373.5 3.6 copy-start.31
  379.2 3.3 copy-start.34
  379.2 3.3 copy-start.49
  379.2 3.3 copy-start.50
  390.1 24.1 %collective-permute-start.3 = (bf16[2,576,768]{2,1,0:T(8,128)(2,1)}, bf16[2,576,768]{2,1,0:T(8,128)(2,1)}, u32[]{:S(2)}, u32[]{:S(2)}) collective-permute-start(bf16[2,576,768]{2,1,0:T(8,128)(2,1)} %pad_maximum_fusion.6), channel_id=1, source_target_pairs={{0,1},{1,0},{2,3},{3,2},{4,5},{5,4},{6,7},{7,6},{8,9},{9,8},{10,11... | collective-permute-start | bytes 5308424 | tf_op jit(solution)/shard_map/ppermute | solution.py:405
  391.8 24.1 %all-to-all-start.8 = ((bf16[4,192,576]{2,1,0:T(8,128)(2,1)}), bf16[4,192,576]{2,1,0:T(8,128)(2,1)}, u32[]{:S(2)}, u32[]{:S(2)}) async-start(bf16[4,192,576]{2,1,0:T(8,128)(2,1)} %bitcast.234), calls=%async_computation.8 | async-start | bytes 1966080 | tf_op jit(solution)/shard_map/all_to_all | solution.py:395
  403.1 4.5 copy-start.18
  407.1 1.5 collective-permute-start.5
  408.6 4.7 collective-permute-start.6
  417.6 19.5 %all-to-all-start.7 = ((f32[8,113,128]{2,1,0:T(8,128)}), f32[8,113,128]{2,1,0:T(8,128)}, u32[]{:S(2)}, u32[]{:S(2)}) async-start(f32[8,113,128]{2,1,0:T(8,128)} %broadcast_in_dim.63), calls=%async_computation.7 | async-start | bytes 983040 | tf_op jit(solution)/shard_map/all_to_all | solution.py:395
  423.5 4.0 copy-start.3
  425.9 21.1 %collective-permute-start.4 = (bf16[576,768]{1,0:T(8,128)(2,1)}, bf16[576,768]{1,0:T(8,128)(2,1)}, u32[]{:S(2)}, u32[]{:S(2)}) collective-permute-start(bf16[576,768]{1,0:T(8,128)(2,1)} %fusion.48), channel_id=1, source_target_pairs={{0,2},{1,3},{2,0},{3,1},{4,6},{5,7},{6,4},{7,5},{8,10},{9,11},{10,... | collective-permute-start | bytes 2654216 | tf_op jit(solution)/shard_map/ppermute | solution.py:405
  432.5 14.5 %copy-start.48 = (f32[768]{0:T(1024)S(1)}, f32[768]{0:T(1024)}, u32[]{:S(2)}) copy-start(f32[768]{0:T(1024)} %reshape.546) | copy-start | bytes 9220
  437.1 32.7 %all-to-all-start.9 = ((bf16[8,192,288]{1,2,0:T(8,128)(2,1)}), bf16[8,192,288]{1,2,0:T(8,128)(2,1)}, u32[]{:S(2)}, u32[]{:S(2)}) async-start(bf16[8,192,288]{1,2,0:T(8,128)(2,1)} %bitcast.230), calls=%async_computation.9 | async-start | bytes 2359296 | tf_op jit(solution)/shard_map/all_to_all | solution.py:395
  441.7 7.8 %copy-start.4 = (bf16[8,72,768]{2,1,0:T(8,128)(2,1)S(1)}, bf16[8,72,768]{2,1,0:T(8,128)(2,1)}, u32[]{:S(2)}) copy-start(bf16[8,72,768]{2,1,0:T(8,128)(2,1)} %copy-done.2) | copy-start | bytes 2654212
  469.8 25.9 %all-to-all-start.6 = ((bf16[8,72,768]{2,1,0:T(8,128)(2,1)}), bf16[8,72,768]{2,1,0:T(8,128)(2,1)S(1)}, u32[]{:S(2)}, u32[]{:S(2)}) async-start(bf16[8,72,768]{2,1,0:T(8,128)(2,1)} %bitcast.58), calls=%async_computation.6 | async-start | bytes 1769472 | tf_op jit(solution)/shard_map/all_to_all | solution.py:395
  479.6 22.6 %copy-start.29 = (bf16[8,72,768]{2,1,0:T(8,128)(2,1)S(1)}, bf16[8,72,768]{2,1,0:T(8,128)(2,1)}, u32[]{:S(2)}) copy-start(bf16[8,72,768]{2,1,0:T(8,128)(2,1)} %copy-done.28) | copy-start | bytes 2654212
  496.7 4.6 collective-permute-start.7
  496.8 4.5 collective-permute-start.8
  498.2 3.1 collective-permute-start.9
  (30 other events, 61.5 us)
Sparse Core Ops, SparseCore 0:
  62.6 97.2 all-gather.4
  268.4 142.5 reduce-scatter.1

commit v7 on v6

--- a/solution.py
+++ b/solution.py
@@ -124,7 +124,6 @@
             kt_ref[h] = jnp.concatenate([keys, lines], axis=1).T
 
     zero = jnp.zeros((TBLK, HD), bf16)
-    query_grads = []
     for h in range(heads):
         q_here = query_rows(mixed_ref, rel_ref, h)
         g_here = g_ref[:, h * HD : (h + 1) * HD]
@@ -143,10 +142,9 @@
             dkv_ref[h, span, :] += mm(probs.astype(bf16), g_wide) + mm(sgrad, q_wide)
             part = mm(kt_ref[h, :, span], sgrad)
             total = part if total is None else total + part
-        query_grads.append(total[:HD].T)
+        dq_ref[h] = HD**-0.5 * total[:HD].T
         rows_ref[h] = total[HD : HD + SMAX].T.astype(bf16)
         cols_ref[h] = total[HD + SMAX :].T.astype(bf16)
-    dq_ref[...] = HD**-0.5 * jnp.concatenate(query_grads, axis=1)
 
     @pl.when(pl.program_id(0) == pl.num_programs(0) - 1)
     def _():
@@ -170,13 +168,13 @@
             pl.BlockSpec((heads, 1, TBLK), lambda t: (0, 0, t)),
         ],
         out_specs=[
-            pl.BlockSpec((TBLK, width), lambda t: (t, 0)),
+            pl.BlockSpec((heads, TBLK, HD), lambda t: (0, t, 0)),
             pl.BlockSpec((heads, TBLK, SMAX), lambda t: (0, t, 0)),
             pl.BlockSpec((heads, TBLK, SMAX), lambda t: (0, t, 0)),
             pl.BlockSpec((tokens, 2 * width), lambda t: (0, 0)),
         ],
         out_shape=[
-            jax.ShapeDtypeStruct((tokens, width), jnp.float32),
+            jax.ShapeDtypeStruct((heads, tokens, HD), jnp.float32),
             jax.ShapeDtypeStruct((heads, tokens, SMAX), jnp.bfloat16),
             jax.ShapeDtypeStruct((heads, tokens, SMAX), jnp.bfloat16),
             jax.ShapeDtypeStruct((tokens, 2 * width), jnp.bfloat16),
@@ -405,17 +403,17 @@
     return lax.ppermute(values, "ha", pairs)
 
 
-def gather_heads(values, beside):
+def gather_heads(values, beside, later):
     me = lax.axis_index("ha")
     far = swap(values, 2)
     near = swap(values, 1)
-    far, near, beside = lax.optimization_barrier((far, near, beside))
+    far, near, beside, later = lax.optimization_barrier((far, near, beside, later))
     corner = swap(far, 1)
     blocks = jnp.stack([values, near, far, corner])
     ordered = [
         lax.dynamic_index_in_dim(blocks, jnp.bitwise_xor(me, i), 0, False) for i in range(4)
     ]
-    return ordered, beside
+    return ordered, beside, later
 
 
 def exchange_heads(parts):
@@ -516,8 +514,8 @@
         axis=0,
     )
     tokens_in = lax.all_to_all(patches, "ga", split_axis=0, concat_axis=1, tiled=True)[0]
-    tokens_in, triple_rows, vectors_all, packed = lax.optimization_barrier(
-        (tokens_in, triple_rows, vectors_all, packed)
+    tokens_in, triple_rows, vectors_all = lax.optimization_barrier(
+        (tokens_in, triple_rows, vectors_all)
     )
     cot_in = lax.all_to_all(cotangent, "ga", split_axis=0, concat_axis=1, tiled=True)[0]
     wide = model_width // head_groups
@@ -562,7 +560,7 @@
         bf16
     )
 
-    blocks_all, triple_own = gather_heads(tokens_in, triple_own)
+    blocks_all, triple_own, packed = gather_heads(tokens_in, triple_own, packed)
     tokens_all = (
         jnp.stack(
             [block.reshape(group_count, block_len, model_width) for block in blocks_all],
@@ -695,18 +693,6 @@
         axis=2,
     ).reshape(device_count * pack_rows, model_width)
     grads_own = lax.psum_scatter(grads_packed, BOTH, scatter_dimension=0, tiled=True)
-    up_own = unpack_up(grads_own[:up_height], up_rows, up_cols).astype(f32)
-    down_own = grads_own[up_height : up_height + out_cols].T.astype(f32)
-    proj_own = (
-        exchange_heads(
-            grads_own[up_height + out_cols :]
-            .reshape(out_share, head_groups, group_width)
-            .transpose(1, 0, 2)
-        )
-        .reshape(out_cols, group_width)
-        .T.astype(f32)
-    )
-
     query_part, height_grad, width_grad, key_value_grad = attend_backward(
         mixed, rel_split, expand, att_grad, att_heads, log_sums
     )
@@ -716,19 +702,12 @@
     height_grad = height_grad.reshape(group_heads, SMAX, SMAX, SMAX)
     width_grad = width_grad.reshape(group_heads, SMAX, SMAX, SMAX)
     query_grad = (
-        query_part
-        + jnp.einsum(
-            "hrwj,rjd->rwhd", height_grad, table_h, preferred_element_type=bf16
-        ).reshape(cap_tokens, group_width)
-        + jnp.einsum(
-            "hrwj,wjd->rwhd", width_grad, table_w, preferred_element_type=bf16
-        ).reshape(cap_tokens, group_width)
-    )
+        query_part.reshape(group_heads, SMAX, SMAX, HD)
+        + jnp.einsum("hrwj,rjd->hrwd", height_grad, table_h, preferred_element_type=f32)
+        + jnp.einsum("hrwj,wjd->hrwd", width_grad, table_w, preferred_element_type=f32)
+    ).astype(bf16)
     mixed_grad = jnp.concatenate(
-        [
-            query_grad.astype(bf16),
-            key_value_grad,
-        ],
+        [query_grad[i].reshape(cap_tokens, HD) for i in range(group_heads)] + [key_value_grad],
         axis=1,
     )
     triple_part = contract_rows(normed_all, mixed_grad).astype(bf16)
@@ -745,8 +724,9 @@
         .reshape(head_groups, local_tokens, model_width)
     )
     norm1_in = scatter_heads(norm1_part)
+    norm1_in, grads_own = lax.optimization_barrier((norm1_in, grads_own))
     triple_rows_grad = (
-        exchange(triple_part.reshape(head_groups, group_width, 3 * group_width), "ha")
+        exchange_heads(triple_part.reshape(head_groups, group_width, 3 * group_width))
         .reshape(head_groups, group_width, 3, group_width)
         .transpose(1, 2, 0, 3)
         .reshape(group_width, group_count, 3 * model_width // group_count)
@@ -798,6 +778,18 @@
     for size in [group_width] * 6 + [hidden_width // head_groups] + [group_width] * 2:
         late.append(last_sum[at : at + size])
         at += size
+
+    up_own = unpack_up(grads_own[:up_height], up_rows, up_cols).astype(f32)
+    down_own = grads_own[up_height : up_height + out_cols].T.astype(f32)
+    proj_own = (
+        exchange_heads(
+            grads_own[up_height + out_cols :]
+            .reshape(out_share, head_groups, group_width)
+            .transpose(1, 0, 2)
+        )
+        .reshape(out_cols, group_width)
+        .T.astype(f32)
+    )
 
     _, norm1_pull = jax.vjp(lambda tokens: layer_norm(tokens, gain32, shift32), tokens32)
     input_grad = (mid_total + norm1_pull(norm1_in)[0]).astype(bf16)

time: 521 us -> 501 us (0.962)
  local copies, waits for them, and re-layouts: 90.5 us -> 60.4 us
  waiting for transfers between devices: 79.4 us -> 96 us
  starting transfers between devices: 52.1 us -> 46.7 us
    ppermute x10 -> x13, waiting for transfers between devices: 8.25 us -> 30.3 us  [swap(): return lax.ppermute(values, 'ha', pairs)]
    convert_element_type x4 -> x0, local copies, waits for them, and re-layouts: 20.7 us -> none  [local(): query_part + jnp.einsum('hrwj,rjd->rwhd', height_grad, table_h, preferred...]
    reshape x1, local copies, waits for them, and re-layouts: 15 us -> 4.34 us  [local(): mixed[:, :group_width].reshape(SMAX, SMAX, group_heads, HD)]
    all_to_all x6 -> x5, waiting for transfers between devices: 61.6 us -> 53.7 us  [exchange(): return lax.all_to_all(values, axis, split_axis=0, concat_axis=0, tiled=True)]
    all_to_all x6 -> x5, starting transfers between devices: 28.1 us -> 23.4 us  [exchange(): return lax.all_to_all(values, axis, split_axis=0, concat_axis=0, tiled=True)]
    unnamed x161 -> x157, local copies, waits for them, and re-layouts: 11.8 us -> 15.9 us
  transfers between devices with their start and end apart: 21 -> 23, of which waited for: 8 -> 10; matrix products, arithmetic and copies ran while one was open for 29% -> 23% of each run, Pallas kernels for 17% -> 18%
where the time goes in v7:
time: 501 us; the launch traced here: 492 us
  Pallas kernels  119 us (24%)
  waiting for transfers between devices  96 us (19%)
  blocking collectives  65.2 us (13%)
  local copies, waits for them, and re-layouts  60.4 us (12%)
  other arithmetic  50.4 us (10%)
  starting transfers between devices  46.7 us (9%)
  matrix products  37.5 us (7%)
  between operations  16.6 us (3%)
    all_to_all x5, waiting for transfers between devices, exchange(): return lax.all_to_all(values, axis, split_axis=0, concat_axis=0, tiled=True)  53.7 us
    pallas_call x1, Pallas kernels, attend_backward(): pl.pallas_call(backward_kernel, grid=(tokens // TBLK,), in_specs=[pl.Bloc...  49.7 us
    all_gather x1, blocking collectives, local(): triple_rows = lax.all_gather(qkv_weight, 'ga', axis=1, tiled=True)  40.9 us
    pallas_call x1, Pallas kernels, attend_forward(): pl.pallas_call(forward_kernel, grid=(tokens // TBLK,), in_specs=[pl.Block...  39.4 us
    ppermute x13, waiting for transfers between devices, swap(): return lax.ppermute(values, 'ha', pairs)  30.3 us
    pallas_call x1, Pallas kernels, feed_forward(): pl.pallas_call(feed_kernel, grid=(steps,), in_specs=[whole(tokens, width)...  29.8 us
    all_to_all x5, starting transfers between devices, exchange(): return lax.all_to_all(values, axis, split_axis=0, concat_axis=0, tiled=True)  23.4 us
    all_to_all x1, blocking collectives, local(): lax.all_to_all(att_grad_tok.reshape(group_count, 1, block_len, head_group...  18.3 us
  transfers between devices with their start and end apart: 23, of which 10 were waited for; matrix products, arithmetic and copies ran while one was open for 23% of the time, Pallas kernels for 18%

profile of v7, /device:TPU:0, one launch (start us, length us, event | category | flops | bytes accessed | tf_op | source)
XLA Modules:
  0.0 491.7 jit_solution(4443671087339358574)
XLA Ops:
  7.3 7.5 %all-to-all-start = ((bf16[8,72,768]{2,1,0:T(8,128)(2,1)}), bf16[8,72,768]{2,1,0:T(8,128)(2,1)S(1)}, u32[]{:S(2)}, u32[]{:S(2)}) async-start(bf16[8,72,768]{2,1,0:T(8,128)(2,1)} %param.18), calls=%async_computation | async-start | bytes 1769472 | tf_op jit(solution)/shard_map/all_to_all | solution.py:516
  15.2 6.1 %all-gather.2 = bf16[4,1,20352]{2,1,0:T(2,128)(2,1)S(1)} all-gather(bf16[1,1,20352]{2,1,0:T(2,128)(2,1)S(1)} %reshape.553), channel_id=2, replica_groups=mesh['ga'=8,'ha'=4] {'ha'}, dimensions={0}, use_global_device_ids=true | all-gather | bytes 203520 | tf_op jit(solution)/shard_map/all_gather | solution.py:501
  21.5 40.9 %all_gather.15 = bf16[192,2304]{0,1:T(8,128)(2,1)S(1)} all-gather(bf16[192,288]{0,1:T(8,128)(2,1)S(1)} %copy.268), channel_id=1, replica_groups=mesh['ga'=8,'ha'=4] {'ga'}, dimensions={1}, use_global_device_ids=true | all-gather | bytes 995328 | tf_op jit(solution)/shard_map/all_gather | solution.py:490
  62.4 1.5 collective-permute-start
  64.7 1.3 copy.271
  66.1 3.6 all-to-all-start.1
  71.8 16.9 %all-to-all-done.1 = bf16[4,192,576]{2,1,0:T(8,128)(2,1)S(1)} async-done(((bf16[4,192,576]{2,1,0:T(8,128)(2,1)}), bf16[4,192,576]{2,1,0:T(8,128)(2,1)S(1)}, u32[]{:S(2)}, u32[]{:S(2)}) %all-to-all-start.1) | async-done | bytes 884768 | tf_op jit(solution)/shard_map/all_to_all | solution.py:393
  88.7 4.2 all-to-all-start.2
  99.4 1.9 fusion.30
  101.2 1.8 convolution_convert_fusion.3
  103.2 2.2 fusion.36.lines_ref
  107.4 1.7 pad_maximum_fusion.1
  111.1 2.4 multiply_reduce_fusion.1
  114.2 3.5 add_convert_fusion
  117.7 3.1 add_convert_fusion.1.mixed_ref
  120.9 1.7 copy-done.2
  123.7 4.3 reshape.567
  128.1 2.1 copy.317
  136.0 3.4 pad_maximum_fusion.4.rel_ref
  139.3 39.4 %attend_forward.1 = (bf16[2304,192]{1,0:T(8,128)(2,1)}, f32[3,1,2304]{2,1,0:T(1,128)}) custom-call(bf16[2304,576]{1,0:T(8,128)(2,1)} %copy-done.2, bf16[3,2304,192]{2,1,0:T(8,128)(2,1)} %pad_maximum_fusion.4.rel_ref, bf16[2304,96]{1,0:T(8,128)(2,1)} %fusion.36.lines_ref), custom_call_target="tpu_custom_call" | custom-call | tf_op jit(solution)/shard_map/attend_forward/pallas_call | solution.py:69
  178.7 3.2 all-gather.5.cloned.1.call-done
  181.9 2.4 copy.283
  184.3 4.3 all-to-all-start.3
  189.3 1.8 fusion.61.mask_ref
  193.5 2.4 slice.147
  195.9 8.6 %all-to-all-done.3 = bf16[8,4,72,1,192]{4,2,0,3,1:T(8,128)(2,1)} async-done(((bf16[8,4,72,1,192]{4,2,0,3,1:T(8,128)(2,1)}), bf16[8,4,72,1,192]{4,2,0,3,1:T(8,128)(2,1)}, u32[]{:S(2)}, u32[]{:S(2)}) %all-to-all-start.3) | async-done | bytes 884768 | tf_op jit(solution)/shard_map/all_to_all | solution.py:598
  204.5 3.2 copy.284
  207.7 3.6 reshape.518
  211.3 3.7 convert_add_fusion.mid_ref
  214.9 29.8 %feed_forward.1 = (bf16[576,768]{1,0:T(8,128)(2,1)}, f32[576,768]{1,0:T(8,128)}, bf16[576,768]{1,0:T(8,128)(2,1)}, f32[4,768]{1,0:T(4,128)}, f32[4,1,768]{2,1,0:...) custom-call(f32[576,768]{1,0:T(8,128)} %convert_add_fusion.mid_ref, ...), custom_call_target="tpu_custom_call" | custom-call | tf_op jit(solution)/shard_map/feed_forward/pallas_call | solution.py:313
  244.7 3.5 convolution_convert_fusion.1
  250.5 5.0 %pad_maximum_fusion = bf16[8,4,216,768]{3,2,1,0:T(8,128)(2,1)} fusion(bf16[8,4,24,768]{3,2,1,0:T(8,128)(2,1)S(1)} %bitcast.253, bf16[8,4,96,768]{3,2,1,0:T(8,128)(2,1)S(1)} %copy-done.22, bf16[8,4,96,768]{3,2,1,0:T(8,128)(2,1)S(1)} %copy-done.21), kind=kLoop, calls=%fused_computation | loop fusion | flops 31850496 | bytes 21233664 | tf_op jit(solution)/shard_map/concatenate | solution.py:687
  255.6 3.7 reshape.522
  259.3 1.5 copy.288
  260.7 18.3 %all_to_all.73 = bf16[8,1,72,4,192]{4,2,0,1,3:T(8,128)(2,1)S(1)} all-to-all(bf16[8,1,72,4,192]{4,2,0,1,3:T(8,128)(2,1)S(1)} %copy.288), channel_id=1, replica_groups=mesh['ga'=8,'ha'=4] {'ha'}, dimensions={3} | all-to-all | bytes 1769472 | tf_op jit(solution)/shard_map/all_to_all | solution.py:676
  280.1 4.4 all-to-all-start.5
  284.5 49.7 %attend_backward.1 = (f32[3,2304,64]{2,1,0:T(8,128)}, bf16[3,2304,48]{2,1,0:T(8,128)(2,1)}, bf16[3,2304,48]{2,1,0:T(8,128)(2,1)}, bf16[2304,384]{1,0:T(8,128)(2,1)}) custom-call(bf16[2304,576]{1,0:T(8,128)(2,1)} %copy-done.2, bf16[3,2304,192]{2,1,0:T(8,128)(2,1)} %pad_maximum_fusion.4.rel_ref, bf16[2304,96]{1,0:T(8,128)(2,1)} %fusion.36.lines_ref, ...), custom_call_target="tpu_custom_call" | custom-call | tf_op jit(solution)/shard_map/attend_backward/pallas_call | solution.py:159
  334.3 2.0 copy.292
  337.9 1.3 copy-done.25
  339.2 1.5 fusion.4
  342.2 2.3 pad_maximum_fusion.5
  344.6 3.3 convolution_convert_fusion.2
  348.3 4.1 fusion.93
  352.7 1.7 copy-done.12
  354.4 1.4 pad_maximum_fusion.6
  356.2 2.8 fusion.22
  359.1 3.4 fusion.40
  363.3 3.4 fusion.37
  367.9 2.3 convert_element_type.221
  371.1 3.6 collective-permute-done.6
  375.8 5.7 %all-to-all-start.7 = ((f32[8,113,128]{2,1,0:T(8,128)}), f32[8,113,128]{2,1,0:T(8,128)S(1)}, u32[]{:S(2)}, u32[]{:S(2)}) async-start(f32[8,113,128]{2,1,0:T(8,128)} %broadcast_in_dim.63), calls=%async_computation.8 | async-start | bytes 983040 | tf_op jit(solution)/shard_map/all_to_all | solution.py:393
  381.5 1.8 convert_element_type.214
  383.3 3.1 fusion.45
  388.1 1.4 collective-permute-start.8
  390.0 24.4 %collective-permute-done.8 = bf16[192,576]{1,0:T(8,128)(2,1)S(1)} collective-permute-done((bf16[192,576]{1,0:T(8,128)(2,1)S(1)}, bf16[192,576]{1,0:T(8,128)(2,1)S(1)}, u32[]{:S(2)}, u32[]{:S(2)}) %collective-permute-start.8) | collective-permute-done | bytes 221216 | tf_op jit(solution)/shard_map/ppermute | solution.py:403
  414.4 1.7 collective-permute-done.9
  418.4 6.0 %all-to-all-start.8 = ((bf16[8,192,288]{1,2,0:T(8,128)(2,1)}), bf16[8,192,288]{1,2,0:T(8,128)(2,1)}, u32[]{:S(2)}, u32[]{:S(2)}) async-start(bf16[8,192,288]{1,2,0:T(8,128)(2,1)} %bitcast.84), calls=%async_computation.9 | async-start | bytes 2359296 | tf_op jit(solution)/shard_map/all_to_all | solution.py:393
  424.6 2.2 fusion.12
  428.9 1.5 add_convert_fusion.2
  430.5 24.4 %all-to-all-done.8 = bf16[8,192,288]{1,2,0:T(8,128)(2,1)} async-done(((bf16[8,192,288]{1,2,0:T(8,128)(2,1)}), bf16[8,192,288]{1,2,0:T(8,128)(2,1)}, u32[]{:S(2)}, u32[]{:S(2)}) %all-to-all-start.8) | async-done | bytes 884768 | tf_op jit(solution)/shard_map/all_to_all | solution.py:393
  454.9 3.7 all-to-all-start.6
  461.3 1.5 convert_reduce_fusion.2
  468.9 12.4 %all-to-all-done.6 = bf16[8,72,768]{2,1,0:T(8,128)(2,1)S(1)} async-done(((bf16[8,72,768]{2,1,0:T(8,128)(2,1)}), bf16[8,72,768]{2,1,0:T(8,128)(2,1)S(1)}, u32[]{:S(2)}, u32[]{:S(2)}) %all-to-all-start.6) | async-done | bytes 884768 | tf_op jit(solution)/shard_map/all_to_all | solution.py:393
  481.3 2.1 copy.379
  (285 shorter events, 51.6 us)
Async XLA Ops:
  7.2 92.2 %copy-start = (bf16[95,64]{0,1:T(8,128)(2,1)S(1)}, bf16[95,64]{0,1:T(8,128)(2,1)}, u32[]{:S(2)}) copy-start(bf16[95,64]{0,1:T(8,128)(2,1)} %param.34) | copy-start | bytes 36484
  7.2 7.5 %copy-start.49 = (bf16[192,96]{1,0:T(8,128)(2,1)S(1)}, bf16[192,96]{1,0:T(8,128)(2,1)}, u32[]{:S(2)}) copy-start(bf16[192,96]{1,0:T(8,128)(2,1)} %param.26) | copy-start | bytes 110596
  7.2 7.8 %copy-start.63 = (bf16[192]{0:T(256)(128)(2,1)S(1)}, bf16[192]{0:T(256)(128)(2,1)}, u32[]{:S(2)}) copy-start(bf16[192]{0:T(256)(128)(2,1)} %param.21) | copy-start | bytes 1156
  7.2 7.8 %copy-start.64 = (bf16[192]{0:T(256)(128)(2,1)S(1)}, bf16[192]{0:T(256)(128)(2,1)}, u32[]{:S(2)}) copy-start(bf16[192]{0:T(256)(128)(2,1)} %param.22) | copy-start | bytes 1156
  7.2 7.8 %copy-start.65 = (bf16[192]{0:T(256)(128)(2,1)S(1)}, bf16[192]{0:T(256)(128)(2,1)}, u32[]{:S(2)}) copy-start(bf16[192]{0:T(256)(128)(2,1)} %param.27) | copy-start | bytes 1156
  7.2 7.8 %copy-start.66 = (bf16[192]{0:T(256)(128)(2,1)S(1)}, bf16[192]{0:T(256)(128)(2,1)}, u32[]{:S(2)}) copy-start(bf16[192]{0:T(256)(128)(2,1)} %param.28) | copy-start | bytes 1156
  7.3 7.8 %copy-start.67 = (bf16[192]{0:T(256)(128)(2,1)S(1)}, bf16[192]{0:T(256)(128)(2,1)}, u32[]{:S(2)}) copy-start(bf16[192]{0:T(256)(128)(2,1)} %param.29) | copy-start | bytes 1156
  7.3 7.8 %copy-start.59 = (bf16[768]{0:T(1024)(128)(2,1)S(1)}, bf16[768]{0:T(1024)(128)(2,1)}, u32[]{:S(2)}) copy-start(bf16[768]{0:T(1024)(128)(2,1)} %param.31) | copy-start | bytes 4612
  7.3 7.8 %copy-start.68 = (bf16[192]{0:T(256)(128)(2,1)S(1)}, bf16[192]{0:T(256)(128)(2,1)}, u32[]{:S(2)}) copy-start(bf16[192]{0:T(256)(128)(2,1)} %param.33) | copy-start | bytes 1156
  7.3 14.1 %copy-start.35 = (bf16[192,288]{1,0:T(8,128)(2,1)S(1)}, bf16[192,288]{1,0:T(8,128)(2,1)}, u32[]{:S(2)}) copy-start(bf16[192,288]{1,0:T(8,128)(2,1)} %param.23) | copy-start | bytes 331780
  7.3 55.1 %all-to-all-start = ((bf16[8,72,768]{2,1,0:T(8,128)(2,1)}), bf16[8,72,768]{2,1,0:T(8,128)(2,1)S(1)}, u32[]{:S(2)}, u32[]{:S(2)}) async-start(bf16[8,72,768]{2,1,0:T(8,128)(2,1)} %param.18), calls=%async_computation | async-start | bytes 1769472 | tf_op jit(solution)/shard_map/all_to_all | solution.py:516
  21.4 84.0 %copy-start.33 = (bf16[4,1,20352]{2,0,1:T(4,128)(2,1)}, bf16[4,1,20352]{2,0,1:T(4,128)(2,1)S(1)}, u32[]{:S(2)}) copy-start(bf16[4,1,20352]{2,0,1:T(4,128)(2,1)S(1)} %copy.371) | copy-start | bytes 488452
  62.4 26.2 %collective-permute-start = (bf16[576,768]{1,0:T(8,128)(2,1)S(1)}, bf16[576,768]{1,0:T(8,128)(2,1)}, u32[]{:S(2)}, u32[]{:S(2)}) collective-permute-start(bf16[576,768]{1,0:T(8,128)(2,1)S(1)} %bitcast.202), channel_id=1, source_target_pairs={{0,2},{1,3},{2,0},{3,1},{4,6},{5,7},{6,4},{7,5},{8,10},{9,11},{10,... | collective-permute-start | bytes 2654216 | tf_op jit(solution)/shard_map/ppermute | solution.py:403
  63.9 24.7 %collective-permute-start.1 = (bf16[576,768]{1,0:T(8,128)(2,1)S(1)}, bf16[576,768]{1,0:T(8,128)(2,1)}, u32[]{:S(2)}, u32[]{:S(2)}) collective-permute-start(bf16[576,768]{1,0:T(8,128)(2,1)S(1)} %bitcast.203), channel_id=1, source_target_pairs={{0,1},{1,0},{2,3},{3,2},{4,5},{5,4},{6,7},{7,6},{8,9},{9,8},{10,11... | collective-permute-start | bytes 2654216 | tf_op jit(solution)/shard_map/ppermute | solution.py:403
  66.1 4.8 copy-start.36
  66.1 4.9 %copy-start.37 = (bf16[768,96]{0,1:T(8,128)(2,1)S(1)}, bf16[768,96]{0,1:T(8,128)(2,1)}, u32[]{:S(2)}) copy-start(bf16[768,96]{0,1:T(8,128)(2,1)} %param.32) | copy-start | bytes 442372
  66.1 22.5 %all-to-all-start.1 = ((bf16[4,192,576]{2,1,0:T(8,128)(2,1)}), bf16[4,192,576]{2,1,0:T(8,128)(2,1)S(1)}, u32[]{:S(2)}, u32[]{:S(2)}) async-start(bf16[4,192,576]{2,1,0:T(8,128)(2,1)} %copy.271), calls=%async_computation.1 | async-start | bytes 1966080 | tf_op jit(solution)/shard_map/all_to_all | solution.py:393
  69.7 112.2 %all-gather.5.cloned.1.call-start = ((), (), s32[]{:S(2)}) async-start(), calls=%async_computation.11 | async-start | bytes 10948608 | tf_op jit(solution)/shard_map/all_gather | solution.py:593
  70.7 22.3 %copy-start.70 = (s32[8]{0:T(128)S(1)}, s32[8]{0:T(128)}, u32[]{:S(2)}) copy-start(s32[8]{0:T(128)} %param.20) | copy-start | bytes 100
  70.7 24.7 %copy-start.61 = (bf16[192]{0:T(256)(128)(2,1)S(1)}, bf16[192]{0:T(256)(128)(2,1)}, u32[]{:S(2)}) copy-start(bf16[192]{0:T(256)(128)(2,1)} %param.25) | copy-start | bytes 1156
  70.7 24.7 %copy-start.62 = (bf16[192]{0:T(256)(128)(2,1)S(1)}, bf16[192]{0:T(256)(128)(2,1)}, u32[]{:S(2)}) copy-start(bf16[192]{0:T(256)(128)(2,1)} %param.24) | copy-start | bytes 1156
  88.6 10.7 %copy-start.28 = (bf16[4,192,576]{2,1,0:T(8,128)(2,1)}, bf16[4,192,576]{2,1,0:T(8,128)(2,1)S(1)}, u32[]{:S(2)}) copy-start(bf16[4,192,576]{2,1,0:T(8,128)(2,1)S(1)} %all-to-all-done.1) | copy-start | bytes 2654212
  88.7 50.7 %all-to-all-start.2 = ((bf16[8,72,768]{2,1,0:T(8,128)(2,1)}), bf16[8,72,768]{2,1,0:T(8,128)(2,1)}, u32[]{:S(2)}, u32[]{:S(2)}) async-start(bf16[8,72,768]{2,1,0:T(8,128)(2,1)} %param.19), calls=%async_computation.2 | async-start | bytes 1769472 | tf_op jit(solution)/shard_map/all_to_all | solution.py:520
  92.9 8.3 %copy-start.50 = (bf16[95,64]{0,1:T(8,128)(2,1)S(1)}, bf16[95,64]{0,1:T(8,128)(2,1)}, u32[]{:S(2)}) copy-start(bf16[95,64]{0,1:T(8,128)(2,1)} %param.35) | copy-start | bytes 36484
  97.0 6.0 %copy-start.39 = (s32[48,48]{0,1:T(8,128)}, s32[48,48]{0,1:T(8,128)S(1)}, u32[]{:S(2)}) copy-start(s32[48,48]{0,1:T(8,128)S(1)} %get-tuple-element.280) | copy-start | bytes 27652
  97.1 6.0 %copy-start.41 = (s32[48,48]{0,1:T(8,128)}, s32[48,48]{0,1:T(8,128)S(1)}, u32[]{:S(2)}) copy-start(s32[48,48]{0,1:T(8,128)S(1)} %get-tuple-element.281) | copy-start | bytes 27652
  98.0 5.0 %copy-start.43 = (f32[48,48]{0,1:T(8,128)}, f32[48,48]{0,1:T(8,128)S(1)}, u32[]{:S(2)}) copy-start(f32[48,48]{0,1:T(8,128)S(1)} %get-tuple-element.282) | copy-start | bytes 27652
  98.0 5.0 %copy-start.45 = (f32[48,48]{0,1:T(8,128)}, f32[48,48]{0,1:T(8,128)S(1)}, u32[]{:S(2)}) copy-start(f32[48,48]{0,1:T(8,128)S(1)} %get-tuple-element.283) | copy-start | bytes 27652
  103.1 4.3 collective-permute-start.2
  109.3 4.9 copy-start.4
  109.3 4.8 copy-start.6
  109.4 4.8 copy-start.8
  114.2 3.5 copy-start.29
  114.2 3.5 copy-start.58
  184.3 6.9 %copy-start.51 = (f32[4,192]{1,0:T(4,128)S(1)}, f32[4,192]{1,0:T(4,128)}, u32[]{:S(2)}) copy-start(f32[4,192]{1,0:T(4,128)} %get-tuple-element.251) | copy-start | bytes 9220
  184.3 6.9 %copy-start.57 = (bf16[4,192]{1,0:T(4,128)(2,1)S(1)}, bf16[4,192]{1,0:T(4,128)(2,1)}, u32[]{:S(2)}) copy-start(bf16[4,192]{1,0:T(4,128)(2,1)} %get-tuple-element.250) | copy-start | bytes 4612
  184.3 7.0 %copy-start.56 = (bf16[4,192]{1,0:T(4,128)(2,1)S(1)}, bf16[4,192]{1,0:T(4,128)(2,1)}, u32[]{:S(2)}) copy-start(bf16[4,192]{1,0:T(4,128)(2,1)} %get-tuple-element.254) | copy-start | bytes 4612
  184.3 7.1 %copy-start.55 = (bf16[4,192]{1,0:T(4,128)(2,1)S(1)}, bf16[4,192]{1,0:T(4,128)(2,1)}, u32[]{:S(2)}) copy-start(bf16[4,192]{1,0:T(4,128)(2,1)} %get-tuple-element.253) | copy-start | bytes 4612
  184.3 7.2 %copy-start.54 = (bf16[4,192]{1,0:T(4,128)(2,1)S(1)}, bf16[4,192]{1,0:T(4,128)(2,1)}, u32[]{:S(2)}) copy-start(bf16[4,192]{1,0:T(4,128)(2,1)} %get-tuple-element.252) | copy-start | bytes 4612
  184.3 20.2 %all-to-all-start.3 = ((bf16[8,4,72,1,192]{4,2,0,3,1:T(8,128)(2,1)}), bf16[8,4,72,1,192]{4,2,0,3,1:T(8,128)(2,1)}, u32[]{:S(2)}, u32[]{:S(2)}) async-start(bf16[8,4,72,1,192]{4,2,0,3,1:T(8,128)(2,1)} %copy.283), calls=%async_computation.3 | async-start | bytes 2359296 | tf_op jit(solution)/shard_map/all_to_all | solution.py:598
  188.6 238.2 %reduce-scatter.2.cloned.1.call-start = ((), (), s32[]{:S(2)}) async-start(), calls=%async_computation.10 | async-start | bytes 10948608 | tf_op jit(solution)/shard_map/reduce_scatter | solution.py:695
  244.7 3.5 copy-start.32
  244.7 3.5 copy-start.69
  244.7 4.6 copy-start.22
  280.1 54.1 %all-to-all-start.5 = ((bf16[8,72,768]{2,1,0:T(8,128)(2,1)}), bf16[8,72,768]{2,1,0:T(8,128)(2,1)}, u32[]{:S(2)}, u32[]{:S(2)}) async-start(bf16[8,72,768]{2,1,0:T(8,128)(2,1)} %bitcast.256), calls=%async_computation.5 | async-start | bytes 1769472 | tf_op jit(solution)/shard_map/all_to_all | solution.py:393
  344.6 3.7 copy-start.30
  344.6 3.6 copy-start.47
  344.6 3.6 copy-start.48
  355.8 25.7 %collective-permute-start.3 = (bf16[2,576,768]{2,1,0:T(8,128)(2,1)}, bf16[2,576,768]{2,1,0:T(8,128)(2,1)}, u32[]{:S(2)}, u32[]{:S(2)}) collective-permute-start(bf16[2,576,768]{2,1,0:T(8,128)(2,1)} %pad_maximum_fusion.6), channel_id=1, source_target_pairs={{0,1},{1,0},{2,3},{3,2},{4,5},{5,4},{6,7},{7,6},{8,9},{9,8},{10,11... | collective-permute-start | bytes 5308424 | tf_op jit(solution)/shard_map/ppermute | solution.py:403
  367.3 2.9 collective-permute-start.5
  370.2 4.5 collective-permute-start.6
  375.8 42.6 %all-to-all-start.7 = ((f32[8,113,128]{2,1,0:T(8,128)}), f32[8,113,128]{2,1,0:T(8,128)S(1)}, u32[]{:S(2)}, u32[]{:S(2)}) async-start(f32[8,113,128]{2,1,0:T(8,128)} %broadcast_in_dim.63), calls=%async_computation.8 | async-start | bytes 983040 | tf_op jit(solution)/shard_map/all_to_all | solution.py:393
  383.3 4.0 copy-start.31
  386.4 38.2 %collective-permute-start.4 = (bf16[576,768]{1,0:T(8,128)(2,1)}, bf16[576,768]{1,0:T(8,128)(2,1)}, u32[]{:S(2)}, u32[]{:S(2)}) collective-permute-start(bf16[576,768]{1,0:T(8,128)(2,1)} %fusion.45), channel_id=1, source_target_pairs={{0,2},{1,3},{2,0},{3,1},{4,6},{5,7},{6,4},{7,5},{8,10},{9,11},{10,... | collective-permute-start | bytes 2654216 | tf_op jit(solution)/shard_map/ppermute | solution.py:403
  388.0 1.9 collective-permute-start.7
  388.1 26.3 %collective-permute-start.8 = (bf16[192,576]{1,0:T(8,128)(2,1)S(1)}, bf16[192,576]{1,0:T(8,128)(2,1)S(1)}, u32[]{:S(2)}, u32[]{:S(2)}) collective-permute-start(bf16[192,576]{1,0:T(8,128)(2,1)S(1)} %get-tuple-element.246), channel_id=1, source_target_pairs={{0,2},{1,3},{2,0},{3,1},{4,6},{5,7},{6,4},{7,5},{8,10},{9,11},{10,... | collective-permute-start | bytes 663560 | tf_op jit(solution)/shard_map/ppermute | solution.py:403
  389.5 26.6 %collective-permute-start.9 = (bf16[192,576]{1,0:T(8,128)(2,1)S(1)}, bf16[192,576]{1,0:T(8,128)(2,1)S(1)}, u32[]{:S(2)}, u32[]{:S(2)}) collective-permute-start(bf16[192,576]{1,0:T(8,128)(2,1)S(1)} %get-tuple-element.245), channel_id=1, source_target_pairs={{0,3},{1,2},{2,1},{3,0},{4,7},{5,6},{6,5},{7,4},{8,11},{9,10},{10,... | collective-permute-start | bytes 663560 | tf_op jit(solution)/shard_map/ppermute | solution.py:403
  418.4 36.5 %all-to-all-start.8 = ((bf16[8,192,288]{1,2,0:T(8,128)(2,1)}), bf16[8,192,288]{1,2,0:T(8,128)(2,1)}, u32[]{:S(2)}, u32[]{:S(2)}) async-start(bf16[8,192,288]{1,2,0:T(8,128)(2,1)} %bitcast.84), calls=%async_computation.9 | async-start | bytes 2359296 | tf_op jit(solution)/shard_map/all_to_all | solution.py:393
  454.9 8.7 %slice-start = ((bf16[216,768]{1,0:T(8,128)(2,1)}), bf16[24,768]{1,0:T(8,128)(2,1)S(1)}, s32[]{:S(2)}) async-start(bf16[216,768]{1,0:T(8,128)(2,1)} %reduce-scatter.2.cloned.1.call-done), calls=%async_computation.12 | async-start | bytes 73728 | tf_op jit(solution)/shard_map/slice | solution.py:786
  454.9 26.4 %all-to-all-start.6 = ((bf16[8,72,768]{2,1,0:T(8,128)(2,1)}), bf16[8,72,768]{2,1,0:T(8,128)(2,1)S(1)}, u32[]{:S(2)}, u32[]{:S(2)}) async-start(bf16[8,72,768]{2,1,0:T(8,128)(2,1)} %bitcast.64), calls=%async_computation.7 | async-start | bytes 1769472 | tf_op jit(solution)/shard_map/all_to_all | solution.py:393
  458.6 7.2 %copy-start.34 = (bf16[216,768]{1,0:T(8,128)(2,1)S(1)}, bf16[216,768]{1,0:T(8,128)(2,1)}, u32[]{:S(2)}) copy-start(bf16[216,768]{1,0:T(8,128)(2,1)} %reduce-scatter.2.cloned.1.call-done) | copy-start | bytes 995332
  463.9 3.6 collective-permute-start.10
  464.1 3.7 collective-permute-start.11
  465.0 3.1 collective-permute-start.12
  (31 other events, 71.4 us)
Sparse Core Ops, SparseCore 0:
  88.8 93.0 all-gather.4
  255.7 146.7 reduce-scatter.1
